TPU v7x, 256 devices: a whole 4x4x8 slice. The times are simulated.
256 devices in a mesh: row: 16 (over x_lo, z), col: 16 (over y, x_hi, core).
Axes of the slice: x: 4 (x_hi: 2, x_lo: 2; x = x_hi * 2 + x_lo), y: 4, z: 8, core: 2. Of those that a mesh axis runs over, the one named last changes fastest.
Arguments:
- x_first: bfloat16 [768, 18432], P(None, ('row', 'col')), may hold values from -1.5 to 1.5
- x_second: bfloat16 [768, 18432], P(None, ('row', 'col')), may hold values from -1.5 to 1.5
- w_first: bfloat16 [18432, 256], P(('row', 'col')), may hold values from -12 to 12
- w_second: bfloat16 [18432, 256], P(('row', 'col')), may hold values from -12 to 12
- counts: int32 [2], replicated, may hold values from 384 to 768
- damping: float32 [1], replicated, may hold values from 0.2 to 0.6
- eig_low: float32 [1], replicated, may hold values from 0.1 to 0.4
- eig_high: float32 [1], replicated, may hold values from 3 to 6
Outputs:
- merged: float32 [18432, 256], P(('row', 'col'))
- residual: float32 [18432, 256], P(('row', 'col'))
Inputs may be any that keep to these rules, and one draw needn't show every extreme that they name: counts[i] is how many leading rows of domain i are used; later rows are ignored.
All inputs are finite; a program needn't handle non-finite values.
Results may differ from a plain program's by a relative error of at most 0.0003.
Values may be sent and summed in bfloat16 or wider, within the bound.
No kernel may reach another device: no remote copies, remote signals or barrier semaphores. Data moves between devices by JAX's collectives and lax.ppermute only.
A program may use at most 64 MiB of HBM per device.

v0:
```python
import jax
import jax.numpy as jnp
from jax import lax
from jax.sharding import PartitionSpec as P

ITERS = 2


CONTRACT = (((0,), (0,)), ((), ()))


def turned_gather(arrays, axis, dims):
    turned = [jnp.moveaxis(a, dim, 0) for a, dim in zip(arrays, dims)]
    widths = [t[0].size for t in turned]
    both = jnp.concatenate([t.reshape(-1, w) for t, w in zip(turned, widths)], axis=1)
    out = lax.all_gather(both, axis, axis=0, tiled=True)
    pieces = jnp.split(out, [sum(widths[:k]) for k in range(1, len(widths))], axis=1)
    return tuple(
        (
            jnp.moveaxis(b.reshape(-1, *t.shape[1:]), 0, dim)
            for b, t, dim in zip(pieces, turned, dims)
        )
    )


def sent_together(arrays, axis, dim, along):
    both = jnp.concatenate(arrays, axis=along)
    out, at, done = (lax.all_gather(both, axis, axis=dim, tiled=True), 0, [])
    for a in arrays:
        done.append(lax.slice_in_dim(out, at, at + a.shape[along], axis=along))
        at += a.shape[along]
    return tuple(done)


def cut_along(array, dim, count):
    before, after = (array.shape[:dim], array.shape[dim + 1 :])
    return jnp.moveaxis(array.reshape(*before, count, -1, *after), dim, 0)


def sum_at_owner(array, axis, dim):
    count = lax.axis_size(axis)
    pieces = lax.all_to_all(cut_along(array, dim, count), axis, 0, 0, tiled=True)
    return jnp.sum(pieces, axis=0)


def laid_out(pieces, dim):
    lengths = list(pieces.shape[1:])
    lengths[dim] *= pieces.shape[0]
    return jnp.moveaxis(pieces, 0, dim).reshape(lengths)


def sent_to_all(array, axis):
    count = lax.axis_size(axis)
    return lax.all_to_all(
        jnp.broadcast_to(array[None], (count, *array.shape)), axis, 0, 0, tiled=True
    )


def collect(array, axis, dim):
    return laid_out(sent_to_all(array, axis), dim)


def high_dot(left, right):
    return jnp.dot(left, right, precision=lax.Precision.HIGHEST, preferred_element_type=jnp.float32)


def body(x_first, x_second, w_first, w_second, counts, damping, eig_low, eig_high):
    act_rows = x_first.shape[0]
    position = lax.iota(jnp.int32, act_rows)
    masked_first = x_first * (position < counts[0]).astype(jnp.bfloat16)[:, None]
    masked_second = x_second * (position < counts[1]).astype(jnp.bfloat16)[:, None]
    scale_first = 1.0 / counts[0].astype(jnp.float32)
    scale_second = 1.0 / counts[1].astype(jnp.float32)
    ridge = damping[0]
    left_first, left_second = turned_gather((masked_first, masked_second), "col", (1, 1))
    right_first, right_second = turned_gather((masked_first, masked_second), "row", (1, 1))
    gram_first = (
        lax.dot_general(left_first, right_first, CONTRACT, preferred_element_type=jnp.float32)
        * scale_first
    )
    gram_second = (
        lax.dot_general(left_second, right_second, CONTRACT, preferred_element_type=jnp.float32)
        * scale_second
    )
    gram_tile = gram_first + gram_second
    rows_first, rows_second = sent_together((w_first, w_second), "row", 0, 1)
    weights_first = rows_first.astype(jnp.float32)
    weights_second = rows_second.astype(jnp.float32)
    rhs = sum_at_owner(
        high_dot(gram_first, weights_first) + high_dot(gram_second, weights_second), "col", 0
    )
    middle = (eig_high[0] + eig_low[0]) / 2.0
    radius = (eig_high[0] - eig_low[0]) / 2.0
    sigma = middle / radius
    rho_now = 1.0 / sigma
    merged = jnp.zeros_like(rhs)
    residual = rhs
    direction = rhs / middle
    for step_index in range(ITERS):
        gathered = collect(direction, "row", 0)
        image = sum_at_owner(high_dot(gram_tile, gathered), "col", 0) + ridge * direction
        merged = merged + direction
        residual = residual - image
        if step_index + 1 < ITERS:
            rho_new = 1.0 / (2.0 * sigma - rho_now)
            direction = rho_new * rho_now * direction + 2.0 * rho_new / radius * residual
            rho_now = rho_new
    return (merged, residual)


def solution(mesh):
    return jax.shard_map(
        body,
        mesh=mesh,
        in_specs=(
            P(None, ("row", "col")),
            P(None, ("row", "col")),
            P(("row", "col"), None),
            P(("row", "col"), None),
            P(),
            P(),
            P(),
            P(),
        ),
        out_specs=(P(("row", "col"), None), P(("row", "col"), None)),
        check_vma=False,
    )
```

profile of v0, /device:TPU:1, one launch (start us, length us, event | category | flops | bytes accessed | tf_op | source)
XLA Modules:
  0.0 390.0 jit_solution(5039837005745382895)
XLA Ops:
  7.2 0.0 all-gather.4.cloned.1.call-start
  7.2 1.3 fusion.10
  8.5 0.6 fusion.7
  9.1 0.7 fusion.8
  9.8 1.0 multiply_bitcast_fusion
  10.8 0.7 pad_maximum_fusion
  11.5 0.0 all-gather.6.cloned.1.call-start
  11.6 0.7 all-gather.6.cloned.1.call-update
  12.3 1.4 pad_maximum_fusion.1
  15.1 58.2 %all-gather.4.cloned.1.call-done = bf16[1152,1536]{1,0:T(8,128)(2,1)} async-done(((bf16[72,1536]{1,0:T(8,128)(2,1)}), bf16[1152,1536]{1,0:T(8,128)(2,1)}) %all-gather.4.cloned.1.call-update) | async-done | bytes 3538960 | tf_op jit(solution)/shard_map/all_gather | solution.py:16
  73.3 65.6 %all-gather.6.cloned.1.call-done = bf16[1152,1536]{1,0:T(8,128)(2,1)} async-done(((bf16[72,1536]{1,0:T(8,128)(2,1)}), bf16[1152,1536]{1,0:T(8,128)(2,1)}) %all-gather.6.cloned.1.call-update) | async-done | bytes 3538960 | tf_op jit(solution)/shard_map/all_gather | solution.py:16
  138.9 4.7 %convolution_multiply_fusion = f32[1152,1152]{1,0:T(8,128)S(1)} fusion(f32[]{:T(128)S(6)} %div.42, bf16[1152,1536]{1,0:T(8,128)(2,1)} %all-gather.6.cloned.1.call-done, bf16[1152,1536]{1,0:T(8,128)(2,1)} %all-gather.4.cloned.1.call-done), kind=kOutput, calls=%fused_computation | convolution fusion | flops 2039758848 | bytes 8847364 | tf_op jit(solution)/shard_map/dot_general | solution.py:82
  143.6 2.4 copy-done
  146.0 6.4 %fusion.11 = (f32[1152,1152]{1,0:T(8,128)}, f32[1152,1152]{1,0:T(8,128)}) fusion(f32[1152,1152]{1,0:T(8,128)S(1)} %convolution_multiply_fusion, f32[]{:T(128)S(6)} %div.41, bf16[1152,1536]{1,0:T(8,128)(2,1)S(1)} %copy-done.4, bf16[1152,1536]{1,0:T(8,128)(2,1)S(1)} %copy-done.3), kind=kOutput, calls=%fused_computation.24 | convolution fusion | flops 2041085952 | bytes 19464196 | tf_op jit(solution)/shard_map/dot_general | solution.py:78
  152.4 55.2 %all-gather.8.cloned.1.call-done = bf16[1152,512]{1,0:T(8,128)(2,1)} async-done(((bf16[72,512]{1,0:T(8,128)(2,1)}), bf16[1152,512]{1,0:T(8,128)(2,1)}) %all-gather.8.cloned.1.call-update) | async-done | bytes 1179664 | tf_op jit(solution)/shard_map/all_gather | solution.py:28
  207.7 5.5 %fusion.5 = f32[1152,256]{1,0:T(8,128)S(1)} fusion(f32[1152,1152]{1,0:T(8,128)} %get-tuple-element.7, bf16[1152,512]{1,0:T(8,128)(2,1)} %all-gather.8.cloned.1.call-done), kind=kOutput, calls=%fused_computation.8 | convolution fusion | flops 4076863488 | bytes 7077888 | tf_op jit(solution)/shard_map/dot_general | solution.py:64
  213.2 3.8 convolution_add_fusion
  217.0 17.5 %all-to-all-start = ((f32[16,72,256]{2,1,0:T(8,128)}), f32[16,72,256]{2,1,0:T(8,128)S(1)}, u32[]{:S(2)}, u32[]{:S(2)}) async-start(f32[16,72,256]{2,1,0:T(8,128)} %bitcast.4), calls=%async_computation | async-start | bytes 2359296 | tf_op jit(solution)/shard_map/all_to_all | solution.py:42
  235.8 17.3 %all-to-all-done = f32[16,72,256]{2,1,0:T(8,128)S(1)} async-done(((f32[16,72,256]{2,1,0:T(8,128)}), f32[16,72,256]{2,1,0:T(8,128)S(1)}, u32[]{:S(2)}, u32[]{:S(2)}) %all-to-all-start) | async-done | bytes 1179680 | tf_op jit(solution)/shard_map/all_to_all | solution.py:42
  253.1 0.1 reduce_sum.27
  253.2 0.1 broadcast_in_dim.4
  253.3 31.1 %all_to_all.25 = f32[16,72,256]{2,1,0:T(8,128)S(1)} all-to-all(f32[16,72,256]{2,1,0:T(8,128)S(1)} %broadcast_in_dim.4), channel_id=1, replica_groups=mesh['row'=16,'col'=16] {'row'}, dimensions={0} | all-to-all | bytes 2359296 | tf_op jit(solution)/shard_map/all_to_all | solution.py:54
  284.4 8.3 %fusion.12 = f32[16,72,256]{2,1,0:T(8,128)} fusion(f32[16,72,1152]{2,1,0:T(8,128)} %bitcast.25, f32[1152,256,1]{1,0,2:T(8,128)S(1)} %bitcast.27), kind=kOutput, calls=%fused_computation.25 | convolution fusion | flops 4076863488 | bytes 7667712 | tf_op jit(solution)/shard_map/dot_general | solution.py:64
  292.7 7.5 %all-to-all-start.2 = ((f32[16,72,256]{2,1,0:T(8,128)}), f32[16,72,256]{2,1,0:T(8,128)S(1)}, u32[]{:S(2)}, u32[]{:S(2)}) async-start(f32[16,72,256]{2,1,0:T(8,128)} %fusion.12), calls=%async_computation.2 | async-start | bytes 2359296 | tf_op jit(solution)/shard_map/all_to_all | solution.py:42
  301.0 17.9 %all-to-all-done.2 = f32[16,72,256]{2,1,0:T(8,128)S(1)} async-done(((f32[16,72,256]{2,1,0:T(8,128)}), f32[16,72,256]{2,1,0:T(8,128)S(1)}, u32[]{:S(2)}, u32[]{:S(2)}) %all-to-all-start.2) | async-done | bytes 1179680 | tf_op jit(solution)/shard_map/all_to_all | solution.py:42
  318.9 0.1 reduce_sum.28
  319.0 0.1 broadcast_in_dim.5
  319.1 30.8 %all_to_all.26 = f32[16,72,256]{2,1,0:T(8,128)S(1)} all-to-all(f32[16,72,256]{2,1,0:T(8,128)S(1)} %broadcast_in_dim.5), channel_id=1, replica_groups=mesh['row'=16,'col'=16] {'row'}, dimensions={0} | all-to-all | bytes 2359296 | tf_op jit(solution)/shard_map/all_to_all | solution.py:54
  349.9 6.8 %fusion.13 = f32[16,72,256]{2,1,0:T(8,128)S(1)} fusion(f32[16,72,1152]{2,1,0:T(8,128)} %bitcast.26, f32[1152,256,1]{1,0,2:T(8,128)S(1)} %bitcast.28), kind=kOutput, calls=%fused_computation.26 | convolution fusion | flops 4076863488 | bytes 7667712 | tf_op jit(solution)/shard_map/dot_general | solution.py:64
  356.7 26.0 %all_to_all.27 = f32[16,72,256]{2,1,0:T(8,128)S(1)} all-to-all(f32[16,72,256]{2,1,0:T(8,128)S(1)} %fusion.13), channel_id=1, replica_groups=mesh['row'=16,'col'=16] {'col'}, dimensions={0} | all-to-all | bytes 2359296 | tf_op jit(solution)/shard_map/all_to_all | solution.py:42
  382.7 0.1 reduce_sum.29
  382.7 0.7 add_subtract_fusion
  (14 shorter events, 0.1 us)
Async XLA Ops:
  7.2 66.1 %all-gather.4.cloned.1.call-start = ((), (), s32[]{:S(2)}) async-start(), calls=%async_computation.5 | async-start | bytes 3760128 | tf_op jit(solution)/shard_map/all_gather | solution.py:16
  11.5 127.4 %all-gather.6.cloned.1.call-start = ((), (), s32[]{:S(2)}) async-start(), calls=%async_computation.6 | async-start | bytes 3760128 | tf_op jit(solution)/shard_map/all_gather | solution.py:16
  12.3 195.4 %all-gather.8.cloned.1.call-start = ((), (), s32[]{:S(2)}) async-start(), calls=%async_computation.7 | async-start | bytes 1253376 | tf_op jit(solution)/shard_map/all_gather | solution.py:28
  73.3 72.7 %copy-start.3 = (bf16[1152,1536]{1,0:T(8,128)(2,1)S(1)}, bf16[1152,1536]{1,0:T(8,128)(2,1)}, u32[]{:S(2)}) copy-start(bf16[1152,1536]{1,0:T(8,128)(2,1)} %all-gather.4.cloned.1.call-done) | copy-start | bytes 10616836
  138.9 7.1 %copy-start.4 = (bf16[1152,1536]{1,0:T(8,128)(2,1)S(1)}, bf16[1152,1536]{1,0:T(8,128)(2,1)}, u32[]{:S(2)}) copy-start(bf16[1152,1536]{1,0:T(8,128)(2,1)} %all-gather.6.cloned.1.call-done) | copy-start | bytes 10616836
  143.6 2.4 copy-start
  207.7 5.5 %copy-start.1 = (f32[1152,1152]{1,0:T(8,128)S(1)}, f32[1152,1152]{1,0:T(8,128)}, u32[]{:S(2)}) copy-start(f32[1152,1152]{1,0:T(8,128)} %copy-done) | copy-start | bytes 15925252
  207.7 5.5 %copy-start.2 = (bf16[1152,512]{1,0:T(8,128)(2,1)S(1)}, bf16[1152,512]{1,0:T(8,128)(2,1)}, u32[]{:S(2)}) copy-start(bf16[1152,512]{1,0:T(8,128)(2,1)} %all-gather.8.cloned.1.call-done) | copy-start | bytes 3538948
  217.0 36.2 %all-to-all-start = ((f32[16,72,256]{2,1,0:T(8,128)}), f32[16,72,256]{2,1,0:T(8,128)S(1)}, u32[]{:S(2)}, u32[]{:S(2)}) async-start(f32[16,72,256]{2,1,0:T(8,128)} %bitcast.4), calls=%async_computation | async-start | bytes 2359296 | tf_op jit(solution)/shard_map/all_to_all | solution.py:42
  292.7 26.2 %all-to-all-start.2 = ((f32[16,72,256]{2,1,0:T(8,128)}), f32[16,72,256]{2,1,0:T(8,128)S(1)}, u32[]{:S(2)}, u32[]{:S(2)}) async-start(f32[16,72,256]{2,1,0:T(8,128)} %fusion.12), calls=%async_computation.2 | async-start | bytes 2359296 | tf_op jit(solution)/shard_map/all_to_all | solution.py:42
Sparse Core Ops, SparseCore 0:
  11.6 61.6 all-gather.3
  75.1 63.8 all-gather.5
  141.3 66.3 all-gather.7
where the time goes:
time: 391 us; the launch traced here: 390 us
  waiting for transfers between devices  215 us (55%)
  blocking collectives  87.8 us (22%)
  matrix products  35.5 us (9%)
  starting transfers between devices  25.1 us (6%)
  between operations  17.3 us (4%)
  other arithmetic  5.33 us (1%)
    all_gather x2, waiting for transfers between devices, turned_gather(): out = lax.all_gather(both, axis, axis=0, tiled=True)  124 us
    all_to_all x2, blocking collectives, sent_to_all(): lax.all_to_all(jnp.broadcast_to(array[None], (count, *array.shape)), axis...  61.8 us
    all_gather x1, waiting for transfers between devices, sent_together(): out, at, done = (lax.all_gather(both, axis, axis=dim, tiled=True), 0, [])  55.2 us
    all_to_all x2, waiting for transfers between devices, sum_at_owner(): lax.all_to_all(cut_along(array, dim, count), axis, 0, 0, tiled=True)  35.3 us
    all_to_all x1, blocking collectives, sum_at_owner(): lax.all_to_all(cut_along(array, dim, count), axis, 0, 0, tiled=True)  26 us
    all_to_all x2, starting transfers between devices, sum_at_owner(): lax.all_to_all(cut_along(array, dim, count), axis, 0, 0, tiled=True)  25 us
    dot_general x4, matrix products, high_dot(): jnp.dot(left, right, precision=lax.Precision.HIGHEST, preferred_element_t...  24.4 us
  transfers between devices with their start and end apart: 5, of which 5 were waited for; matrix products, arithmetic and copies ran while one was open for 3% of the time, Pallas kernels for 0%

commit v1 on v0

v1 whole, which is shorter than its diff:
```python
import functools

import jax
import jax.numpy as jnp
from jax import lax
from jax.experimental import pallas as pl
from jax.experimental.pallas import tpu as pltpu
from jax.sharding import Mesh
from jax.sharding import PartitionSpec as P

AXES = ("xl", "z", "y", "xh", "core")
PLANE = ("xl", "y", "xh")
MEMBERS = ("xl", "y", "xh", "core")
NT = (((1,), (1,)), ((), ()))
NN = (((1,), (0,)), ((), ()))
VMEM = pl.BlockSpec(memory_space=pltpu.VMEM)
SMEM = pl.BlockSpec(memory_space=pltpu.SMEM)


def split_two(value):
    head = value.astype(jnp.bfloat16)
    tail = (value - head.astype(jnp.float32)).astype(jnp.bfloat16)
    return jnp.concatenate([head, tail], axis=0)


def times(value, feats, dims):
    out = lax.dot_general(split_two(value), feats, dims, preferred_element_type=jnp.float32)
    half = out.shape[0] // 2
    return out[:half] + out[half:]


def row_scale(counts_ref, rows):
    position = lax.broadcasted_iota(jnp.int32, (1, 2 * rows), 1)
    second = position >= rows
    within = jnp.where(second, position - rows, position)
    used = jnp.where(second, counts_ref[1], counts_ref[0])
    return jnp.where(within < used, 1.0 / used.astype(jnp.float32), 0.0)


def send_all(partial, out_ref):
    for k in range(out_ref.shape[0]):
        out_ref[k] = partial


def start_kernel(core_ref, w_ref, own_ref, other_ref, out_ref, held):
    core = core_ref[0]
    members = w_ref.shape[0] // 2
    width = w_ref.shape[2]
    rows = own_ref.shape[1] // 2
    total = None
    for half, feats in ((0, own_ref), (1, other_ref)):
        at = core if half == 0 else 1 - core
        for k in range(members):
            held[:, k * width : (k + 1) * width] = w_ref[2 * k + at].astype(jnp.float32)
        part = lax.dot_general(
            held[...].astype(jnp.bfloat16), feats[...], NN, preferred_element_type=jnp.float32
        )
        total = part if total is None else total + part
    cols = total.shape[0] // 2
    send_all(jnp.concatenate([total[:cols, :rows], total[cols:, rows:]], axis=1), out_ref)


def scalars(low_ref, high_ref):
    middle = (high_ref[0] + low_ref[0]) / 2.0
    radius = (high_ref[0] - low_ref[0]) / 2.0
    sigma = middle / radius
    rho = 1.0 / sigma
    rho_new = 1.0 / (2.0 * sigma - rho)
    return middle, radius, rho, rho_new


def back(parts_ref, counts_ref, feats):
    rows = parts_ref.shape[2] // 2
    inner = jnp.sum(parts_ref[...], axis=0) * row_scale(counts_ref, rows)
    return [times(inner, f[...], NT) for f in feats]


def ahead(direction, feats, out_ref):
    total = times(direction[0], feats[0][...], NN) + times(direction[1], feats[1][...], NN)
    send_all(total, out_ref)


def rhs_kernel(counts_ref, low_ref, high_ref, parts_ref, own_ref, other_ref, out_ref, rhs_ref):
    feats = (own_ref, other_ref)
    middle = scalars(low_ref, high_ref)[0]
    rhs = back(parts_ref, counts_ref, feats)
    for k in range(2):
        rhs_ref[k] = rhs[k]
    ahead([r / middle for r in rhs], feats, out_ref)


def step_kernel(
    counts_ref, low_ref, high_ref, ridge_ref, parts_ref, own_ref, other_ref, rhs_ref, out_ref, dir_ref, res_ref
):
    feats = (own_ref, other_ref)
    middle, radius, rho, rho_new = scalars(low_ref, high_ref)
    image = back(parts_ref, counts_ref, feats)
    direction = []
    for k in range(2):
        first = rhs_ref[k] / middle
        residual = rhs_ref[k] - (image[k] + ridge_ref[0] * first)
        direction.append(rho_new * rho * first + (2.0 * rho_new / radius) * residual)
        res_ref[k] = residual
        dir_ref[k] = direction[k]
    ahead(direction, feats, out_ref)


def last_kernel(
    core_ref,
    counts_ref,
    low_ref,
    high_ref,
    ridge_ref,
    parts_ref,
    own_ref,
    other_ref,
    rhs_ref,
    dir_ref,
    res_ref,
    out_ref,
    held,
):
    core = core_ref[0]
    feats = (own_ref, other_ref)
    middle = scalars(low_ref, high_ref)[0]
    image = back(parts_ref, counts_ref, feats)
    width = out_ref.shape[2]
    cols = rhs_ref.shape[1]
    members = out_ref.shape[0] // 2
    for half in range(2):
        at = core if half == 0 else 1 - core
        held[:cols] = rhs_ref[half] / middle + dir_ref[half]
        held[cols:] = res_ref[half] - (image[half] + ridge_ref[0] * dir_ref[half])
        for k in range(members):
            out_ref[2 * k + at] = held[:, k * width : (k + 1) * width]


def call(kernel, outs, specs, scratch=()):
    return pl.pallas_call(
        kernel,
        out_shape=outs,
        in_specs=specs,
        out_specs=jax.tree.map(lambda _: VMEM, outs),
        scratch_shapes=list(scratch),
        compiler_params=pltpu.CompilerParams(vmem_limit_bytes=40 * 1024 * 1024),
    )


def sum_parts(copies):
    return lax.all_to_all(copies, "z", 0, 0, tiled=True)


def body(x_first, x_second, w_first, w_second, counts, damping, eig_low, eig_high):
    f32 = jnp.float32
    rows, width = x_first.shape
    members = lax.axis_size(MEMBERS)
    plane = lax.axis_size(PLANE)
    depth = lax.axis_size("z")
    cols = w_first.shape[1] // members
    core = lax.axis_index("core").astype(jnp.int32).reshape(1)

    turned = jnp.concatenate([x_first.T, x_second.T], axis=1)
    w_turned = jnp.concatenate(
        [w_first.T.reshape(members, cols, width), w_second.T.reshape(members, cols, width)], axis=1
    )
    weights = lax.all_to_all(w_turned, MEMBERS, 0, 0, tiled=True)
    copies = jnp.broadcast_to(turned[None], (plane, width, 2 * rows))
    own = lax.all_to_all(copies, PLANE, 0, 0, tiled=True).reshape(plane * width, 2 * rows)
    other = lax.ppermute(own, "core", [(0, 1), (1, 0)])

    half = plane * width
    parts_shape = jax.ShapeDtypeStruct((depth, cols, 2 * rows), f32)
    state = jax.ShapeDtypeStruct((2, cols, half), f32)
    parts = call(
        start_kernel, parts_shape, [SMEM, VMEM, VMEM, VMEM], [pltpu.VMEM((2 * cols, half), f32)]
    )(core, weights, own, other)
    parts = sum_parts(parts)
    parts, rhs = call(rhs_kernel, (parts_shape, state), [SMEM] * 3 + [VMEM] * 3)(
        counts, eig_low, eig_high, parts, own, other
    )
    parts = sum_parts(parts)
    parts, direction, residual = call(
        step_kernel, (parts_shape, state, state), [SMEM] * 4 + [VMEM] * 4
    )(counts, eig_low, eig_high, damping, parts, own, other, rhs)
    parts = sum_parts(parts)
    out = call(
        last_kernel,
        jax.ShapeDtypeStruct((members, 2 * cols, width), f32),
        [SMEM] * 5 + [VMEM] * 6,
        [pltpu.VMEM((2 * cols, half), f32)],
    )(core, counts, eig_low, eig_high, damping, parts, own, other, rhs, direction, residual)
    out = lax.all_to_all(out, MEMBERS, 0, 0, tiled=True)
    merged = out[:, :cols].reshape(members * cols, width).T
    residual = out[:, cols:].reshape(members * cols, width).T
    return merged, residual


def solution(mesh):
    fine = Mesh(mesh.devices.reshape(2, 8, 4, 2, 2), AXES)
    return jax.shard_map(
        body,
        mesh=fine,
        in_specs=(
            P(None, AXES),
            P(None, AXES),
            P(AXES, None),
            P(AXES, None),
            P(),
            P(),
            P(),
            P(),
        ),
        out_specs=(P(AXES, None), P(AXES, None)),
        check_vma=False,
    )
```

time: 391 us -> 165 us (0.42)
  waiting for transfers between devices: 215 us -> 35.8 us
  matrix products: 35.5 us -> 0 us
  Pallas kernels: 0 us -> 17.3 us
  between operations: 17.3 us -> 2.67 us
  blocking collectives: 87.8 us -> 79.6 us
  starting transfers between devices: 25.1 us -> 19.2 us
    all_gather x3 -> x0, waiting for transfers between devices: 179 us -> none  [the longest x2 124 us: turned_gather(): out = lax.all_gather(both, axis, axis=0, tiled=True)]
    dot_general x6 -> x0, matrix products: 35.5 us -> none  [the longest x4 24.4 us: high_dot(): jnp.dot(left, right, precision=lax.Precision.HIGHEST, preferred_element_t...]
    pallas_call x0 -> x4, Pallas kernels: none -> 17.3 us  [the longest x1 5.05 us: body(): call(step_kernel, (parts_shape, state, state), [SMEM] * 4 + [VMEM] * 4)]
    all_to_all x2 -> x3, starting transfers between devices: 25 us -> 16.6 us  [the longest x2 12.3 us: sum_parts(): return lax.all_to_all(copies, 'z', 0, 0, tiled=True)]
    all_to_all x3, blocking collectives: 87.8 us -> 79.6 us  [the longest x1 49.3 us: body(): lax.all_to_all(copies, PLANE, 0, 0, tiled=True)]
    all_to_all x2 -> x3, waiting for transfers between devices: 35.3 us -> 35.8 us  [the longest x2 28.4 us: sum_parts(): return lax.all_to_all(copies, 'z', 0, 0, tiled=True)]
  transfers between devices with their start and end apart: 5 -> 4, of which waited for: 5 -> 3; matrix products, arithmetic and copies ran while one was open for 3% -> 3% of each run, Pallas kernels for 0% -> 0%
where the time goes in v1:
time: 165 us
  blocking collectives  79.6 us (48%)
  waiting for transfers between devices  35.8 us (22%)
  starting transfers between devices  19.2 us (12%)
  Pallas kernels  17.3 us (10%)
  local copies, waits for them, and re-layouts  7.7 us (5%)
  between operations  2.67 us (2%)
  other arithmetic  2.5 us (2%)
    all_to_all x1, blocking collectives, body(): lax.all_to_all(copies, PLANE, 0, 0, tiled=True)  49.3 us
    all_to_all x2, waiting for transfers between devices, sum_parts(): return lax.all_to_all(copies, 'z', 0, 0, tiled=True)  28.4 us
    all_to_all x1, blocking collectives, sum_parts(): return lax.all_to_all(copies, 'z', 0, 0, tiled=True)  16.7 us
    all_to_all x1, blocking collectives, body(): out = lax.all_to_all(out, MEMBERS, 0, 0, tiled=True)  13.5 us
    all_to_all x2, starting transfers between devices, sum_parts(): return lax.all_to_all(copies, 'z', 0, 0, tiled=True)  12.3 us
    all_to_all x1, waiting for transfers between devices, body(): weights = lax.all_to_all(w_turned, MEMBERS, 0, 0, tiled=True)  7.37 us
    pallas_call x1, Pallas kernels, body(): call(step_kernel, (parts_shape, state, state), [SMEM] * 4 + [VMEM] * 4)  5.05 us
    pallas_call x1, Pallas kernels, body(): call(rhs_kernel, (parts_shape, state), [SMEM] * 3 + [VMEM] * 3)  5.01 us
  transfers between devices with their start and end apart: 4, of which 3 were waited for; matrix products, arithmetic and copies ran while one was open for 3% of the time, Pallas kernels for 0%

profile of v1, /device:TPU:1, one launch (start us, length us, event | category | flops | bytes accessed | tf_op | source)
XLA Modules:
  0.0 164.7 jit_solution(8091640892132416588)
XLA Ops:
  0.6 1.0 pad_maximum_fusion
  1.6 0.2 broadcast_in_dim.2
  1.8 49.3 %all_to_all.30 = bf16[16,72,1536]{2,1,0:T(8,128)(2,1)S(1)} all-to-all(bf16[16,72,1536]{2,1,0:T(8,128)(2,1)S(1)} %broadcast_in_dim.2), channel_id=1, replica_groups=mesh['xl'=2,'z'=8,'y'=4,'xh'=2,'core'=2] {'xl','y','xh'}, dimensions={0} | all-to-all | bytes 7077888 | tf_op jit(solution)/shard_map/all_to_all | solution.py:168
  51.2 2.6 %collective-permute-start = (bf16[1152,1536]{1,0:T(8,128)(2,1)S(1)}, bf16[1152,1536]{1,0:T(8,128)(2,1)}, u32[]{:S(2)}, u32[]{:S(2)}) collective-permute-start(bf16[1152,1536]{1,0:T(8,128)(2,1)S(1)} %bitcast.14), channel_id=1, source_target_pairs={{0,1},{1,0},{2,3},{3,2},{4,5},{5,4},{6,7},{7,6},{8,9},{9,8},{10,11... | collective-permute-start | bytes 10616840 | tf_op jit(solution)/shard_map/ppermute | solution.py:169
  53.7 1.5 copy.10
  55.2 1.5 copy.11
  56.7 1.5 pad_maximum_fusion.1
  58.3 4.3 %all-to-all-start = ((bf16[32,16,72]{2,1,0:T(8,128)(2,1)}), bf16[32,16,72]{2,1,0:T(8,128)(2,1)}, u32[]{:S(2)}, u32[]{:S(2)}) async-start(bf16[32,16,72]{2,1,0:T(8,128)(2,1)} %pad_maximum_fusion.1), calls=%async_computation | async-start | bytes 262144 | tf_op jit(solution)/shard_map/all_to_all | solution.py:166
  62.6 7.4 %all-to-all-done.w_ref = bf16[32,16,72]{2,1,0:T(8,128)(2,1)} async-done(((bf16[32,16,72]{2,1,0:T(8,128)(2,1)}), bf16[32,16,72]{2,1,0:T(8,128)(2,1)}, u32[]{:S(2)}, u32[]{:S(2)}) %all-to-all-start) | async-done | bytes 73760 | tf_op jit(solution)/shard_map/all_to_all | solution.py:166
  70.0 0.0 collective-permute-done.other_ref
  70.0 0.0 copy-start.5
  70.0 3.2 %shard_map.95 = f32[8,8,1536]{2,1,0:T(8,128)S(1)} custom-call(s32[1]{0:T(128)} %bitcast.core_ref, bf16[32,16,72]{2,1,0:T(8,128)(2,1)} %all-to-all-done.w_ref, bf16[1152,1536]{1,0:T(8,128)(2,1)S(1)} %bitcast.15, bf16[1152,1536]{1,0:T(8,128)(2,1)} %collective-permute-done.other_ref), custom_call_target="tpu_custom_call" | custom-call | tf_op jit(solution)/shard_map/pallas_call | solution.py:174
  73.2 0.0 copy-start
  73.2 0.7 copy-done
  74.0 8.2 %all-to-all-start.2 = ((f32[8,8,1536]{2,1,0:T(8,128)}), f32[8,8,1536]{2,1,0:T(8,128)}, u32[]{:S(2)}, u32[]{:S(2)}) async-start(f32[8,8,1536]{2,1,0:T(8,128)} %copy-done), calls=%async_computation.2 | async-start | bytes 786432 | tf_op jit(solution)/shard_map/all_to_all | solution.py:150
  83.4 13.9 %all-to-all-done.2.parts_ref = f32[8,8,1536]{2,1,0:T(8,128)} async-done(((f32[8,8,1536]{2,1,0:T(8,128)}), f32[8,8,1536]{2,1,0:T(8,128)}, u32[]{:S(2)}, u32[]{:S(2)}) %all-to-all-start.2) | async-done | bytes 393248 | tf_op jit(solution)/shard_map/all_to_all | solution.py:150
  97.3 0.0 copy-done.5
  97.3 5.0 %shard_map.96 = (f32[8,8,1536]{2,1,0:T(8,128)S(1)}, f32[2,8,1152]{2,1,0:T(8,128)S(1)}) custom-call(s32[2]{0:T(128)S(1)} %copy-done.5, f32[1]{0:T(128)S(6)} %copy.15.low_ref, f32[1]{0:T(128)S(6)} %copy.16.high_ref, f32[8,8,1536]{2,1,0:T(8,128)} %all-to-all-done.2.parts_ref, bf16[1152,1536]{1,0:T(8,128)(2,1)S(1)} %bitcast.16, ...), custom_call_target="tpu_custom_call" | custom-call | tf_op jit(solution)/shard_map/pallas_call | solution.py:178
  102.4 0.0 copy-start.1
  102.4 0.7 copy-done.1
  103.1 0.0 copy-start.2
  103.1 0.6 copy-done.2
  103.7 4.1 %all-to-all-start.3 = ((f32[8,8,1536]{2,1,0:T(8,128)}), f32[8,8,1536]{2,1,0:T(8,128)}, u32[]{:S(2)}, u32[]{:S(2)}) async-start(f32[8,8,1536]{2,1,0:T(8,128)} %copy-done.1), calls=%async_computation.3 | async-start | bytes 786432 | tf_op jit(solution)/shard_map/all_to_all | solution.py:150
  108.5 14.5 %all-to-all-done.3.parts_ref = f32[8,8,1536]{2,1,0:T(8,128)} async-done(((f32[8,8,1536]{2,1,0:T(8,128)}), f32[8,8,1536]{2,1,0:T(8,128)}, u32[]{:S(2)}, u32[]{:S(2)}) %all-to-all-start.3) | async-done | bytes 393248 | tf_op jit(solution)/shard_map/all_to_all | solution.py:150
  123.0 0.9 copy-done.3
  123.9 5.1 %shard_map.97 = (f32[8,8,1536]{2,1,0:T(8,128)S(1)}, f32[2,8,1152]{2,1,0:T(8,128)S(1)}, f32[2,8,1152]{2,1,0:T(8,128)S(1)}) custom-call(s32[2]{0:T(128)S(1)} %copy-done.5, f32[1]{0:T(128)S(6)} %copy.15.low_ref, f32[1]{0:T(128)S(6)} %copy.16.high_ref, f32[1]{0:T(128)S(6)} %copy.14.ridge_ref, f32[8,8,1536]{2,1,0:T(8,128)} %all-to-all-done.3.parts_ref, ...), custom_call_target="tpu_custom_call" | custom-call | tf_op jit(solution)/shard_map/pallas_call | solution.py:182
  128.9 16.7 %all_to_all.31.parts_ref = f32[8,8,1536]{2,1,0:T(8,128)S(1)} all-to-all(f32[8,8,1536]{2,1,0:T(8,128)S(1)} %get-tuple-element.9), channel_id=1, replica_groups=mesh['xl'=2,'z'=8,'y'=4,'xh'=2,'core'=2] {'z'}, dimensions={0} | all-to-all | bytes 786432 | tf_op jit(solution)/shard_map/all_to_all | solution.py:150
  145.6 0.0 copy-done.4
  145.6 4.0 %shard_map.98 = f32[32,16,72]{2,1,0:T(8,128)S(1)} custom-call(s32[1]{0:T(128)} %bitcast.core_ref, s32[2]{0:T(128)S(1)} %copy-done.5, f32[1]{0:T(128)S(6)} %copy.15.low_ref, f32[1]{0:T(128)S(6)} %copy.16.high_ref, f32[1]{0:T(128)S(6)} %copy.14.ridge_ref, f32[8,8,1536]{2,1,0:T(8,128)S(1)} %all_to_all.31.parts_ref, bf16[1152,1536]{1,0:T(8,128)(2,1)S(1)} %bitcast.18, ...), custom_call_target="tpu_custom_call" | custom-call | tf_op jit(solution)/shard_map/pallas_call | solution.py:186
  149.7 13.5 %all_to_all.32 = f32[32,16,72]{2,1,0:T(8,128)S(1)} all-to-all(f32[32,16,72]{2,1,0:T(8,128)S(1)} %shard_map.98), channel_id=1, replica_groups=mesh['xl'=2,'z'=8,'y'=4,'xh'=2,'core'=2] {'xl','y','xh','core'}, dimensions={0} | all-to-all | bytes 294912 | tf_op jit(solution)/shard_map/all_to_all | solution.py:192
  163.2 0.7 copy.13
  164.0 0.7 copy.12
  (3 shorter events, 0.0 us)
Async XLA Ops:
  51.2 18.8 %collective-permute-start = (bf16[1152,1536]{1,0:T(8,128)(2,1)S(1)}, bf16[1152,1536]{1,0:T(8,128)(2,1)}, u32[]{:S(2)}, u32[]{:S(2)}) collective-permute-start(bf16[1152,1536]{1,0:T(8,128)(2,1)S(1)} %bitcast.14), channel_id=1, source_target_pairs={{0,1},{1,0},{2,3},{3,2},{4,5},{5,4},{6,7},{7,6},{8,9},{9,8},{10,11... | collective-permute-start | bytes 10616840 | tf_op jit(solution)/shard_map/ppermute | solution.py:169
  58.3 11.7 %all-to-all-start = ((bf16[32,16,72]{2,1,0:T(8,128)(2,1)}), bf16[32,16,72]{2,1,0:T(8,128)(2,1)}, u32[]{:S(2)}, u32[]{:S(2)}) async-start(bf16[32,16,72]{2,1,0:T(8,128)(2,1)} %pad_maximum_fusion.1), calls=%async_computation | async-start | bytes 262144 | tf_op jit(solution)/shard_map/all_to_all | solution.py:166
  70.0 27.3 %copy-start.5 = (s32[2]{0:T(128)S(1)}, s32[2]{0:T(128)}, u32[]{:S(2)}) copy-start(s32[2]{0:T(128)} %counts_ref.5) | copy-start | bytes 28
  73.2 0.8 copy-start
  74.0 23.4 %all-to-all-start.2 = ((f32[8,8,1536]{2,1,0:T(8,128)}), f32[8,8,1536]{2,1,0:T(8,128)}, u32[]{:S(2)}, u32[]{:S(2)}) async-start(f32[8,8,1536]{2,1,0:T(8,128)} %copy-done), calls=%async_computation.2 | async-start | bytes 786432 | tf_op jit(solution)/shard_map/all_to_all | solution.py:150
  102.4 0.8 copy-start.1
  103.1 0.6 copy-start.2
  103.7 19.2 %all-to-all-start.3 = ((f32[8,8,1536]{2,1,0:T(8,128)}), f32[8,8,1536]{2,1,0:T(8,128)}, u32[]{:S(2)}, u32[]{:S(2)}) async-start(f32[8,8,1536]{2,1,0:T(8,128)} %copy-done.1), calls=%async_computation.3 | async-start | bytes 786432 | tf_op jit(solution)/shard_map/all_to_all | solution.py:150
  123.0 0.9 copy-start.3
  123.9 21.8 %copy-start.4 = (f32[2,8,1152]{2,1,0:T(8,128)S(1)}, f32[2,8,1152]{2,1,0:T(8,128)}, u32[]{:S(2)}) copy-start(f32[2,8,1152]{2,1,0:T(8,128)} %copy-done.2) | copy-start | bytes 221188

commit v2 on v1

v2 whole, which is shorter than its diff:
```python
import jax
import jax.numpy as jnp
from jax import lax
from jax.experimental import pallas as pl
from jax.experimental.pallas import tpu as pltpu
from jax.sharding import Mesh
from jax.sharding import PartitionSpec as P

AXES = ("xl", "z", "y", "xh", "core")
MEMBERS = ("xl", "y", "xh", "core")
SIDE = 4
ORDER = (0, 1, 3, 2)
NT = (((1,), (1,)), ((), ()))
NN = (((1,), (0,)), ((), ()))
VMEM = pl.BlockSpec(memory_space=pltpu.VMEM)
SMEM = pl.BlockSpec(memory_space=pltpu.SMEM)


def member(x, y, core):
    return (((x % 2) * SIDE + y) * 2 + x // 2) * 2 + core


def ring_pairs(shift, first):
    pairs = []
    for x in range(SIDE):
        for y in range(SIDE):
            for core in range(2):
                if (core == 0) == first:
                    to = member(x, (y + shift) % SIDE, core)
                else:
                    to = member((x + shift) % SIDE, y, core)
                pairs.append((member(x, y, core), to))
    return pairs


def along(value, shift, first):
    return lax.ppermute(value, MEMBERS, ring_pairs(shift, first))


def swap(value):
    return lax.ppermute(value, "core", [(0, 1), (1, 0)])


def split_two(value):
    head = value.astype(jnp.bfloat16)
    tail = (value - head.astype(jnp.float32)).astype(jnp.bfloat16)
    return jnp.concatenate([head, tail], axis=0)


def times(value, feats, dims):
    out = lax.dot_general(split_two(value), feats, dims, preferred_element_type=jnp.float32)
    half = out.shape[0] // 2
    return out[:half] + out[half:]


def send_all(partial, out_ref):
    for k in range(out_ref.shape[0]):
        out_ref[k] = partial


def source(place_ref, first, second):
    x, y, core = place_ref[0], place_ref[1], place_ref[2]
    back_x = jnp.where(core == 0, second, first)
    back_y = jnp.where(core == 0, first, second)
    at_x = lax.rem(x + SIDE - back_x, SIDE)
    at_y = lax.rem(y + SIDE - back_y, SIDE)
    return ((lax.rem(at_x, 2) * SIDE + at_y) * 2 + lax.div(at_x, 2)) * 2


def piece(refs, outer, inner):
    deep = refs[0].shape[0] // SIDE
    if outer < 3:
        return refs[outer][inner * deep : (inner + 1) * deep]
    ref = refs[3 + inner // 2]
    return ref[(inner % 2) * deep : (inner % 2 + 1) * deep]


def start_kernel(place_ref, counts_ref, low_ref, high_ref, ridge_ref, w_ref, *refs):
    mine, theirs = refs[:5], refs[5:10]
    feats_ref, out_ref, scale_ref, coef_ref, held = refs[10:]
    core = place_ref[2]
    deep = mine[0].shape[0] // SIDE
    rows = mine[0].shape[1]
    width = deep // 2
    cols = w_ref.shape[2]
    for outer in range(SIDE):
        for inner in range(SIDE):
            at = (outer * SIDE + inner) * deep
            feats_ref[at : at + deep, :rows] = piece(mine, outer, inner)
            feats_ref[at : at + deep, rows:] = piece(theirs, inner, outer)
            origin = source(place_ref, ORDER[inner], ORDER[outer])
            for k in range(2):
                here = at + k * width
                held[:cols, here : here + width] = w_ref[origin + k, core].astype(jnp.float32)
                held[cols:, here : here + width] = w_ref[origin + k, 1 - core].astype(jnp.float32)
    weights = held[...].astype(jnp.bfloat16)
    first = lax.dot_general(
        weights[:cols], feats_ref[:, :rows], NN, preferred_element_type=jnp.float32
    )
    second = lax.dot_general(
        weights[cols:], feats_ref[:, rows:], NN, preferred_element_type=jnp.float32
    )
    send_all(jnp.concatenate([first, second], axis=1), out_ref)

    position = lax.broadcasted_iota(jnp.int32, (1, 2 * rows), 1)
    other = position >= rows
    within = jnp.where(other, position - rows, position)
    used = jnp.where(other, counts_ref[1 - core], counts_ref[core])
    scale_ref[...] = jnp.where(within < used, 1.0 / used.astype(jnp.float32), 0.0)

    one = jnp.ones((1, 128), jnp.float32)
    low, high = one * low_ref[0], one * high_ref[0]
    middle, radius = (high + low) / 2.0, (high - low) / 2.0
    sigma = middle / radius
    rho = 1.0 / sigma
    rho_new = 1.0 / (2.0 * sigma - rho)
    coef_ref[0:1] = middle
    coef_ref[1:2] = one * ridge_ref[0]
    coef_ref[2:3] = rho_new * rho
    coef_ref[3:4] = 2.0 * rho_new / radius


def ahead(direction, scale_ref, feats_ref, out_ref):
    feats = feats_ref[...]
    send_all(times(times(direction * scale_ref[...], feats, NT), feats, NN), out_ref)


def rhs_kernel(coef_ref, scale_ref, parts_ref, feats_ref, out_ref, rhs_ref):
    rhs = jnp.sum(parts_ref[...], axis=0)
    rhs_ref[...] = rhs
    ahead(rhs / coef_ref[0:1, 0:1], scale_ref, feats_ref, out_ref)


def step_kernel(coef_ref, scale_ref, parts_ref, feats_ref, rhs_ref, out_ref, dir_ref, res_ref):
    first = rhs_ref[...] / coef_ref[0:1, 0:1]
    image = jnp.sum(parts_ref[...], axis=0) + coef_ref[1:2, 0:1] * first
    residual = rhs_ref[...] - image
    direction = coef_ref[2:3, 0:1] * first + coef_ref[3:4, 0:1] * residual
    dir_ref[...] = direction
    res_ref[...] = residual
    ahead(direction, scale_ref, feats_ref, out_ref)


def last_kernel(
    place_ref, coef_ref, scale_ref, parts_ref, feats_ref, rhs_ref, dir_ref, res_ref, out_ref, held
):
    direction = dir_ref[...]
    image = jnp.sum(parts_ref[...], axis=0) + coef_ref[1:2, 0:1] * direction
    residual = res_ref[...] - image
    merged = rhs_ref[...] / coef_ref[0:1, 0:1] + direction
    both = jnp.concatenate([merged, residual], axis=0) * scale_ref[...]
    held[...] = times(both, feats_ref[...], NT)
    width = out_ref.shape[2]
    for outer in range(SIDE):
        for inner in range(SIDE):
            at = (outer * SIDE + inner) * 2 * width
            origin = source(place_ref, ORDER[inner], ORDER[outer])
            for k in range(2):
                out_ref[origin + k] = held[:, at + k * width : at + (k + 1) * width]


def call(kernel, outs, specs, scratch=()):
    return pl.pallas_call(
        kernel,
        out_shape=outs,
        in_specs=specs,
        out_specs=jax.tree.map(lambda _: VMEM, outs),
        scratch_shapes=list(scratch),
        compiler_params=pltpu.CompilerParams(vmem_limit_bytes=32 * 1024 * 1024),
    )


def sum_parts(copies):
    return lax.all_to_all(copies, "z", 0, 0, tiled=True)


def body(x_first, x_second, w_first, w_second, counts, damping, eig_low, eig_high):
    f32 = jnp.float32
    shape = jax.ShapeDtypeStruct
    rows, width = x_first.shape
    members = lax.axis_size(MEMBERS)
    depth = lax.axis_size("z")
    cols = w_first.shape[1] // members
    core = lax.axis_index("core")
    place = jnp.stack([lax.axis_index("xh") * 2 + lax.axis_index("xl"), lax.axis_index("y"), core])
    place = place.astype(jnp.int32)

    w_turned = jnp.stack(
        [w.T.reshape(members, cols, width) for w in (w_first, w_second)], axis=1
    )
    lead = core == 0
    mine = jnp.where(lead, x_first, x_second).T
    give = jnp.where(lead, x_second, x_first).T
    got = swap(give)
    block = jnp.where(
        lead, jnp.concatenate([mine, got], axis=0), jnp.concatenate([got, mine], axis=0)
    )
    near = jnp.concatenate([block] + [along(block, k, True) for k in ORDER[1:]], axis=0)
    near, w_turned = lax.optimization_barrier((near, w_turned))
    back, front = along(near, 1, False), along(near, 3, False)
    weights = lax.all_to_all(w_turned, MEMBERS, 0, 0, tiled=True)
    back, front, weights = lax.optimization_barrier((back, front, weights))
    half = near.shape[0] // 2
    far_low, far_high = along(back[:half], 1, False), along(front[half:], 3, False)
    pieces = [near, back, front, far_low, far_high]
    swapped = [swap(p) for p in pieces]


    total = members * width
    copies = shape((depth, cols, 2 * rows), f32)
    state = shape((cols, 2 * rows), f32)
    feats, parts, scale, coef = call(
        start_kernel,
        (
            shape((total, 2 * rows), jnp.bfloat16),
            copies,
            shape((1, 2 * rows), f32),
            shape((4, 128), f32),
        ),
        [SMEM] * 5 + [VMEM] * 11,
        [pltpu.VMEM((2 * cols, total), f32)],
    )(place, counts, eig_low, eig_high, damping, weights, *pieces, *swapped)
    parts = sum_parts(parts)
    parts, rhs = call(rhs_kernel, (copies, state), [VMEM] * 4)(coef, scale, parts, feats)
    parts = sum_parts(parts)
    parts, direction, residual = call(step_kernel, (copies, state, state), [VMEM] * 5)(
        coef, scale, parts, feats, rhs
    )
    parts = sum_parts(parts)
    out = call(
        last_kernel,
        shape((members, 2 * cols, width), f32),
        [SMEM] + [VMEM] * 7,
        [pltpu.VMEM((2 * cols, total), f32)],
    )(place, coef, scale, parts, feats, rhs, direction, residual)
    out = lax.all_to_all(out, MEMBERS, 0, 0, tiled=True)
    merged = out[:, :cols].reshape(members * cols, width).T
    residual = out[:, cols:].reshape(members * cols, width).T
    return merged, residual


def solution(mesh):
    fine = Mesh(mesh.devices.reshape(2, 8, SIDE, 2, 2), AXES)
    return jax.shard_map(
        body,
        mesh=fine,
        in_specs=(
            P(None, AXES),
            P(None, AXES),
            P(AXES, None),
            P(AXES, None),
            P(),
            P(),
            P(),
            P(),
        ),
        out_specs=(P(AXES, None), P(AXES, None)),
        check_vma=False,
    )
```

time: 165 us -> 132 us (0.80)
  waiting for transfers between devices: 35.8 us -> 21.1 us
  blocking collectives: 79.6 us -> 70.1 us
  Pallas kernels: 17.3 us -> 12.4 us
  local copies, waits for them, and re-layouts: 7.7 us -> 3.28 us
    all_to_all x1 -> x0, blocking collectives: 49.3 us -> none  [body(): lax.all_to_all(copies, PLANE, 0, 0, tiled=True)]
    all_to_all x1 -> x3, blocking collectives: 16.7 us -> 55.1 us  [sum_parts(): return lax.all_to_all(copies, 'z', 0, 0, tiled=True)]
    all_to_all x2 -> x0, waiting for transfers between devices: 28.4 us -> none  [sum_parts(): return lax.all_to_all(copies, 'z', 0, 0, tiled=True)]
    all_to_all x2 -> x0, starting transfers between devices: 12.3 us -> none  [sum_parts(): return lax.all_to_all(copies, 'z', 0, 0, tiled=True)]
    ppermute x1 -> x13, waiting for transfers between devices: 0.01 us -> 11.1 us  [the longest x7 10.1 us: along(): return lax.ppermute(value, MEMBERS, ring_pairs(shift, first))]
    ppermute x1 -> x13, starting transfers between devices: 2.57 us -> 12.4 us  [the longest x6 6.33 us: swap(): return lax.ppermute(value, 'core', [(0, 1), (1, 0)])]
    pallas_call x4, Pallas kernels: 17.3 us -> 12.4 us  [the longest x1 3.25 us: body(): call(step_kernel, (copies, state, state), [VMEM] * 5)]
    all_to_all x1, starting transfers between devices: 4.35 us -> 7.77 us  [body(): weights = lax.all_to_all(w_turned, MEMBERS, 0, 0, tiled=True)]
  transfers between devices with their start and end apart: 4 -> 14, of which waited for: 3 -> 7; matrix products, arithmetic and copies ran while one was open for 3% -> 2% of each run, Pallas kernels for 0% -> 0%
where the time goes in v2:
time: 132 us
  blocking collectives  70.1 us (53%)
  waiting for transfers between devices  21.1 us (16%)
  starting transfers between devices  20.2 us (15%)
  Pallas kernels  12.4 us (9%)
  local copies, waits for them, and re-layouts  3.28 us (2%)
  between operations  2.69 us (2%)
  other arithmetic  1.83 us (1%)
    all_to_all x3, blocking collectives, sum_parts(): return lax.all_to_all(copies, 'z', 0, 0, tiled=True)  55.1 us
    all_to_all x1, blocking collectives, body(): out = lax.all_to_all(out, MEMBERS, 0, 0, tiled=True)  15 us
    ppermute x7, waiting for transfers between devices, along(): return lax.ppermute(value, MEMBERS, ring_pairs(shift, first))  10.1 us
    all_to_all x1, waiting for transfers between devices, body(): weights = lax.all_to_all(w_turned, MEMBERS, 0, 0, tiled=True)  9.98 us
    all_to_all x1, starting transfers between devices, body(): weights = lax.all_to_all(w_turned, MEMBERS, 0, 0, tiled=True)  7.77 us
    ppermute x6, starting transfers between devices, swap(): return lax.ppermute(value, 'core', [(0, 1), (1, 0)])  6.33 us
    ppermute x7, starting transfers between devices, along(): return lax.ppermute(value, MEMBERS, ring_pairs(shift, first))  6.08 us
    pallas_call x1, Pallas kernels, body(): call(step_kernel, (copies, state, state), [VMEM] * 5)  3.25 us
  transfers between devices with their start and end apart: 14, of which 7 were waited for; matrix products, arithmetic and copies ran while one was open for 2% of the time, Pallas kernels for 0%

profile of v2, /device:TPU:1, one launch (start us, length us, event | category | flops | bytes accessed | tf_op | source)
XLA Modules:
  0.0 131.6 jit_solution(14227549355001902084)
XLA Ops:
  0.6 1.0 select_bitcast_fusion.1
  1.6 3.3 %collective-permute-start = (bf16[72,768]{1,0:T(8,128)(2,1)S(1)}, bf16[72,768]{1,0:T(8,128)(2,1)S(1)}, u32[]{:S(2)}, u32[]{:S(2)}) collective-permute-start(bf16[72,768]{1,0:T(8,128)(2,1)S(1)} %get-tuple-element.33), channel_id=1, source_target_pairs={{0,1},{1,0},{2,3},{3,2},{4,5},{5,4},{6,7},{7,6},{8,9},{9,8},{10,11... | collective-permute-start | bytes 331784 | tf_op jit(solution)/shard_map/ppermute | solution.py:41
  4.9 1.0 collective-permute-done
  5.9 1.1 collective-permute-start.3
  7.0 0.9 collective-permute-start.2
  7.9 0.6 collective-permute-start.1
  8.5 0.9 copy.10
  9.4 0.9 copy.11
  10.3 0.7 pad_maximum_fusion.1
  11.0 1.6 %collective-permute-done.3 = bf16[144,768]{1,0:T(8,128)(2,1)S(1)} collective-permute-done((bf16[144,768]{1,0:T(8,128)(2,1)S(1)}, bf16[144,768]{1,0:T(8,128)(2,1)S(1)}, u32[]{:S(2)}, u32[]{:S(2)}) %collective-permute-start.3) | collective-permute-done | bytes 221216 | tf_op jit(solution)/shard_map/ppermute | solution.py:37
  12.6 0.7 collective-permute-done.2
  13.3 1.6 %collective-permute-done.1 = bf16[144,768]{1,0:T(8,128)(2,1)S(1)} collective-permute-done((bf16[144,768]{1,0:T(8,128)(2,1)S(1)}, bf16[144,768]{1,0:T(8,128)(2,1)S(1)}, u32[]{:S(2)}, u32[]{:S(2)}) %collective-permute-start.1) | collective-permute-done | bytes 221216 | tf_op jit(solution)/shard_map/ppermute | solution.py:37
  15.0 1.9 %collective-permute-start.5 = (bf16[576,768]{1,0:T(8,128)(2,1)S(1)}, bf16[576,768]{1,0:T(8,128)(2,1)S(1)}, u32[]{:S(2)}, u32[]{:S(2)}) collective-permute-start(bf16[576,768]{1,0:T(8,128)(2,1)S(1)} %pad_maximum_fusion.refs_0_), channel_id=1, source_target_pairs={{0,130},{1,13},{4,134},{5,1},{8,138},{9,5},{12,142},{13,9},{128,0}... | collective-permute-start | bytes 2654216 | tf_op jit(solution)/shard_map/ppermute | solution.py:37
  16.9 7.8 %all-to-all-start = ((bf16[32,2,8,72]{3,2,1,0:T(8,128)(2,1)}), bf16[32,2,8,72]{3,2,1,0:T(8,128)(2,1)}, u32[]{:S(2)}, u32[]{:S(2)}) async-start(bf16[32,2,8,72]{3,2,1,0:T(8,128)(2,1)} %pad_maximum_fusion.1), calls=%async_computation | async-start | bytes 262144 | tf_op jit(solution)/shard_map/all_to_all | solution.py:201
  24.7 0.4 collective-permute-start.8
  25.1 10.0 %all-to-all-done.w_ref = bf16[32,2,8,72]{3,2,1,0:T(8,128)(2,1)} async-done(((bf16[32,2,8,72]{3,2,1,0:T(8,128)(2,1)}), bf16[32,2,8,72]{3,2,1,0:T(8,128)(2,1)}, u32[]{:S(2)}, u32[]{:S(2)}) %all-to-all-start) | async-done | bytes 73760 | tf_op jit(solution)/shard_map/all_to_all | solution.py:201
  35.1 1.2 collective-permute-start.7
  36.3 0.4 collective-permute-start.6
  36.8 1.0 collective-permute-start.9
  37.7 5.0 %collective-permute-done.7.refs_4_ = bf16[288,768]{1,0:T(8,128)(2,1)} collective-permute-done((bf16[288,768]{1,0:T(8,128)(2,1)S(1)}, bf16[288,768]{1,0:T(8,128)(2,1)}, u32[]{:S(2)}, u32[]{:S(2)}) %collective-permute-start.7) | collective-permute-done | bytes 442400 | tf_op jit(solution)/shard_map/ppermute | solution.py:37
  42.8 1.2 collective-permute-start.12
  44.0 1.1 collective-permute-done.6.refs_3_
  47.6 3.1 %shard_map.95 = (bf16[2304,1536]{1,0:T(8,128)(2,1)S(1)}, f32[8,8,1536]{2,1,0:T(8,128)S(1)}, f32[1,1536]{1,0:T(1,128)S(1)}, f32[4,128]{1,0:T(4,128)S(1)}) custom-call(s32[3]{0:T(128)S(1)} %pad_add_fusion.place_ref, s32[2]{0:T(128)S(1)} %copy-done, f32[1]{0:T(128)S(6)} %copy.15.low_ref, f32[1]{0:T(128)S(6)} %copy.16.high_ref, f32[1]{0:T(128)S(6)} %copy.14.ridge_ref, ...), custom_call_target="tpu_custom_call" | custom-call | tf_op jit(solution)/shard_map/pallas_call | solution.py:212
  50.7 23.1 %all_to_all.25.parts_ref = f32[8,8,1536]{2,1,0:T(8,128)S(1)} all-to-all(f32[8,8,1536]{2,1,0:T(8,128)S(1)} %get-tuple-element.23), channel_id=1, replica_groups=mesh['xl'=2,'z'=8,'y'=4,'xh'=2,'core'=2] {'z'}, dimensions={0} | all-to-all | bytes 786432 | tf_op jit(solution)/shard_map/all_to_all | solution.py:174
  73.8 3.2 %shard_map.96 = (f32[8,8,1536]{2,1,0:T(8,128)S(1)}, f32[8,1536]{1,0:T(8,128)S(1)}) custom-call(f32[4,128]{1,0:T(4,128)S(1)} %get-tuple-element.21.coef_ref, f32[1,1536]{1,0:T(1,128)S(1)} %get-tuple-element.22.scale_ref, f32[8,8,1536]{2,1,0:T(8,128)S(1)} %all_to_all.25.parts_ref, bf16[2304,1536]{1,0:T(8,128)(2,1)S(1)} %get-tuple-element.24.feats_ref), custom_call_target="tpu_custom_call" | custom-call | tf_op jit(solution)/shard_map/pallas_call | solution.py:224
  77.1 16.6 %all_to_all.26.parts_ref = f32[8,8,1536]{2,1,0:T(8,128)S(1)} all-to-all(f32[8,8,1536]{2,1,0:T(8,128)S(1)} %get-tuple-element.25), channel_id=1, replica_groups=mesh['xl'=2,'z'=8,'y'=4,'xh'=2,'core'=2] {'z'}, dimensions={0} | all-to-all | bytes 786432 | tf_op jit(solution)/shard_map/all_to_all | solution.py:174
  93.6 3.2 %shard_map.97 = (f32[8,8,1536]{2,1,0:T(8,128)S(1)}, f32[8,1536]{1,0:T(8,128)S(1)}, f32[8,1536]{1,0:T(8,128)S(1)}) custom-call(f32[4,128]{1,0:T(4,128)S(1)} %get-tuple-element.21.coef_ref, f32[1,1536]{1,0:T(1,128)S(1)} %get-tuple-element.22.scale_ref, f32[8,8,1536]{2,1,0:T(8,128)S(1)} %all_to_all.26.parts_ref, ...), custom_call_target="tpu_custom_call" | custom-call | tf_op jit(solution)/shard_map/pallas_call | solution.py:226
  96.9 15.5 %all_to_all.27.parts_ref = f32[8,8,1536]{2,1,0:T(8,128)S(1)} all-to-all(f32[8,8,1536]{2,1,0:T(8,128)S(1)} %get-tuple-element.27), channel_id=1, replica_groups=mesh['xl'=2,'z'=8,'y'=4,'xh'=2,'core'=2] {'z'}, dimensions={0} | all-to-all | bytes 786432 | tf_op jit(solution)/shard_map/all_to_all | solution.py:174
  112.4 2.8 %shard_map.98 = f32[32,16,72]{2,1,0:T(8,128)S(1)} custom-call(s32[3]{0:T(128)S(1)} %pad_add_fusion.place_ref, f32[4,128]{1,0:T(4,128)S(1)} %get-tuple-element.21.coef_ref, f32[1,1536]{1,0:T(1,128)S(1)} %get-tuple-element.22.scale_ref, f32[8,8,1536]{2,1,0:T(8,128)S(1)} %all_to_all.27.parts_ref, bf16[2304,1536]{1,0:T(8,128)(2,1)S(1)} %get-tuple-element.24.feats_ref, ...), custom_call_target="tpu_custom_call" | custom-call | tf_op jit(solution)/shard_map/pallas_call | solution.py:230
  115.1 15.0 %all_to_all.28 = f32[32,16,72]{2,1,0:T(8,128)S(1)} all-to-all(f32[32,16,72]{2,1,0:T(8,128)S(1)} %shard_map.98), channel_id=1, replica_groups=mesh['xl'=2,'z'=8,'y'=4,'xh'=2,'core'=2] {'xl','y','xh','core'}, dimensions={0} | all-to-all | bytes 294912 | tf_op jit(solution)/shard_map/all_to_all | solution.py:236
  130.1 0.7 copy.13
  130.8 0.7 copy.12
  (18 shorter events, 0.7 us)
Async XLA Ops:
  1.6 4.3 %collective-permute-start = (bf16[72,768]{1,0:T(8,128)(2,1)S(1)}, bf16[72,768]{1,0:T(8,128)(2,1)S(1)}, u32[]{:S(2)}, u32[]{:S(2)}) collective-permute-start(bf16[72,768]{1,0:T(8,128)(2,1)S(1)} %get-tuple-element.33), channel_id=1, source_target_pairs={{0,1},{1,0},{2,3},{3,2},{4,5},{5,4},{6,7},{7,6},{8,9},{9,8},{10,11... | collective-permute-start | bytes 331784 | tf_op jit(solution)/shard_map/ppermute | solution.py:41
  5.9 6.7 %collective-permute-start.3 = (bf16[144,768]{1,0:T(8,128)(2,1)S(1)}, bf16[144,768]{1,0:T(8,128)(2,1)S(1)}, u32[]{:S(2)}, u32[]{:S(2)}) collective-permute-start(bf16[144,768]{1,0:T(8,128)(2,1)S(1)} %maximum_select_fusion), channel_id=1, source_target_pairs={{0,8},{1,3},{4,12},{5,7},{8,0},{9,11},{12,4},{13,15},{128,136},{12... | collective-permute-start | bytes 663560 | tf_op jit(solution)/shard_map/ppermute | solution.py:37
  7.0 6.3 %collective-permute-start.2 = (bf16[144,768]{1,0:T(8,128)(2,1)S(1)}, bf16[144,768]{1,0:T(8,128)(2,1)S(1)}, u32[]{:S(2)}, u32[]{:S(2)}) collective-permute-start(bf16[144,768]{1,0:T(8,128)(2,1)S(1)} %maximum_select_fusion), channel_id=1, source_target_pairs={{0,12},{1,131},{4,0},{5,135},{8,4},{9,139},{12,8},{13,143},{128,14... | collective-permute-start | bytes 663560 | tf_op jit(solution)/shard_map/ppermute | solution.py:37
  7.9 7.1 %collective-permute-start.1 = (bf16[144,768]{1,0:T(8,128)(2,1)S(1)}, bf16[144,768]{1,0:T(8,128)(2,1)S(1)}, u32[]{:S(2)}, u32[]{:S(2)}) collective-permute-start(bf16[144,768]{1,0:T(8,128)(2,1)S(1)} %maximum_select_fusion), channel_id=1, source_target_pairs={{0,4},{1,129},{4,8},{5,133},{8,12},{9,137},{12,0},{13,141},{128,13... | collective-permute-start | bytes 663560 | tf_op jit(solution)/shard_map/ppermute | solution.py:37
  11.0 36.6 %copy-start = (s32[2]{0:T(128)S(1)}, s32[2]{0:T(128)}, u32[]{:S(2)}) copy-start(s32[2]{0:T(128)} %counts_ref.1) | copy-start | bytes 28
  15.0 20.1 %collective-permute-start.5 = (bf16[576,768]{1,0:T(8,128)(2,1)S(1)}, bf16[576,768]{1,0:T(8,128)(2,1)S(1)}, u32[]{:S(2)}, u32[]{:S(2)}) collective-permute-start(bf16[576,768]{1,0:T(8,128)(2,1)S(1)} %pad_maximum_fusion.refs_0_), channel_id=1, source_target_pairs={{0,130},{1,13},{4,134},{5,1},{8,138},{9,5},{12,142},{13,9},{128,0}... | collective-permute-start | bytes 2654216 | tf_op jit(solution)/shard_map/ppermute | solution.py:37
  16.9 18.2 %collective-permute-start.4 = (bf16[576,768]{1,0:T(8,128)(2,1)S(1)}, bf16[576,768]{1,0:T(8,128)(2,1)S(1)}, u32[]{:S(2)}, u32[]{:S(2)}) collective-permute-start(bf16[576,768]{1,0:T(8,128)(2,1)S(1)} %pad_maximum_fusion.refs_0_), channel_id=1, source_target_pairs={{0,128},{1,5},{4,132},{5,9},{8,136},{9,13},{12,140},{13,1},{128,2}... | collective-permute-start | bytes 2654216 | tf_op jit(solution)/shard_map/ppermute | solution.py:37
  16.9 18.2 %all-to-all-start = ((bf16[32,2,8,72]{3,2,1,0:T(8,128)(2,1)}), bf16[32,2,8,72]{3,2,1,0:T(8,128)(2,1)}, u32[]{:S(2)}, u32[]{:S(2)}) async-start(bf16[32,2,8,72]{3,2,1,0:T(8,128)(2,1)} %pad_maximum_fusion.1), calls=%async_computation | async-start | bytes 262144 | tf_op jit(solution)/shard_map/all_to_all | solution.py:201
  24.7 22.8 %collective-permute-start.8 = (bf16[576,768]{1,0:T(8,128)(2,1)S(1)}, bf16[576,768]{1,0:T(8,128)(2,1)S(1)}, u32[]{:S(2)}, u32[]{:S(2)}) collective-permute-start(bf16[576,768]{1,0:T(8,128)(2,1)S(1)} %pad_maximum_fusion.refs_0_), channel_id=1, source_target_pairs={{0,1},{1,0},{2,3},{3,2},{4,5},{5,4},{6,7},{7,6},{8,9},{9,8},{10,11... | collective-permute-start | bytes 2654216 | tf_op jit(solution)/shard_map/ppermute | solution.py:41
  35.1 7.6 %collective-permute-start.7 = (bf16[288,768]{1,0:T(8,128)(2,1)S(1)}, bf16[288,768]{1,0:T(8,128)(2,1)}, u32[]{:S(2)}, u32[]{:S(2)}) collective-permute-start(bf16[288,768]{1,0:T(8,128)(2,1)S(1)} %slice.13), channel_id=1, source_target_pairs={{0,130},{1,13},{4,134},{5,1},{8,138},{9,5},{12,142},{13,9},{128,0}... | collective-permute-start | bytes 1327112 | tf_op jit(solution)/shard_map/ppermute | solution.py:37
  36.3 8.8 %collective-permute-start.6 = (bf16[288,768]{1,0:T(8,128)(2,1)S(1)}, bf16[288,768]{1,0:T(8,128)(2,1)}, u32[]{:S(2)}, u32[]{:S(2)}) collective-permute-start(bf16[288,768]{1,0:T(8,128)(2,1)S(1)} %slice.12), channel_id=1, source_target_pairs={{0,128},{1,5},{4,132},{5,9},{8,136},{9,13},{12,140},{13,1},{128,2}... | collective-permute-start | bytes 1327112 | tf_op jit(solution)/shard_map/ppermute | solution.py:37
  36.8 10.8 %collective-permute-start.9 = (bf16[576,768]{1,0:T(8,128)(2,1)S(1)}, bf16[576,768]{1,0:T(8,128)(2,1)}, u32[]{:S(2)}, u32[]{:S(2)}) collective-permute-start(bf16[576,768]{1,0:T(8,128)(2,1)S(1)} %collective-permute-done.4.refs_1_), channel_id=1, source_target_pairs={{0,1},{1,0},{2,3},{3,2},{4,5},{5,4},{6,7},{7,6},{8,9},{9,8},{10,11... | collective-permute-start | bytes 2654216 | tf_op jit(solution)/shard_map/ppermute | solution.py:41
  37.7 9.8 %collective-permute-start.10 = (bf16[576,768]{1,0:T(8,128)(2,1)S(1)}, bf16[576,768]{1,0:T(8,128)(2,1)}, u32[]{:S(2)}, u32[]{:S(2)}) collective-permute-start(bf16[576,768]{1,0:T(8,128)(2,1)S(1)} %collective-permute-done.5.refs_2_), channel_id=1, source_target_pairs={{0,1},{1,0},{2,3},{3,2},{4,5},{5,4},{6,7},{7,6},{8,9},{9,8},{10,11... | collective-permute-start | bytes 2654216 | tf_op jit(solution)/shard_map/ppermute | solution.py:41
  42.8 4.8 %collective-permute-start.12 = (bf16[288,768]{1,0:T(8,128)(2,1)}, bf16[288,768]{1,0:T(8,128)(2,1)}, u32[]{:S(2)}, u32[]{:S(2)}) collective-permute-start(bf16[288,768]{1,0:T(8,128)(2,1)} %collective-permute-done.7.refs_4_), channel_id=1, source_target_pairs={{0,1},{1,0},{2,3},{3,2},{4,5},{5,4},{6,7},{7,6},{8,9},{9,8},{10,11... | collective-permute-start | bytes 1327112 | tf_op jit(solution)/shard_map/ppermute | solution.py:41
  45.1 2.4 %collective-permute-start.11 = (bf16[288,768]{1,0:T(8,128)(2,1)}, bf16[288,768]{1,0:T(8,128)(2,1)}, u32[]{:S(2)}, u32[]{:S(2)}) collective-permute-start(bf16[288,768]{1,0:T(8,128)(2,1)} %collective-permute-done.6.refs_3_), channel_id=1, source_target_pairs={{0,1},{1,0},{2,3},{3,2},{4,5},{5,4},{6,7},{7,6},{8,9},{9,8},{10,11... | collective-permute-start | bytes 1327112 | tf_op jit(solution)/shard_map/ppermute | solution.py:41

commit v3 on v2

--- a/solution.py
+++ b/solution.py
@@ -10,6 +10,10 @@
 MEMBERS = ("xl", "y", "xh", "core")
 SIDE = 4
 ORDER = (0, 1, 3, 2)
+TILE = 128
+STEPS = 256.0
+LARGEST = 32767.0
+SMALLEST = 2.0**-125
 NT = (((1,), (1,)), ((), ()))
 NN = (((1,), (0,)), ((), ()))
 VMEM = pl.BlockSpec(memory_space=pltpu.VMEM)
@@ -53,9 +57,35 @@
     return out[:half] + out[half:]
 
 
+def code(value):
+    rows, lanes = value.shape
+    spot = lax.broadcasted_iota(jnp.int32, (rows, TILE), 1)
+    notes = jnp.zeros((rows, TILE), jnp.float32)
+    pieces = []
+    for t in range(lanes // TILE):
+        tile = value[:, t * TILE : (t + 1) * TILE]
+        peak = jnp.maximum(jnp.max(jnp.abs(tile), axis=1, keepdims=True), SMALLEST)
+        note = jnp.ceil(jnp.log2(peak) * STEPS) + 1.0
+        pieces.append(jnp.round(tile * jnp.exp2(note * (-1.0 / STEPS)) * LARGEST))
+        notes = jnp.where(spot == t, note, notes)
+    return jnp.concatenate(pieces + [notes], axis=1).astype(jnp.int32).astype(jnp.int16)
+
+
+def sum_coded(parts_ref, places):
+    tiles = parts_ref.shape[2] // TILE - 1
+    totals = [0.0] * tiles
+    for place in places:
+        part = parts_ref[place].astype(jnp.int32).astype(jnp.float32)
+        scales = jnp.exp2(part[:, tiles * TILE :] * (1.0 / STEPS))
+        for t in range(tiles):
+            totals[t] = totals[t] + part[:, t * TILE : (t + 1) * TILE] * scales[:, t : t + 1]
+    return jnp.concatenate(totals, axis=1) * (1.0 / LARGEST)
+
+
 def send_all(partial, out_ref):
+    coded = code(partial)
     for k in range(out_ref.shape[0]):
-        out_ref[k] = partial
+        out_ref[k] = coded
 
 
 def source(place_ref, first, second):
@@ -75,32 +105,64 @@
     return ref[(inner % 2) * deep : (inner % 2 + 1) * deep]
 
 
-def start_kernel(place_ref, counts_ref, low_ref, high_ref, ridge_ref, w_ref, *refs):
+def deal_kernel(place_ref, keep_ref, got_ref, *refs):
+    out_refs, (held,) = refs[:SIDE], refs[SIDE:]
+    lead = place_ref[2] == 0
+    keep = keep_ref[...].astype(jnp.float32)
+    got = got_ref[:, got_ref.shape[1] - keep.shape[1] :].astype(jnp.float32)
+    chips, each = held.shape[1:3]
+    for k, rows in enumerate((jnp.where(lead, keep, got), jnp.where(lead, got, keep))):
+        turned = rows.T
+        for chip in range(chips):
+            held[k, chip] = turned[chip * each : (chip + 1) * each]
+    line = jnp.where(lead, place_ref[1], place_ref[0])
+    for k, out_ref in zip(ORDER, out_refs):
+        at = lax.rem(line + k, SIDE)
+        for across in range(SIDE):
+            x, y = jnp.where(lead, across, at), jnp.where(lead, at, across)
+            chip = (lax.rem(x, 2) * SIDE + y) * 2 + lax.div(x, 2)
+            for core in range(2):
+                rows = slice(across * each, (across + 1) * each)
+                out_ref[core, rows] = held[core, chip].astype(out_ref.dtype)
+
+
+def line_kernel(place_ref, near_ref, *refs):
+    w_refs, out_refs, (held, total) = refs[:SIDE], refs[SIDE : 2 * SIDE], refs[2 * SIDE :]
+    width = w_refs[0].shape[2]
+    for j, w_ref in enumerate(w_refs):
+        for k in range(2):
+            at = (2 * j + k) * width
+            held[:, at : at + width] = w_ref[k].astype(jnp.float32)
+    out = lax.dot_general(
+        held[...].astype(jnp.bfloat16), near_ref[...], NN, preferred_element_type=jnp.float32
+    )
+    each = out.shape[0] // SIDE
+    for k in range(SIDE):
+        total[k] = out[k * each : (k + 1) * each]
+    across = jnp.where(place_ref[2] == 0, place_ref[0], place_ref[1])
+    for k, out_ref in zip(ORDER, out_refs):
+        out_ref[...] = total[lax.rem(across + k, SIDE)]
+
+
+def plane_kernel(own_ref, back_ref, front_ref, far_ref, out_ref):
+    total = own_ref[...] + back_ref[...] + front_ref[...] + far_ref[...]
+    cols = out_ref.shape[1]
+    coded = [code(total[k * cols : (k + 1) * cols]) for k in range(2)]
+    for k in range(out_ref.shape[0]):
+        out_ref[k] = coded[k % 2]
+
+
+def rhs_kernel(place_ref, counts_ref, low_ref, high_ref, ridge_ref, parts_ref, *refs):
     mine, theirs = refs[:5], refs[5:10]
-    feats_ref, out_ref, scale_ref, coef_ref, held = refs[10:]
+    feats_ref, out_ref, rhs_ref, scale_ref, coef_ref = refs[10:]
     core = place_ref[2]
     deep = mine[0].shape[0] // SIDE
     rows = mine[0].shape[1]
-    width = deep // 2
-    cols = w_ref.shape[2]
     for outer in range(SIDE):
         for inner in range(SIDE):
             at = (outer * SIDE + inner) * deep
             feats_ref[at : at + deep, :rows] = piece(mine, outer, inner)
             feats_ref[at : at + deep, rows:] = piece(theirs, inner, outer)
-            origin = source(place_ref, ORDER[inner], ORDER[outer])
-            for k in range(2):
-                here = at + k * width
-                held[:cols, here : here + width] = w_ref[origin + k, core].astype(jnp.float32)
-                held[cols:, here : here + width] = w_ref[origin + k, 1 - core].astype(jnp.float32)
-    weights = held[...].astype(jnp.bfloat16)
-    first = lax.dot_general(
-        weights[:cols], feats_ref[:, :rows], NN, preferred_element_type=jnp.float32
-    )
-    second = lax.dot_general(
-        weights[cols:], feats_ref[:, rows:], NN, preferred_element_type=jnp.float32
-    )
-    send_all(jnp.concatenate([first, second], axis=1), out_ref)
 
     position = lax.broadcasted_iota(jnp.int32, (1, 2 * rows), 1)
     other = position >= rows
@@ -119,21 +181,21 @@
     coef_ref[2:3] = rho_new * rho
     coef_ref[3:4] = 2.0 * rho_new / radius
 
+    half = parts_ref.shape[0] // 2
+    for at, side in ((core, 0), (1 - core, 1)):
+        total = sum_coded(parts_ref, [2 * k + at for k in range(half)])
+        rhs_ref[:, side * rows : (side + 1) * rows] = total
+    ahead(rhs_ref[...] / coef_ref[0:1, 0:1], scale_ref, feats_ref, out_ref)
+
 
 def ahead(direction, scale_ref, feats_ref, out_ref):
     feats = feats_ref[...]
     send_all(times(times(direction * scale_ref[...], feats, NT), feats, NN), out_ref)
 
 
-def rhs_kernel(coef_ref, scale_ref, parts_ref, feats_ref, out_ref, rhs_ref):
-    rhs = jnp.sum(parts_ref[...], axis=0)
-    rhs_ref[...] = rhs
-    ahead(rhs / coef_ref[0:1, 0:1], scale_ref, feats_ref, out_ref)
-
-
 def step_kernel(coef_ref, scale_ref, parts_ref, feats_ref, rhs_ref, out_ref, dir_ref, res_ref):
     first = rhs_ref[...] / coef_ref[0:1, 0:1]
-    image = jnp.sum(parts_ref[...], axis=0) + coef_ref[1:2, 0:1] * first
+    image = sum_coded(parts_ref, range(parts_ref.shape[0])) + coef_ref[1:2, 0:1] * first
     residual = rhs_ref[...] - image
     direction = coef_ref[2:3, 0:1] * first + coef_ref[3:4, 0:1] * residual
     dir_ref[...] = direction
@@ -145,7 +207,7 @@
     place_ref, coef_ref, scale_ref, parts_ref, feats_ref, rhs_ref, dir_ref, res_ref, out_ref, held
 ):
     direction = dir_ref[...]
-    image = jnp.sum(parts_ref[...], axis=0) + coef_ref[1:2, 0:1] * direction
+    image = sum_coded(parts_ref, range(parts_ref.shape[0])) + coef_ref[1:2, 0:1] * direction
     residual = res_ref[...] - image
     merged = rhs_ref[...] / coef_ref[0:1, 0:1] + direction
     both = jnp.concatenate([merged, residual], axis=0) * scale_ref[...]
@@ -185,43 +247,61 @@
     place = jnp.stack([lax.axis_index("xh") * 2 + lax.axis_index("xl"), lax.axis_index("y"), core])
     place = place.astype(jnp.int32)
 
-    w_turned = jnp.stack(
-        [w.T.reshape(members, cols, width) for w in (w_first, w_second)], axis=1
-    )
     lead = core == 0
     mine = jnp.where(lead, x_first, x_second).T
     give = jnp.where(lead, x_second, x_first).T
-    got = swap(give)
+    keep_w, give_w = jnp.where(lead, w_first, w_second), jnp.where(lead, w_second, w_first)
+    got_all = swap(jnp.concatenate([give, give_w], axis=1))
+    got = got_all[:, :rows]
     block = jnp.where(
         lead, jnp.concatenate([mine, got], axis=0), jnp.concatenate([got, mine], axis=0)
     )
-    near = jnp.concatenate([block] + [along(block, k, True) for k in ORDER[1:]], axis=0)
-    near, w_turned = lax.optimization_barrier((near, w_turned))
-    back, front = along(near, 1, False), along(near, 3, False)
-    weights = lax.all_to_all(w_turned, MEMBERS, 0, 0, tiled=True)
-    back, front, weights = lax.optimization_barrier((back, front, weights))
+    ring = [along(block, k, True) for k in ORDER[1:]]
+
+    hand = shape((2, SIDE * 2 * cols, width), jnp.bfloat16)
+    dealt = call(
+        deal_kernel,
+        [hand] * SIDE,
+        [SMEM] + [VMEM] * 2,
+        [pltpu.VMEM((2, members // 2, 2 * cols, width), f32)],
+    )(place, keep_w, got_all)
+    dealt = [dealt[0]] + [along(d, k, True) for k, d in zip(ORDER[1:], dealt[1:])]
+    ring, dealt = lax.optimization_barrier((ring, dealt))
+    near = jnp.concatenate([block] + ring, axis=0)
+
+    shares = call(
+        line_kernel,
+        [shape((2 * cols, rows), f32)] * SIDE,
+        [SMEM] + [VMEM] * (1 + SIDE),
+        [
+            pltpu.VMEM((hand.shape[1], near.shape[0]), f32),
+            pltpu.VMEM((SIDE, 2 * cols, rows), f32),
+        ],
+    )(place, near, *dealt)
+    shares, ahead_near = lax.optimization_barrier((shares, near))
+    shares = [shares[0]] + [along(d, k, False) for k, d in zip(ORDER[1:], shares[1:])]
+    back, front = along(ahead_near, 1, False), along(ahead_near, 3, False)
+    parts = call(plane_kernel, shape((2 * depth, cols, rows + TILE), jnp.int16), [VMEM] * SIDE)(*shares)
     half = near.shape[0] // 2
     far_low, far_high = along(back[:half], 1, False), along(front[half:], 3, False)
+    parts = lax.all_to_all(parts, ("z", "core"), 0, 0, tiled=True)
     pieces = [near, back, front, far_low, far_high]
     swapped = [swap(p) for p in pieces]
 
-
     total = members * width
-    copies = shape((depth, cols, 2 * rows), f32)
+    copies = shape((depth, cols, 2 * rows + TILE), jnp.int16)
     state = shape((cols, 2 * rows), f32)
-    feats, parts, scale, coef = call(
-        start_kernel,
+    feats, parts, rhs, scale, coef = call(
+        rhs_kernel,
         (
             shape((total, 2 * rows), jnp.bfloat16),
             copies,
+            state,
             shape((1, 2 * rows), f32),
             shape((4, 128), f32),
         ),
         [SMEM] * 5 + [VMEM] * 11,
-        [pltpu.VMEM((2 * cols, total), f32)],
-    )(place, counts, eig_low, eig_high, damping, weights, *pieces, *swapped)
-    parts = sum_parts(parts)
-    parts, rhs = call(rhs_kernel, (copies, state), [VMEM] * 4)(coef, scale, parts, feats)
+    )(place, counts, eig_low, eig_high, damping, parts, *pieces, *swapped)
     parts = sum_parts(parts)
     parts, direction, residual = call(step_kernel, (copies, state, state), [VMEM] * 5)(
         coef, scale, parts, feats, rhs

time: 132 us -> 125 us (0.947)
  blocking collectives: 70.1 us -> 39.5 us
  starting transfers between devices: 20.2 us -> 40.1 us
  waiting for transfers between devices: 21.1 us -> 24.8 us
  local copies, waits for them, and re-layouts: 3.28 us -> 1.53 us
  Pallas kernels: 12.4 us -> 14.1 us
    all_to_all x3 -> x2, blocking collectives: 55.1 us -> 26.2 us  [sum_parts(): return lax.all_to_all(copies, 'z', 0, 0, tiled=True)]
    ppermute x6, starting transfers between devices: 6.33 us -> 17.7 us  [swap(): return lax.ppermute(value, 'core', [(0, 1), (1, 0)])]
    ppermute x7 -> x13, starting transfers between devices: 6.08 us -> 13.8 us  [along(): return lax.ppermute(value, MEMBERS, ring_pairs(shift, first))]
    ppermute x7 -> x13, waiting for transfers between devices: 10.1 us -> 14.6 us  [along(): return lax.ppermute(value, MEMBERS, ring_pairs(shift, first))]
    transpose x2 -> x0, local copies, waits for them, and re-layouts: 1.76 us -> none  [body(): w.T.reshape(members, cols, width)]
    all_to_all x1, blocking collectives: 15 us -> 13.2 us  [body(): out = lax.all_to_all(out, MEMBERS, 0, 0, tiled=True)]
    pallas_call x2 -> x4, Pallas kernels: 6.39 us -> 7.85 us  [the longest x1 5.5 us: body(): call(rhs_kernel, (shape((total, 2 * rows), jnp.bfloat16), copies, state,...]
  transfers between devices with their start and end apart: 14 -> 20, of which waited for: 7 -> 6; matrix products, arithmetic and copies ran while one was open for 2% -> 0% of each run, Pallas kernels for 0% -> 1%
where the time goes in v3:
time: 125 us
  starting transfers between devices  40.1 us (32%)
  blocking collectives  39.5 us (32%)
  waiting for transfers between devices  24.8 us (20%)
  Pallas kernels  14.1 us (11%)
  between operations  2.72 us (2%)
  other arithmetic  1.96 us (2%)
  local copies, waits for them, and re-layouts  1.53 us (1%)
    all_to_all x2, blocking collectives, sum_parts(): return lax.all_to_all(copies, 'z', 0, 0, tiled=True)  26.2 us
    ppermute x6, starting transfers between devices, swap(): return lax.ppermute(value, 'core', [(0, 1), (1, 0)])  17.7 us
    ppermute x13, waiting for transfers between devices, along(): return lax.ppermute(value, MEMBERS, ring_pairs(shift, first))  14.6 us
    ppermute x13, starting transfers between devices, along(): return lax.ppermute(value, MEMBERS, ring_pairs(shift, first))  13.8 us
    all_to_all x1, blocking collectives, body(): out = lax.all_to_all(out, MEMBERS, 0, 0, tiled=True)  13.2 us
    all_to_all x1, waiting for transfers between devices, body(): parts = lax.all_to_all(parts, ('z', 'core'), 0, 0, tiled=True)  9.1 us
    all_to_all x1, starting transfers between devices, body(): parts = lax.all_to_all(parts, ('z', 'core'), 0, 0, tiled=True)  8.59 us
    pallas_call x1, Pallas kernels, body(): call(rhs_kernel, (shape((total, 2 * rows), jnp.bfloat16), copies, state,...  5.5 us
  transfers between devices with their start and end apart: 20, of which 6 were waited for; matrix products, arithmetic and copies ran while one was open for 0% of the time, Pallas kernels for 1%

profile of v3, /device:TPU:1, one launch (start us, length us, event | category | flops | bytes accessed | tf_op | source)
XLA Modules:
  0.0 124.6 jit_solution(1199690974418005318)
XLA Ops:
  0.6 0.8 broadcast_select_fusion
  1.4 1.0 select_bitcast_fusion.1
  2.4 3.3 %collective-permute-start = (bf16[72,1024]{1,0:T(8,128)(2,1)S(1)}, bf16[72,1024]{1,0:T(8,128)(2,1)S(1)}, u32[]{:S(2)}, u32[]{:S(2)}) collective-permute-start(bf16[72,1024]{1,0:T(8,128)(2,1)S(1)} %pad_maximum_fusion.1), channel_id=1, source_target_pairs={{0,1},{1,0},{2,3},{3,2},{4,5},{5,4},{6,7},{7,6},{8,9},{9,8},{10,11... | collective-permute-start | bytes 442376 | tf_op jit(solution)/shard_map/ppermute | solution.py:45
  5.8 1.0 collective-permute-done.got_ref
  6.8 1.1 collective-permute-start.3
  7.9 0.9 collective-permute-start.2
  10.5 2.4 %collective-permute-start.5 = (bf16[2,64,72]{2,1,0:T(8,128)(2,1)S(1)}, bf16[2,64,72]{2,1,0:T(8,128)(2,1)S(1)}, u32[]{:S(2)}, u32[]{:S(2)}) collective-permute-start(bf16[2,64,72]{2,1,0:T(8,128)(2,1)S(1)} %get-tuple-element.32), channel_id=1, source_target_pairs={{0,12},{1,131},{4,0},{5,135},{8,4},{9,139},{12,8},{13,143},{128,14... | collective-permute-start | bytes 55304 | tf_op jit(solution)/shard_map/ppermute | solution.py:41
  12.9 3.3 %collective-permute-done.4.refs_1_ = bf16[2,64,72]{2,1,0:T(8,128)(2,1)S(1)} collective-permute-done((bf16[2,64,72]{2,1,0:T(8,128)(2,1)S(1)}, bf16[2,64,72]{2,1,0:T(8,128)(2,1)S(1)}, u32[]{:S(2)}, u32[]{:S(2)}) %collective-permute-start.4) | collective-permute-done | bytes 18464 | tf_op jit(solution)/shard_map/ppermute | solution.py:41
  16.2 1.0 collective-permute-start.6
  17.2 3.3 %collective-permute-done.6.refs_3_ = bf16[2,64,72]{2,1,0:T(8,128)(2,1)S(1)} collective-permute-done((bf16[2,64,72]{2,1,0:T(8,128)(2,1)S(1)}, bf16[2,64,72]{2,1,0:T(8,128)(2,1)S(1)}, u32[]{:S(2)}, u32[]{:S(2)}) %collective-permute-start.6) | collective-permute-done | bytes 18464 | tf_op jit(solution)/shard_map/ppermute | solution.py:41
  20.6 0.9 shard_map.96
  21.5 2.0 %collective-permute-start.11 = (bf16[576,768]{1,0:T(8,128)(2,1)S(1)}, bf16[576,768]{1,0:T(8,128)(2,1)S(1)}, u32[]{:S(2)}, u32[]{:S(2)}) collective-permute-start(bf16[576,768]{1,0:T(8,128)(2,1)S(1)} %pad_maximum_fusion.near_ref.refs_0_), channel_id=1, source_target_pairs={{0,130},{1,13},{4,134},{5,1},{8,138},{9,5},{12,142},{13,9},{128,0}... | collective-permute-start | bytes 2654216 | tf_op jit(solution)/shard_map/ppermute | solution.py:41
  23.5 2.7 %collective-permute-start.8 = (f32[16,768]{1,0:T(8,128)S(1)}, f32[16,768]{1,0:T(8,128)S(1)}, u32[]{:S(2)}, u32[]{:S(2)}) collective-permute-start(f32[16,768]{1,0:T(8,128)S(1)} %get-tuple-element.47), channel_id=1, source_target_pairs={{0,130},{1,13},{4,134},{5,1},{8,138},{9,5},{12,142},{13,9},{128,0}... | collective-permute-start | bytes 147464 | tf_op jit(solution)/shard_map/ppermute | solution.py:41
  26.2 1.2 collective-permute-start.9
  27.3 6.4 %collective-permute-done.11.refs_2_ = bf16[576,768]{1,0:T(8,128)(2,1)S(1)} collective-permute-done((bf16[576,768]{1,0:T(8,128)(2,1)S(1)}, bf16[576,768]{1,0:T(8,128)(2,1)S(1)}, u32[]{:S(2)}, u32[]{:S(2)}) %collective-permute-start.11) | collective-permute-done | bytes 884768 | tf_op jit(solution)/shard_map/ppermute | solution.py:41
  33.7 3.9 %collective-permute-start.14 = (bf16[576,768]{1,0:T(8,128)(2,1)S(1)}, bf16[576,768]{1,0:T(8,128)(2,1)}, u32[]{:S(2)}, u32[]{:S(2)}) collective-permute-start(bf16[576,768]{1,0:T(8,128)(2,1)S(1)} %pad_maximum_fusion.near_ref.refs_0_), channel_id=1, source_target_pairs={{0,1},{1,0},{2,3},{3,2},{4,5},{5,4},{6,7},{7,6},{8,9},{9,8},{10,11... | collective-permute-start | bytes 2654216 | tf_op jit(solution)/shard_map/ppermute | solution.py:45
  38.0 1.3 %collective-permute-start.12 = (bf16[288,768]{1,0:T(8,128)(2,1)S(1)}, bf16[288,768]{1,0:T(8,128)(2,1)}, u32[]{:S(2)}, u32[]{:S(2)}) collective-permute-start(bf16[288,768]{1,0:T(8,128)(2,1)S(1)} %slice.21), channel_id=1, source_target_pairs={{0,128},{1,5},{4,132},{5,9},{8,136},{9,13},{12,140},{13,1},{128,2}... | collective-permute-start | bytes 1327112 | tf_op jit(solution)/shard_map/ppermute | solution.py:41
  39.4 4.1 %collective-permute-start.16 = (bf16[576,768]{1,0:T(8,128)(2,1)S(1)}, bf16[576,768]{1,0:T(8,128)(2,1)}, u32[]{:S(2)}, u32[]{:S(2)}) collective-permute-start(bf16[576,768]{1,0:T(8,128)(2,1)S(1)} %collective-permute-done.11.refs_2_), channel_id=1, source_target_pairs={{0,1},{1,0},{2,3},{3,2},{4,5},{5,4},{6,7},{7,6},{8,9},{9,8},{10,11... | collective-permute-start | bytes 2654216 | tf_op jit(solution)/shard_map/ppermute | solution.py:45
  43.5 1.7 %collective-permute-done.13.refs_4_ = bf16[288,768]{1,0:T(8,128)(2,1)S(1)} collective-permute-done((bf16[288,768]{1,0:T(8,128)(2,1)S(1)}, bf16[288,768]{1,0:T(8,128)(2,1)S(1)}, u32[]{:S(2)}, u32[]{:S(2)}) %collective-permute-start.13) | collective-permute-done | bytes 442400 | tf_op jit(solution)/shard_map/ppermute | solution.py:41
  45.2 4.4 %collective-permute-start.18 = (bf16[288,768]{1,0:T(8,128)(2,1)S(1)}, bf16[288,768]{1,0:T(8,128)(2,1)}, u32[]{:S(2)}, u32[]{:S(2)}) collective-permute-start(bf16[288,768]{1,0:T(8,128)(2,1)S(1)} %collective-permute-done.13.refs_4_), channel_id=1, source_target_pairs={{0,1},{1,0},{2,3},{3,2},{4,5},{5,4},{6,7},{7,6},{8,9},{9,8},{10,11... | collective-permute-start | bytes 1327112 | tf_op jit(solution)/shard_map/ppermute | solution.py:45
  49.6 1.8 %collective-permute-start.17 = (bf16[288,768]{1,0:T(8,128)(2,1)}, bf16[288,768]{1,0:T(8,128)(2,1)}, u32[]{:S(2)}, u32[]{:S(2)}) collective-permute-start(bf16[288,768]{1,0:T(8,128)(2,1)} %collective-permute-done.12.refs_3_), channel_id=1, source_target_pairs={{0,1},{1,0},{2,3},{3,2},{4,5},{5,4},{6,7},{7,6},{8,9},{9,8},{10,11... | collective-permute-start | bytes 1327112 | tf_op jit(solution)/shard_map/ppermute | solution.py:45
  51.4 0.8 shard_map.97
  52.2 8.6 %all-to-all-start = ((s16[16,8,896]{2,1,0:T(8,128)(2,1)}), s16[16,8,896]{2,1,0:T(8,128)(2,1)S(1)}, u32[]{:S(2)}, u32[]{:S(2)}) async-start(s16[16,8,896]{2,1,0:T(8,128)(2,1)} %shard_map.97), calls=%async_computation | async-start | bytes 458752 | tf_op jit(solution)/shard_map/all_to_all | solution.py:287
  62.8 9.1 %all-to-all-done.parts_ref = s16[16,8,896]{2,1,0:T(8,128)(2,1)S(1)} async-done(((s16[16,8,896]{2,1,0:T(8,128)(2,1)}), s16[16,8,896]{2,1,0:T(8,128)(2,1)S(1)}, u32[]{:S(2)}, u32[]{:S(2)}) %all-to-all-start) | async-done | bytes 229408 | tf_op jit(solution)/shard_map/all_to_all | solution.py:287
  71.9 5.5 %shard_map.98 = (bf16[2304,1536]{1,0:T(8,128)(2,1)S(1)}, s16[8,8,1664]{2,1,0:T(8,128)(2,1)S(1)}, f32[8,1536]{1,0:T(8,128)S(1)}, f32[1,1536]{1,0:T(1,128)S(1)}, f32[4,128]{1,0:T(4,128)S(1)}) custom-call(s32[3]{0:T(128)S(1)} %pad_add_fusion.place_ref, s32[2]{0:T(128)S(1)} %copy-done, f32[1]{0:T(128)S(6)} %copy.13.low_ref, f32[1]{0:T(128)S(6)} %copy.14.high_ref, ...), custom_call_target="tpu_custom_call" | custom-call | tf_op jit(solution)/shard_map/pallas_call | solution.py:294
  77.4 13.7 %all_to_all.20.parts_ref = s16[8,8,1664]{2,1,0:T(8,128)(2,1)S(1)} all-to-all(s16[8,8,1664]{2,1,0:T(8,128)(2,1)S(1)} %get-tuple-element.52), channel_id=1, replica_groups=mesh['xl'=2,'z'=8,'y'=4,'xh'=2,'core'=2] {'z'}, dimensions={0} | all-to-all | bytes 425984 | tf_op jit(solution)/shard_map/all_to_all | solution.py:236
  91.1 3.4 %shard_map.99 = (s16[8,8,1664]{2,1,0:T(8,128)(2,1)S(1)}, f32[8,1536]{1,0:T(8,128)S(1)}, f32[8,1536]{1,0:T(8,128)S(1)}) custom-call(f32[4,128]{1,0:T(4,128)S(1)} %get-tuple-element.50.coef_ref, f32[1,1536]{1,0:T(1,128)S(1)} %get-tuple-element.51.scale_ref, s16[8,8,1664]{2,1,0:T(8,128)(2,1)S(1)} %all_to_all.20.parts_ref, ...), custom_call_target="tpu_custom_call" | custom-call | tf_op jit(solution)/shard_map/pallas_call | solution.py:306
  94.5 12.6 %all_to_all.21.parts_ref = s16[8,8,1664]{2,1,0:T(8,128)(2,1)S(1)} all-to-all(s16[8,8,1664]{2,1,0:T(8,128)(2,1)S(1)} %get-tuple-element.55), channel_id=1, replica_groups=mesh['xl'=2,'z'=8,'y'=4,'xh'=2,'core'=2] {'z'}, dimensions={0} | all-to-all | bytes 425984 | tf_op jit(solution)/shard_map/all_to_all | solution.py:236
  107.1 2.8 %shard_map.100 = f32[32,16,72]{2,1,0:T(8,128)S(1)} custom-call(s32[3]{0:T(128)S(1)} %pad_add_fusion.place_ref, f32[4,128]{1,0:T(4,128)S(1)} %get-tuple-element.50.coef_ref, f32[1,1536]{1,0:T(1,128)S(1)} %get-tuple-element.51.scale_ref, s16[8,8,1664]{2,1,0:T(8,128)(2,1)S(1)} %all_to_all.21.parts_ref, bf16[2304,1536]{1,0:T(8,128)(2,1)S(1)} %get-tuple-element.53.feats_ref, ...), custom_call_target="tpu_custom_call" | custom-call | tf_op jit(solution)/shard_map/pallas_call | solution.py:310
  109.9 13.2 %all_to_all.22 = f32[32,16,72]{2,1,0:T(8,128)S(1)} all-to-all(f32[32,16,72]{2,1,0:T(8,128)S(1)} %shard_map.100), channel_id=1, replica_groups=mesh['xl'=2,'z'=8,'y'=4,'xh'=2,'core'=2] {'xl','y','xh','core'}, dimensions={0} | all-to-all | bytes 294912 | tf_op jit(solution)/shard_map/all_to_all | solution.py:316
  123.2 0.7 copy.11
  123.9 0.7 copy.10
  (31 shorter events, 2.4 us)
Async XLA Ops:
  2.4 4.3 %collective-permute-start = (bf16[72,1024]{1,0:T(8,128)(2,1)S(1)}, bf16[72,1024]{1,0:T(8,128)(2,1)S(1)}, u32[]{:S(2)}, u32[]{:S(2)}) collective-permute-start(bf16[72,1024]{1,0:T(8,128)(2,1)S(1)} %pad_maximum_fusion.1), channel_id=1, source_target_pairs={{0,1},{1,0},{2,3},{3,2},{4,5},{5,4},{6,7},{7,6},{8,9},{9,8},{10,11... | collective-permute-start | bytes 442376 | tf_op jit(solution)/shard_map/ppermute | solution.py:45
  6.8 13.7 %collective-permute-start.3 = (bf16[144,768]{1,0:T(8,128)(2,1)S(1)}, bf16[144,768]{1,0:T(8,128)(2,1)S(1)}, u32[]{:S(2)}, u32[]{:S(2)}) collective-permute-start(bf16[144,768]{1,0:T(8,128)(2,1)S(1)} %maximum_select_fusion), channel_id=1, source_target_pairs={{0,8},{1,3},{4,12},{5,7},{8,0},{9,11},{12,4},{13,15},{128,136},{12... | collective-permute-start | bytes 663560 | tf_op jit(solution)/shard_map/ppermute | solution.py:41
  7.9 12.6 %collective-permute-start.2 = (bf16[144,768]{1,0:T(8,128)(2,1)S(1)}, bf16[144,768]{1,0:T(8,128)(2,1)S(1)}, u32[]{:S(2)}, u32[]{:S(2)}) collective-permute-start(bf16[144,768]{1,0:T(8,128)(2,1)S(1)} %maximum_select_fusion), channel_id=1, source_target_pairs={{0,12},{1,131},{4,0},{5,135},{8,4},{9,139},{12,8},{13,143},{128,14... | collective-permute-start | bytes 663560 | tf_op jit(solution)/shard_map/ppermute | solution.py:41
  8.8 11.7 %collective-permute-start.1 = (bf16[144,768]{1,0:T(8,128)(2,1)S(1)}, bf16[144,768]{1,0:T(8,128)(2,1)S(1)}, u32[]{:S(2)}, u32[]{:S(2)}) collective-permute-start(bf16[144,768]{1,0:T(8,128)(2,1)S(1)} %maximum_select_fusion), channel_id=1, source_target_pairs={{0,4},{1,129},{4,8},{5,133},{8,12},{9,137},{12,0},{13,141},{128,13... | collective-permute-start | bytes 663560 | tf_op jit(solution)/shard_map/ppermute | solution.py:41
  10.1 6.1 %collective-permute-start.4 = (bf16[2,64,72]{2,1,0:T(8,128)(2,1)S(1)}, bf16[2,64,72]{2,1,0:T(8,128)(2,1)S(1)}, u32[]{:S(2)}, u32[]{:S(2)}) collective-permute-start(bf16[2,64,72]{2,1,0:T(8,128)(2,1)S(1)} %get-tuple-element.31), channel_id=1, source_target_pairs={{0,4},{1,129},{4,8},{5,133},{8,12},{9,137},{12,0},{13,141},{128,13... | collective-permute-start | bytes 55304 | tf_op jit(solution)/shard_map/ppermute | solution.py:41
  10.5 6.7 %collective-permute-start.5 = (bf16[2,64,72]{2,1,0:T(8,128)(2,1)S(1)}, bf16[2,64,72]{2,1,0:T(8,128)(2,1)S(1)}, u32[]{:S(2)}, u32[]{:S(2)}) collective-permute-start(bf16[2,64,72]{2,1,0:T(8,128)(2,1)S(1)} %get-tuple-element.32), channel_id=1, source_target_pairs={{0,12},{1,131},{4,0},{5,135},{8,4},{9,139},{12,8},{13,143},{128,14... | collective-permute-start | bytes 55304 | tf_op jit(solution)/shard_map/ppermute | solution.py:41
  16.2 4.3 %collective-permute-start.6 = (bf16[2,64,72]{2,1,0:T(8,128)(2,1)S(1)}, bf16[2,64,72]{2,1,0:T(8,128)(2,1)S(1)}, u32[]{:S(2)}, u32[]{:S(2)}) collective-permute-start(bf16[2,64,72]{2,1,0:T(8,128)(2,1)S(1)} %get-tuple-element.33), channel_id=1, source_target_pairs={{0,8},{1,3},{4,12},{5,7},{8,0},{9,11},{12,4},{13,15},{128,136},{12... | collective-permute-start | bytes 55304 | tf_op jit(solution)/shard_map/ppermute | solution.py:41
  20.6 51.4 %copy-start = (s32[2]{0:T(128)S(1)}, s32[2]{0:T(128)}, u32[]{:S(2)}) copy-start(s32[2]{0:T(128)} %counts_ref.1) | copy-start | bytes 28
  21.5 12.3 %collective-permute-start.11 = (bf16[576,768]{1,0:T(8,128)(2,1)S(1)}, bf16[576,768]{1,0:T(8,128)(2,1)S(1)}, u32[]{:S(2)}, u32[]{:S(2)}) collective-permute-start(bf16[576,768]{1,0:T(8,128)(2,1)S(1)} %pad_maximum_fusion.near_ref.refs_0_), channel_id=1, source_target_pairs={{0,130},{1,13},{4,134},{5,1},{8,138},{9,5},{12,142},{13,9},{128,0}... | collective-permute-start | bytes 2654216 | tf_op jit(solution)/shard_map/ppermute | solution.py:41
  23.5 14.2 %collective-permute-start.10 = (bf16[576,768]{1,0:T(8,128)(2,1)S(1)}, bf16[576,768]{1,0:T(8,128)(2,1)S(1)}, u32[]{:S(2)}, u32[]{:S(2)}) collective-permute-start(bf16[576,768]{1,0:T(8,128)(2,1)S(1)} %pad_maximum_fusion.near_ref.refs_0_), channel_id=1, source_target_pairs={{0,128},{1,5},{4,132},{5,9},{8,136},{9,13},{12,140},{13,1},{128,2}... | collective-permute-start | bytes 2654216 | tf_op jit(solution)/shard_map/ppermute | solution.py:41
  23.5 14.5 %collective-permute-start.7 = (f32[16,768]{1,0:T(8,128)S(1)}, f32[16,768]{1,0:T(8,128)S(1)}, u32[]{:S(2)}, u32[]{:S(2)}) collective-permute-start(f32[16,768]{1,0:T(8,128)S(1)} %get-tuple-element.46), channel_id=1, source_target_pairs={{0,128},{1,5},{4,132},{5,9},{8,136},{9,13},{12,140},{13,1},{128,2}... | collective-permute-start | bytes 147464 | tf_op jit(solution)/shard_map/ppermute | solution.py:41
  23.5 15.9 %collective-permute-start.8 = (f32[16,768]{1,0:T(8,128)S(1)}, f32[16,768]{1,0:T(8,128)S(1)}, u32[]{:S(2)}, u32[]{:S(2)}) collective-permute-start(f32[16,768]{1,0:T(8,128)S(1)} %get-tuple-element.47), channel_id=1, source_target_pairs={{0,130},{1,13},{4,134},{5,1},{8,138},{9,5},{12,142},{13,9},{128,0}... | collective-permute-start | bytes 147464 | tf_op jit(solution)/shard_map/ppermute | solution.py:41
  26.2 17.3 %collective-permute-start.9 = (f32[16,768]{1,0:T(8,128)S(1)}, f32[16,768]{1,0:T(8,128)S(1)}, u32[]{:S(2)}, u32[]{:S(2)}) collective-permute-start(f32[16,768]{1,0:T(8,128)S(1)} %get-tuple-element.48), channel_id=1, source_target_pairs={{0,2},{1,9},{4,6},{5,13},{8,10},{9,1},{12,14},{13,5},{128,130},{12... | collective-permute-start | bytes 147464 | tf_op jit(solution)/shard_map/ppermute | solution.py:41
  33.7 38.2 %collective-permute-start.14 = (bf16[576,768]{1,0:T(8,128)(2,1)S(1)}, bf16[576,768]{1,0:T(8,128)(2,1)}, u32[]{:S(2)}, u32[]{:S(2)}) collective-permute-start(bf16[576,768]{1,0:T(8,128)(2,1)S(1)} %pad_maximum_fusion.near_ref.refs_0_), channel_id=1, source_target_pairs={{0,1},{1,0},{2,3},{3,2},{4,5},{5,4},{6,7},{7,6},{8,9},{9,8},{10,11... | collective-permute-start | bytes 2654216 | tf_op jit(solution)/shard_map/ppermute | solution.py:45
  37.7 7.5 %collective-permute-start.13 = (bf16[288,768]{1,0:T(8,128)(2,1)S(1)}, bf16[288,768]{1,0:T(8,128)(2,1)S(1)}, u32[]{:S(2)}, u32[]{:S(2)}) collective-permute-start(bf16[288,768]{1,0:T(8,128)(2,1)S(1)} %slice.22), channel_id=1, source_target_pairs={{0,130},{1,13},{4,134},{5,1},{8,138},{9,5},{12,142},{13,9},{128,0}... | collective-permute-start | bytes 1327112 | tf_op jit(solution)/shard_map/ppermute | solution.py:41
  38.0 11.6 %collective-permute-start.12 = (bf16[288,768]{1,0:T(8,128)(2,1)S(1)}, bf16[288,768]{1,0:T(8,128)(2,1)}, u32[]{:S(2)}, u32[]{:S(2)}) collective-permute-start(bf16[288,768]{1,0:T(8,128)(2,1)S(1)} %slice.21), channel_id=1, source_target_pairs={{0,128},{1,5},{4,132},{5,9},{8,136},{9,13},{12,140},{13,1},{128,2}... | collective-permute-start | bytes 1327112 | tf_op jit(solution)/shard_map/ppermute | solution.py:41
  39.4 32.5 %collective-permute-start.16 = (bf16[576,768]{1,0:T(8,128)(2,1)S(1)}, bf16[576,768]{1,0:T(8,128)(2,1)}, u32[]{:S(2)}, u32[]{:S(2)}) collective-permute-start(bf16[576,768]{1,0:T(8,128)(2,1)S(1)} %collective-permute-done.11.refs_2_), channel_id=1, source_target_pairs={{0,1},{1,0},{2,3},{3,2},{4,5},{5,4},{6,7},{7,6},{8,9},{9,8},{10,11... | collective-permute-start | bytes 2654216 | tf_op jit(solution)/shard_map/ppermute | solution.py:45
  43.5 28.5 %collective-permute-start.15 = (bf16[576,768]{1,0:T(8,128)(2,1)S(1)}, bf16[576,768]{1,0:T(8,128)(2,1)}, u32[]{:S(2)}, u32[]{:S(2)}) collective-permute-start(bf16[576,768]{1,0:T(8,128)(2,1)S(1)} %collective-permute-done.10.refs_1_), channel_id=1, source_target_pairs={{0,1},{1,0},{2,3},{3,2},{4,5},{5,4},{6,7},{7,6},{8,9},{9,8},{10,11... | collective-permute-start | bytes 2654216 | tf_op jit(solution)/shard_map/ppermute | solution.py:45
  45.2 26.7 %collective-permute-start.18 = (bf16[288,768]{1,0:T(8,128)(2,1)S(1)}, bf16[288,768]{1,0:T(8,128)(2,1)}, u32[]{:S(2)}, u32[]{:S(2)}) collective-permute-start(bf16[288,768]{1,0:T(8,128)(2,1)S(1)} %collective-permute-done.13.refs_4_), channel_id=1, source_target_pairs={{0,1},{1,0},{2,3},{3,2},{4,5},{5,4},{6,7},{7,6},{8,9},{9,8},{10,11... | collective-permute-start | bytes 1327112 | tf_op jit(solution)/shard_map/ppermute | solution.py:45
  49.6 22.3 %collective-permute-start.17 = (bf16[288,768]{1,0:T(8,128)(2,1)}, bf16[288,768]{1,0:T(8,128)(2,1)}, u32[]{:S(2)}, u32[]{:S(2)}) collective-permute-start(bf16[288,768]{1,0:T(8,128)(2,1)} %collective-permute-done.12.refs_3_), channel_id=1, source_target_pairs={{0,1},{1,0},{2,3},{3,2},{4,5},{5,4},{6,7},{7,6},{8,9},{9,8},{10,11... | collective-permute-start | bytes 1327112 | tf_op jit(solution)/shard_map/ppermute | solution.py:45
  52.2 19.6 %all-to-all-start = ((s16[16,8,896]{2,1,0:T(8,128)(2,1)}), s16[16,8,896]{2,1,0:T(8,128)(2,1)S(1)}, u32[]{:S(2)}, u32[]{:S(2)}) async-start(s16[16,8,896]{2,1,0:T(8,128)(2,1)} %shard_map.97), calls=%async_computation | async-start | bytes 458752 | tf_op jit(solution)/shard_map/all_to_all | solution.py:287

commit v4 on v3

--- a/solution.py
+++ b/solution.py
@@ -24,21 +24,34 @@
     return (((x % 2) * SIDE + y) * 2 + x // 2) * 2 + core
 
 
-def ring_pairs(shift, first):
+def ring_pairs(shift):
     pairs = []
     for x in range(SIDE):
         for y in range(SIDE):
             for core in range(2):
-                if (core == 0) == first:
+                if core == 0:
+                    to = member((x + shift) % SIDE, y, core)
+                else:
                     to = member(x, (y + shift) % SIDE, core)
-                else:
-                    to = member((x + shift) % SIDE, y, core)
                 pairs.append((member(x, y, core), to))
     return pairs
 
 
-def along(value, shift, first):
-    return lax.ppermute(value, MEMBERS, ring_pairs(shift, first))
+def lines(first):
+    groups = []
+    for core in range(2):
+        for other in range(SIDE):
+            spots = [(k, other) if (core == 0) != first else (other, k) for k in range(SIDE)]
+            groups.append([member(x, y, core) for x, y in spots])
+    return groups
+
+
+def exchange(blocks, first):
+    return lax.all_to_all(blocks, MEMBERS, 0, 0, axis_index_groups=lines(first), tiled=True)
+
+
+def along(value, shift):
+    return lax.ppermute(value, MEMBERS, ring_pairs(shift))
 
 
 def swap(value):
@@ -97,55 +110,53 @@
     return ((lax.rem(at_x, 2) * SIDE + at_y) * 2 + lax.div(at_x, 2)) * 2
 
 
-def piece(refs, outer, inner):
-    deep = refs[0].shape[0] // SIDE
-    if outer < 3:
-        return refs[outer][inner * deep : (inner + 1) * deep]
-    ref = refs[3 + inner // 2]
-    return ref[(inner % 2) * deep : (inner % 2 + 1) * deep]
-
-
-def deal_kernel(place_ref, keep_ref, got_ref, *refs):
-    out_refs, (held,) = refs[:SIDE], refs[SIDE:]
+def line_place(place_ref):
+    x, y, lead = place_ref[0], place_ref[1], place_ref[2] == 0
+    return jnp.where(lead, y, x), jnp.where(lead, x, y)
+
+
+def pack_kernel(place_ref, block_ref, keep_ref, got_ref, out_ref, held, strip):
     lead = place_ref[2] == 0
+    deep = block_ref.shape[0]
     keep = keep_ref[...].astype(jnp.float32)
     got = got_ref[:, got_ref.shape[1] - keep.shape[1] :].astype(jnp.float32)
-    chips, each = held.shape[1:3]
+    chips, each, width = held.shape[1:]
     for k, rows in enumerate((jnp.where(lead, keep, got), jnp.where(lead, got, keep))):
         turned = rows.T
         for chip in range(chips):
             held[k, chip] = turned[chip * each : (chip + 1) * each]
-    line = jnp.where(lead, place_ref[1], place_ref[0])
-    for k, out_ref in zip(ORDER, out_refs):
-        at = lax.rem(line + k, SIDE)
+    strip[...] = jnp.zeros_like(strip)
+    for at in range(SIDE):
+        out_ref[at, :deep] = block_ref[...]
         for across in range(SIDE):
             x, y = jnp.where(lead, across, at), jnp.where(lead, at, across)
             chip = (lax.rem(x, 2) * SIDE + y) * 2 + lax.div(x, 2)
             for core in range(2):
-                rows = slice(across * each, (across + 1) * each)
-                out_ref[core, rows] = held[core, chip].astype(out_ref.dtype)
-
-
-def line_kernel(place_ref, near_ref, *refs):
-    w_refs, out_refs, (held, total) = refs[:SIDE], refs[SIDE : 2 * SIDE], refs[2 * SIDE :]
-    width = w_refs[0].shape[2]
-    for j, w_ref in enumerate(w_refs):
-        for k in range(2):
-            at = (2 * j + k) * width
-            held[:, at : at + width] = w_ref[k].astype(jnp.float32)
+                here = (2 * across + core) * width
+                strip[:, here : here + width] = held[core, chip]
+        out_ref[at, deep:] = strip[...].astype(out_ref.dtype)
+
+
+def line_kernel(packed_ref, near_ref, out_ref, held):
+    places, deep, rows = near_ref.shape
+    each = out_ref.shape[1]
+    for at in range(places):
+        strip = packed_ref[at, deep:].astype(jnp.float32)
+        for across in range(SIDE):
+            part = strip[:, across * deep : (across + 1) * deep]
+            held[across * each : (across + 1) * each, at * deep : (at + 1) * deep] = part
     out = lax.dot_general(
-        held[...].astype(jnp.bfloat16), near_ref[...], NN, preferred_element_type=jnp.float32
-    )
-    each = out.shape[0] // SIDE
-    for k in range(SIDE):
-        total[k] = out[k * each : (k + 1) * each]
-    across = jnp.where(place_ref[2] == 0, place_ref[0], place_ref[1])
-    for k, out_ref in zip(ORDER, out_refs):
-        out_ref[...] = total[lax.rem(across + k, SIDE)]
-
-
-def plane_kernel(own_ref, back_ref, front_ref, far_ref, out_ref):
-    total = own_ref[...] + back_ref[...] + front_ref[...] + far_ref[...]
+        held[...].astype(jnp.bfloat16),
+        near_ref[...].reshape(places * deep, rows),
+        NN,
+        preferred_element_type=jnp.float32,
+    )
+    for across in range(SIDE):
+        out_ref[across] = out[across * each : (across + 1) * each]
+
+
+def plane_kernel(shares_ref, out_ref):
+    total = jnp.sum(shares_ref[...], axis=0)
     cols = out_ref.shape[1]
     coded = [code(total[k * cols : (k + 1) * cols]) for k in range(2)]
     for k in range(out_ref.shape[0]):
@@ -153,16 +164,18 @@
 
 
 def rhs_kernel(place_ref, counts_ref, low_ref, high_ref, ridge_ref, parts_ref, *refs):
-    mine, theirs = refs[:5], refs[5:10]
-    feats_ref, out_ref, rhs_ref, scale_ref, coef_ref = refs[10:]
+    mine, theirs = refs[:SIDE], refs[SIDE : 2 * SIDE]
+    feats_ref, out_ref, rhs_ref, scale_ref, coef_ref = refs[2 * SIDE :]
     core = place_ref[2]
-    deep = mine[0].shape[0] // SIDE
-    rows = mine[0].shape[1]
+    deep, rows = mine[0].shape[1:]
+    line, across = line_place(place_ref)
     for outer in range(SIDE):
+        there = lax.rem(across + SIDE - ORDER[outer], SIDE)
         for inner in range(SIDE):
+            here = lax.rem(line + SIDE - ORDER[inner], SIDE)
             at = (outer * SIDE + inner) * deep
-            feats_ref[at : at + deep, :rows] = piece(mine, outer, inner)
-            feats_ref[at : at + deep, rows:] = piece(theirs, inner, outer)
+            feats_ref[at : at + deep, :rows] = mine[outer][here]
+            feats_ref[at : at + deep, rows:] = theirs[inner][there]
 
     position = lax.broadcasted_iota(jnp.int32, (1, 2 * rows), 1)
     other = position >= rows
@@ -256,36 +269,28 @@
     block = jnp.where(
         lead, jnp.concatenate([mine, got], axis=0), jnp.concatenate([got, mine], axis=0)
     )
-    ring = [along(block, k, True) for k in ORDER[1:]]
-
-    hand = shape((2, SIDE * 2 * cols, width), jnp.bfloat16)
-    dealt = call(
-        deal_kernel,
-        [hand] * SIDE,
-        [SMEM] + [VMEM] * 2,
-        [pltpu.VMEM((2, members // 2, 2 * cols, width), f32)],
-    )(place, keep_w, got_all)
-    dealt = [dealt[0]] + [along(d, k, True) for k, d in zip(ORDER[1:], dealt[1:])]
-    ring, dealt = lax.optimization_barrier((ring, dealt))
-    near = jnp.concatenate([block] + ring, axis=0)
-
+    packed = call(
+        pack_kernel,
+        shape((SIDE, block.shape[0] + 2 * cols, rows), jnp.bfloat16),
+        [SMEM] + [VMEM] * 3,
+        [pltpu.VMEM((2, members // 2, 2 * cols, width), f32), pltpu.VMEM((2 * cols, rows), f32)],
+    )(place, block, keep_w, got_all)
+    packed = exchange(packed, True)
+    near = packed[:, : block.shape[0]]
+    back, front = along(near, 1), along(near, 3)
     shares = call(
         line_kernel,
-        [shape((2 * cols, rows), f32)] * SIDE,
-        [SMEM] + [VMEM] * (1 + SIDE),
-        [
-            pltpu.VMEM((hand.shape[1], near.shape[0]), f32),
-            pltpu.VMEM((SIDE, 2 * cols, rows), f32),
-        ],
-    )(place, near, *dealt)
-    shares, ahead_near = lax.optimization_barrier((shares, near))
-    shares = [shares[0]] + [along(d, k, False) for k, d in zip(ORDER[1:], shares[1:])]
-    back, front = along(ahead_near, 1, False), along(ahead_near, 3, False)
-    parts = call(plane_kernel, shape((2 * depth, cols, rows + TILE), jnp.int16), [VMEM] * SIDE)(*shares)
-    half = near.shape[0] // 2
-    far_low, far_high = along(back[:half], 1, False), along(front[half:], 3, False)
+        shape((SIDE, 2 * cols, rows), f32),
+        [VMEM] * 2,
+        [pltpu.VMEM((SIDE * 2 * cols, SIDE * block.shape[0]), f32)],
+    )(packed, near)
+    shares = exchange(shares, False)
+    shares, back, front = lax.optimization_barrier((shares, back, front))
+    parts = call(plane_kernel, shape((2 * depth, cols, rows + TILE), jnp.int16), [VMEM])(shares)
+    far = along(back, 1)
     parts = lax.all_to_all(parts, ("z", "core"), 0, 0, tiled=True)
-    pieces = [near, back, front, far_low, far_high]
+    parts, far = lax.optimization_barrier((parts, far))
+    pieces = [near, back, front, far]
     swapped = [swap(p) for p in pieces]
 
     total = members * width
@@ -300,7 +305,7 @@
             shape((1, 2 * rows), f32),
             shape((4, 128), f32),
         ),
-        [SMEM] * 5 + [VMEM] * 11,
+        [SMEM] * 5 + [VMEM] * (1 + 2 * SIDE),
     )(place, counts, eig_low, eig_high, damping, parts, *pieces, *swapped)
     parts = sum_parts(parts)
     parts, direction, residual = call(step_kernel, (copies, state, state), [VMEM] * 5)(

time: 125 us -> 118 us (0.944)
  blocking collectives: 39.5 us -> 67.8 us
  starting transfers between devices: 40.1 us -> 17.6 us
  waiting for transfers between devices: 24.8 us -> 12 us
    all_to_all x0 -> x2, blocking collectives: none -> 26.1 us  [exchange(): lax.all_to_all(blocks, MEMBERS, 0, 0, axis_index_groups=lines(first), til...]
    ppermute x13 -> x3, waiting for transfers between devices: 14.6 us -> 0.01 us  [along(): return lax.ppermute(value, MEMBERS, ring_pairs(shift))]
    ppermute x6 -> x5, starting transfers between devices: 17.7 us -> 4.03 us  [swap(): return lax.ppermute(value, 'core', [(0, 1), (1, 0)])]
    ppermute x13 -> x3, starting transfers between devices: 13.8 us -> 2.3 us  [along(): return lax.ppermute(value, MEMBERS, ring_pairs(shift))]
    all_to_all x1, starting transfers between devices: 8.59 us -> 11.3 us  [body(): parts = lax.all_to_all(parts, ('z', 'core'), 0, 0, tiled=True)]
    all_to_all x1, blocking collectives: 13.2 us -> 15.5 us  [body(): out = lax.all_to_all(out, MEMBERS, 0, 0, tiled=True)]
  transfers between devices with their start and end apart: 20 -> 9, of which waited for: 6 -> 3; matrix products, arithmetic and copies ran while one was open for 0% -> 0% of each run, Pallas kernels for 1% -> 1%
where the time goes in v4:
time: 118 us; the launch traced here: 117 us
  blocking collectives  67.8 us (57%)
  starting transfers between devices  17.6 us (15%)
  Pallas kernels  13.5 us (11%)
  waiting for transfers between devices  12 us (10%)
  between operations  2.69 us (2%)
  other arithmetic  1.89 us (2%)
  local copies, waits for them, and re-layouts  1.53 us (1%)
    all_to_all x2, blocking collectives, sum_parts(): return lax.all_to_all(copies, 'z', 0, 0, tiled=True)  26.2 us
    all_to_all x2, blocking collectives, exchange(): lax.all_to_all(blocks, MEMBERS, 0, 0, axis_index_groups=lines(first), til...  26.1 us
    all_to_all x1, blocking collectives, body(): out = lax.all_to_all(out, MEMBERS, 0, 0, tiled=True)  15.5 us
    all_to_all x1, starting transfers between devices, body(): parts = lax.all_to_all(parts, ('z', 'core'), 0, 0, tiled=True)  11.3 us
    all_to_all x1, waiting for transfers between devices, body(): parts = lax.all_to_all(parts, ('z', 'core'), 0, 0, tiled=True)  10.4 us
    pallas_call x1, Pallas kernels, body(): call(rhs_kernel, (shape((total, 2 * rows), jnp.bfloat16), copies, state,...  5.39 us
    ppermute x5, starting transfers between devices, swap(): return lax.ppermute(value, 'core', [(0, 1), (1, 0)])  4.03 us
    pallas_call x1, Pallas kernels, body(): call(step_kernel, (copies, state, state), [VMEM] * 5)  3.39 us
  transfers between devices with their start and end apart: 9, of which 3 were waited for; matrix products, arithmetic and copies ran while one was open for 0% of the time, Pallas kernels for 1%

profile of v4, /device:TPU:1, one launch (start us, length us, event | category | flops | bytes accessed | tf_op | source)
XLA Modules:
  0.0 117.0 jit_solution(3342838952097457627)
XLA Ops:
  0.6 0.8 broadcast_select_fusion
  1.4 1.0 select_bitcast_fusion.1
  2.4 3.3 %collective-permute-start = (bf16[72,1024]{1,0:T(8,128)(2,1)S(1)}, bf16[72,1024]{1,0:T(8,128)(2,1)S(1)}, u32[]{:S(2)}, u32[]{:S(2)}) collective-permute-start(bf16[72,1024]{1,0:T(8,128)(2,1)S(1)} %pad_maximum_fusion), channel_id=1, source_target_pairs={{0,1},{1,0},{2,3},{3,2},{4,5},{5,4},{6,7},{7,6},{8,9},{9,8},{10,11... | collective-permute-start | bytes 442376 | tf_op jit(solution)/shard_map/ppermute | solution.py:58
  5.8 0.1 pad_add_fusion.place_ref
  5.8 0.9 collective-permute-done.got_ref
  6.8 0.8 shard_map.95
  7.6 12.0 %all_to_all.30.packed_ref = bf16[4,160,768]{2,1,0:T(8,128)(2,1)S(1)} all-to-all(bf16[4,160,768]{2,1,0:T(8,128)(2,1)S(1)} %shard_map.95), channel_id=1, replica_groups={{0,4,8,12},{128,132,136,140},{2,6,10,14},{130,134,138,142},{1,129,3,131..., dimensions={0} | all-to-all | bytes 1966080 | tf_op jit(solution)/shard_map/all_to_all | solution.py:50
  19.6 0.1 slice.17.near_ref.refs_0_
  19.7 2.3 %collective-permute-start.2 = (bf16[4,144,768]{2,1,0:T(8,128)(2,1)S(1)}, bf16[4,144,768]{2,1,0:T(8,128)(2,1)S(1)}, u32[]{:S(2)}, u32[]{:S(2)}) collective-permute-start(bf16[4,144,768]{2,1,0:T(8,128)(2,1)S(1)} %slice.17.near_ref.refs_0_), channel_id=1, source_target_pairs={{0,130},{1,13},{4,134},{5,1},{8,138},{9,5},{12,142},{13,9},{128,0}... | collective-permute-start | bytes 2654216 | tf_op jit(solution)/shard_map/ppermute | solution.py:54
  22.0 0.0 collective-permute-start.1
  22.0 0.3 shard_map.96
  22.3 14.1 %all_to_all.31.shares_ref = f32[4,16,768]{2,1,0:T(8,128)S(1)} all-to-all(f32[4,16,768]{2,1,0:T(8,128)S(1)} %shard_map.96), channel_id=1, replica_groups={{0,128,2,130},{4,132,6,134},{8,136,10,138},{12,140,14,142},{1,5,9,13},{..., dimensions={0} | all-to-all | bytes 393216 | tf_op jit(solution)/shard_map/all_to_all | solution.py:50
  36.4 0.0 collective-permute-done.2.refs_2_
  36.4 0.0 collective-permute-done.1.refs_1_
  36.4 0.0 collective-permute-start.3
  36.5 0.8 shard_map.97
  37.2 11.3 %all-to-all-start.2 = ((s16[16,8,896]{2,1,0:T(8,128)(2,1)}), s16[16,8,896]{2,1,0:T(8,128)(2,1)S(1)}, u32[]{:S(2)}, u32[]{:S(2)}) async-start(s16[16,8,896]{2,1,0:T(8,128)(2,1)} %shard_map.97), calls=%async_computation.2 | async-start | bytes 458752 | tf_op jit(solution)/shard_map/all_to_all | solution.py:291
  48.6 0.2 collective-permute-start.4
  48.8 0.3 collective-permute-start.5
  49.1 0.2 collective-permute-start.6
  49.3 10.4 %all-to-all-done.2.parts_ref = s16[16,8,896]{2,1,0:T(8,128)(2,1)S(1)} async-done(((s16[16,8,896]{2,1,0:T(8,128)(2,1)}), s16[16,8,896]{2,1,0:T(8,128)(2,1)S(1)}, u32[]{:S(2)}, u32[]{:S(2)}) %all-to-all-start.2) | async-done | bytes 229408 | tf_op jit(solution)/shard_map/all_to_all | solution.py:291
  59.6 0.0 collective-permute-done.3.refs_3_
  61.6 0.0 collective-permute-done.6.refs_6_
  61.6 0.7 collective-permute-done.7.refs_7_
  62.3 5.4 %shard_map.98 = (bf16[2304,1536]{1,0:T(8,128)(2,1)S(1)}, s16[8,8,1664]{2,1,0:T(8,128)(2,1)S(1)}, f32[8,1536]{1,0:T(8,128)S(1)}, f32[1,1536]{1,0:T(1,128)S(1)}, f32[4,128]{1,0:T(4,128)S(1)}) custom-call(s32[3]{0:T(128)S(1)} %pad_add_fusion.place_ref, s32[2]{0:T(128)S(1)} %copy-done, f32[1]{0:T(128)S(6)} %copy.13.low_ref, f32[1]{0:T(128)S(6)} %copy.14.high_ref, ...), custom_call_target="tpu_custom_call" | custom-call | tf_op jit(solution)/shard_map/pallas_call | solution.py:299
  67.7 13.7 %all_to_all.32.parts_ref = s16[8,8,1664]{2,1,0:T(8,128)(2,1)S(1)} all-to-all(s16[8,8,1664]{2,1,0:T(8,128)(2,1)S(1)} %get-tuple-element.22), channel_id=1, replica_groups=mesh['xl'=2,'z'=8,'y'=4,'xh'=2,'core'=2] {'z'}, dimensions={0} | all-to-all | bytes 425984 | tf_op jit(solution)/shard_map/all_to_all | solution.py:249
  81.3 3.4 %shard_map.99 = (s16[8,8,1664]{2,1,0:T(8,128)(2,1)S(1)}, f32[8,1536]{1,0:T(8,128)S(1)}, f32[8,1536]{1,0:T(8,128)S(1)}) custom-call(f32[4,128]{1,0:T(4,128)S(1)} %get-tuple-element.20.coef_ref, f32[1,1536]{1,0:T(1,128)S(1)} %get-tuple-element.21.scale_ref, s16[8,8,1664]{2,1,0:T(8,128)(2,1)S(1)} %all_to_all.32.parts_ref, ...), custom_call_target="tpu_custom_call" | custom-call | tf_op jit(solution)/shard_map/pallas_call | solution.py:311
  84.7 12.6 %all_to_all.33.parts_ref = s16[8,8,1664]{2,1,0:T(8,128)(2,1)S(1)} all-to-all(s16[8,8,1664]{2,1,0:T(8,128)(2,1)S(1)} %get-tuple-element.25), channel_id=1, replica_groups=mesh['xl'=2,'z'=8,'y'=4,'xh'=2,'core'=2] {'z'}, dimensions={0} | all-to-all | bytes 425984 | tf_op jit(solution)/shard_map/all_to_all | solution.py:249
  97.3 2.8 %shard_map.100 = f32[32,16,72]{2,1,0:T(8,128)S(1)} custom-call(s32[3]{0:T(128)S(1)} %pad_add_fusion.place_ref, f32[4,128]{1,0:T(4,128)S(1)} %get-tuple-element.20.coef_ref, f32[1,1536]{1,0:T(1,128)S(1)} %get-tuple-element.21.scale_ref, s16[8,8,1664]{2,1,0:T(8,128)(2,1)S(1)} %all_to_all.33.parts_ref, bf16[2304,1536]{1,0:T(8,128)(2,1)S(1)} %get-tuple-element.23.feats_ref, ...), custom_call_target="tpu_custom_call" | custom-call | tf_op jit(solution)/shard_map/pallas_call | solution.py:315
  100.1 15.5 %all_to_all.34 = f32[32,16,72]{2,1,0:T(8,128)S(1)} all-to-all(f32[32,16,72]{2,1,0:T(8,128)S(1)} %shard_map.100), channel_id=1, replica_groups=mesh['xl'=2,'z'=8,'y'=4,'xh'=2,'core'=2] {'xl','y','xh','core'}, dimensions={0} | all-to-all | bytes 294912 | tf_op jit(solution)/shard_map/all_to_all | solution.py:321
  115.6 0.7 copy.11
  116.3 0.7 copy.10
  (9 shorter events, 0.1 us)
Async XLA Ops:
  0.6 61.6 %copy-start = (s32[2]{0:T(128)S(1)}, s32[2]{0:T(128)}, u32[]{:S(2)}) copy-start(s32[2]{0:T(128)} %counts_ref.1) | copy-start | bytes 28
  2.4 4.3 %collective-permute-start = (bf16[72,1024]{1,0:T(8,128)(2,1)S(1)}, bf16[72,1024]{1,0:T(8,128)(2,1)S(1)}, u32[]{:S(2)}, u32[]{:S(2)}) collective-permute-start(bf16[72,1024]{1,0:T(8,128)(2,1)S(1)} %pad_maximum_fusion), channel_id=1, source_target_pairs={{0,1},{1,0},{2,3},{3,2},{4,5},{5,4},{6,7},{7,6},{8,9},{9,8},{10,11... | collective-permute-start | bytes 442376 | tf_op jit(solution)/shard_map/ppermute | solution.py:58
  19.7 16.8 %collective-permute-start.2 = (bf16[4,144,768]{2,1,0:T(8,128)(2,1)S(1)}, bf16[4,144,768]{2,1,0:T(8,128)(2,1)S(1)}, u32[]{:S(2)}, u32[]{:S(2)}) collective-permute-start(bf16[4,144,768]{2,1,0:T(8,128)(2,1)S(1)} %slice.17.near_ref.refs_0_), channel_id=1, source_target_pairs={{0,130},{1,13},{4,134},{5,1},{8,138},{9,5},{12,142},{13,9},{128,0}... | collective-permute-start | bytes 2654216 | tf_op jit(solution)/shard_map/ppermute | solution.py:54
  22.0 14.5 %collective-permute-start.1 = (bf16[4,144,768]{2,1,0:T(8,128)(2,1)S(1)}, bf16[4,144,768]{2,1,0:T(8,128)(2,1)S(1)}, u32[]{:S(2)}, u32[]{:S(2)}) collective-permute-start(bf16[4,144,768]{2,1,0:T(8,128)(2,1)S(1)} %slice.17.near_ref.refs_0_), channel_id=1, source_target_pairs={{0,128},{1,5},{4,132},{5,9},{8,136},{9,13},{12,140},{13,1},{128,2}... | collective-permute-start | bytes 2654216 | tf_op jit(solution)/shard_map/ppermute | solution.py:54
  36.4 23.2 %collective-permute-start.3 = (bf16[4,144,768]{2,1,0:T(8,128)(2,1)S(1)}, bf16[4,144,768]{2,1,0:T(8,128)(2,1)}, u32[]{:S(2)}, u32[]{:S(2)}) collective-permute-start(bf16[4,144,768]{2,1,0:T(8,128)(2,1)S(1)} %collective-permute-done.1.refs_1_), channel_id=1, source_target_pairs={{0,128},{1,5},{4,132},{5,9},{8,136},{9,13},{12,140},{13,1},{128,2}... | collective-permute-start | bytes 2654216 | tf_op jit(solution)/shard_map/ppermute | solution.py:54
  37.2 22.4 %all-to-all-start.2 = ((s16[16,8,896]{2,1,0:T(8,128)(2,1)}), s16[16,8,896]{2,1,0:T(8,128)(2,1)S(1)}, u32[]{:S(2)}, u32[]{:S(2)}) async-start(s16[16,8,896]{2,1,0:T(8,128)(2,1)} %shard_map.97), calls=%async_computation.2 | async-start | bytes 458752 | tf_op jit(solution)/shard_map/all_to_all | solution.py:291
  48.6 13.0 %collective-permute-start.4 = (bf16[4,144,768]{2,1,0:T(8,128)(2,1)S(1)}, bf16[4,144,768]{2,1,0:T(8,128)(2,1)}, u32[]{:S(2)}, u32[]{:S(2)}) collective-permute-start(bf16[4,144,768]{2,1,0:T(8,128)(2,1)S(1)} %slice.17.near_ref.refs_0_), channel_id=1, source_target_pairs={{0,1},{1,0},{2,3},{3,2},{4,5},{5,4},{6,7},{7,6},{8,9},{9,8},{10,11... | collective-permute-start | bytes 2654216 | tf_op jit(solution)/shard_map/ppermute | solution.py:58
  48.8 12.8 %collective-permute-start.5 = (bf16[4,144,768]{2,1,0:T(8,128)(2,1)S(1)}, bf16[4,144,768]{2,1,0:T(8,128)(2,1)}, u32[]{:S(2)}, u32[]{:S(2)}) collective-permute-start(bf16[4,144,768]{2,1,0:T(8,128)(2,1)S(1)} %collective-permute-done.1.refs_1_), channel_id=1, source_target_pairs={{0,1},{1,0},{2,3},{3,2},{4,5},{5,4},{6,7},{7,6},{8,9},{9,8},{10,11... | collective-permute-start | bytes 2654216 | tf_op jit(solution)/shard_map/ppermute | solution.py:58
  49.1 12.5 %collective-permute-start.6 = (bf16[4,144,768]{2,1,0:T(8,128)(2,1)S(1)}, bf16[4,144,768]{2,1,0:T(8,128)(2,1)}, u32[]{:S(2)}, u32[]{:S(2)}) collective-permute-start(bf16[4,144,768]{2,1,0:T(8,128)(2,1)S(1)} %collective-permute-done.2.refs_2_), channel_id=1, source_target_pairs={{0,1},{1,0},{2,3},{3,2},{4,5},{5,4},{6,7},{7,6},{8,9},{9,8},{10,11... | collective-permute-start | bytes 2654216 | tf_op jit(solution)/shard_map/ppermute | solution.py:58
  59.6 2.6 %collective-permute-start.7 = (bf16[4,144,768]{2,1,0:T(8,128)(2,1)}, bf16[4,144,768]{2,1,0:T(8,128)(2,1)S(1)}, u32[]{:S(2)}, u32[]{:S(2)}) collective-permute-start(bf16[4,144,768]{2,1,0:T(8,128)(2,1)} %collective-permute-done.3.refs_3_), channel_id=1, source_target_pairs={{0,1},{1,0},{2,3},{3,2},{4,5},{5,4},{6,7},{7,6},{8,9},{9,8},{10,11... | collective-permute-start | bytes 2654216 | tf_op jit(solution)/shard_map/ppermute | solution.py:58

commit v5 on v4

--- a/solution.py
+++ b/solution.py
@@ -118,8 +118,8 @@
 def pack_kernel(place_ref, block_ref, keep_ref, got_ref, out_ref, held, strip):
     lead = place_ref[2] == 0
     deep = block_ref.shape[0]
-    keep = keep_ref[...].astype(jnp.float32)
-    got = got_ref[:, got_ref.shape[1] - keep.shape[1] :].astype(jnp.float32)
+    keep = keep_ref[:, block_ref.shape[1] :].astype(jnp.float32)
+    got = got_ref[:, block_ref.shape[1] :].astype(jnp.float32)
     chips, each, width = held.shape[1:]
     for k, rows in enumerate((jnp.where(lead, keep, got), jnp.where(lead, got, keep))):
         turned = rows.T
@@ -163,20 +163,22 @@
         out_ref[k] = coded[k % 2]
 
 
-def rhs_kernel(place_ref, counts_ref, low_ref, high_ref, ridge_ref, parts_ref, *refs):
-    mine, theirs = refs[:SIDE], refs[SIDE : 2 * SIDE]
-    feats_ref, out_ref, rhs_ref, scale_ref, coef_ref = refs[2 * SIDE :]
+def lay_kernel(place_ref, *refs):
+    mine, theirs = refs[:SIDE], refs[SIDE : SIDE + 2]
+    own_ref, other_ref = refs[SIDE + 2 :]
+    deep = mine[0].shape[1]
+    line, _ = line_place(place_ref)
+    for inner in range(SIDE):
+        here = lax.rem(line + SIDE - ORDER[inner], SIDE)
+        for outer in range(SIDE):
+            at = (inner * SIDE + outer) * deep
+            own_ref[at : at + deep] = mine[outer][here]
+    lay_others(place_ref, theirs, other_ref)
+
+
+def coef_kernel(place_ref, counts_ref, low_ref, high_ref, ridge_ref, scale_ref, coef_ref):
     core = place_ref[2]
-    deep, rows = mine[0].shape[1:]
-    line, across = line_place(place_ref)
-    for outer in range(SIDE):
-        there = lax.rem(across + SIDE - ORDER[outer], SIDE)
-        for inner in range(SIDE):
-            here = lax.rem(line + SIDE - ORDER[inner], SIDE)
-            at = (outer * SIDE + inner) * deep
-            feats_ref[at : at + deep, :rows] = mine[outer][here]
-            feats_ref[at : at + deep, rows:] = theirs[inner][there]
-
+    rows = scale_ref.shape[1] // 2
     position = lax.broadcasted_iota(jnp.int32, (1, 2 * rows), 1)
     other = position >= rows
     within = jnp.where(other, position - rows, position)
@@ -194,44 +196,80 @@
     coef_ref[2:3] = rho_new * rho
     coef_ref[3:4] = 2.0 * rho_new / radius
 
+
+def lay_others(place_ref, theirs, other_ref):
+    deep = theirs[0].shape[1]
+    _, across = line_place(place_ref)
+    for inner in range(2):
+        for outer in range(SIDE):
+            there = lax.rem(across + SIDE - ORDER[outer], SIDE)
+            at = (inner * SIDE + outer) * deep
+            other_ref[at : at + deep] = theirs[inner][there]
+
+
+def rhs_kernel(place_ref, coef_ref, scale_ref, parts_ref, own_ref, first_ref, *refs):
+    theirs, (second_ref, out_ref, rhs_ref) = refs[:2], refs[2:]
+    core = place_ref[2]
+    rows = own_ref.shape[1]
+    lay_others(place_ref, theirs, second_ref)
     half = parts_ref.shape[0] // 2
     for at, side in ((core, 0), (1 - core, 1)):
         total = sum_coded(parts_ref, [2 * k + at for k in range(half)])
         rhs_ref[:, side * rows : (side + 1) * rows] = total
-    ahead(rhs_ref[...] / coef_ref[0:1, 0:1], scale_ref, feats_ref, out_ref)
-
-
-def ahead(direction, scale_ref, feats_ref, out_ref):
-    feats = feats_ref[...]
-    send_all(times(times(direction * scale_ref[...], feats, NT), feats, NN), out_ref)
-
-
-def step_kernel(coef_ref, scale_ref, parts_ref, feats_ref, rhs_ref, out_ref, dir_ref, res_ref):
+    ahead(rhs_ref[...] / coef_ref[0:1, 0:1], scale_ref, (own_ref, first_ref, second_ref), out_ref)
+
+
+def to_features(value, feats):
+    own, first, second = (f[...] for f in feats)
+    rows = own.shape[1]
+    other = jnp.concatenate(
+        [times(value[:, rows:], first, NT), times(value[:, rows:], second, NT)], axis=1
+    )
+    return times(value[:, :rows], own, NT) + other
+
+
+def ahead(direction, scale_ref, feats, out_ref):
+    own, first, second = (f[...] for f in feats)
+    half = first.shape[0]
+    inner = to_features(direction * scale_ref[...], feats)
+    left = times(inner, own, NN)
+    right = times(inner[:, :half], first, NN) + times(inner[:, half:], second, NN)
+    send_all(jnp.concatenate([left, right], axis=1), out_ref)
+
+
+def step_kernel(coef_ref, scale_ref, parts_ref, *refs):
+    feats, (rhs_ref, out_ref, dir_ref, res_ref) = refs[:3], refs[3:]
     first = rhs_ref[...] / coef_ref[0:1, 0:1]
     image = sum_coded(parts_ref, range(parts_ref.shape[0])) + coef_ref[1:2, 0:1] * first
     residual = rhs_ref[...] - image
     direction = coef_ref[2:3, 0:1] * first + coef_ref[3:4, 0:1] * residual
     dir_ref[...] = direction
     res_ref[...] = residual
-    ahead(direction, scale_ref, feats_ref, out_ref)
-
-
-def last_kernel(
-    place_ref, coef_ref, scale_ref, parts_ref, feats_ref, rhs_ref, dir_ref, res_ref, out_ref, held
-):
+    ahead(direction, scale_ref, feats, out_ref)
+
+
+def last_kernel(place_ref, coef_ref, scale_ref, parts_ref, *refs):
+    feats, (rhs_ref, dir_ref, res_ref, out_ref, held) = refs[:3], refs[3:]
     direction = dir_ref[...]
     image = sum_coded(parts_ref, range(parts_ref.shape[0])) + coef_ref[1:2, 0:1] * direction
     residual = res_ref[...] - image
     merged = rhs_ref[...] / coef_ref[0:1, 0:1] + direction
     both = jnp.concatenate([merged, residual], axis=0) * scale_ref[...]
-    held[...] = times(both, feats_ref[...], NT)
+    held[...] = to_features(both, feats)
     width = out_ref.shape[2]
-    for outer in range(SIDE):
-        for inner in range(SIDE):
-            at = (outer * SIDE + inner) * 2 * width
+    for inner in range(SIDE):
+        for outer in range(SIDE):
+            at = (inner * SIDE + outer) * 2 * width
             origin = source(place_ref, ORDER[inner], ORDER[outer])
             for k in range(2):
                 out_ref[origin + k] = held[:, at + k * width : at + (k + 1) * width]
+
+
+def turn_kernel(blocks_ref, merged_ref, residual_ref):
+    members, both, width = blocks_ref.shape
+    cols = both // 2
+    merged_ref[...] = blocks_ref[:, :cols].reshape(members * cols, width).T
+    residual_ref[...] = blocks_ref[:, cols:].reshape(members * cols, width).T
 
 
 def call(kernel, outs, specs, scratch=()):
@@ -261,11 +299,11 @@
     place = place.astype(jnp.int32)
 
     lead = core == 0
-    mine = jnp.where(lead, x_first, x_second).T
-    give = jnp.where(lead, x_second, x_first).T
-    keep_w, give_w = jnp.where(lead, w_first, w_second), jnp.where(lead, w_second, w_first)
-    got_all = swap(jnp.concatenate([give, give_w], axis=1))
-    got = got_all[:, :rows]
+    first = jnp.concatenate([x_first.T, w_first], axis=1)
+    second = jnp.concatenate([x_second.T, w_second], axis=1)
+    kept, give = jnp.where(lead, first, second), jnp.where(lead, second, first)
+    got_all = swap(give)
+    mine, got = kept[:, :rows], got_all[:, :rows]
     block = jnp.where(
         lead, jnp.concatenate([mine, got], axis=0), jnp.concatenate([got, mine], axis=0)
     )
@@ -274,7 +312,7 @@
         shape((SIDE, block.shape[0] + 2 * cols, rows), jnp.bfloat16),
         [SMEM] + [VMEM] * 3,
         [pltpu.VMEM((2, members // 2, 2 * cols, width), f32), pltpu.VMEM((2 * cols, rows), f32)],
-    )(place, block, keep_w, got_all)
+    )(place, block, kept, got_all)
     packed = exchange(packed, True)
     near = packed[:, : block.shape[0]]
     back, front = along(near, 1), along(near, 3)
@@ -288,40 +326,45 @@
     shares, back, front = lax.optimization_barrier((shares, back, front))
     parts = call(plane_kernel, shape((2 * depth, cols, rows + TILE), jnp.int16), [VMEM])(shares)
     far = along(back, 1)
+    parts, eig_low, eig_high, damping = lax.optimization_barrier(
+        (parts, eig_low, eig_high, damping)
+    )
+    scale, coef = call(
+        coef_kernel, (shape((1, 2 * rows), f32), shape((4, 128), f32)), [SMEM] * 5
+    )(place, counts, eig_low, eig_high, damping)
     parts = lax.all_to_all(parts, ("z", "core"), 0, 0, tiled=True)
-    parts, far = lax.optimization_barrier((parts, far))
+    parts, far, scale, coef = lax.optimization_barrier((parts, far, scale, coef))
     pieces = [near, back, front, far]
     swapped = [swap(p) for p in pieces]
 
     total = members * width
     copies = shape((depth, cols, 2 * rows + TILE), jnp.int16)
     state = shape((cols, 2 * rows), f32)
-    feats, parts, rhs, scale, coef = call(
+    own, first = call(
+        lay_kernel,
+        (shape((total, rows), jnp.bfloat16), shape((total // 2, rows), jnp.bfloat16)),
+        [SMEM] + [VMEM] * (SIDE + 2),
+    )(place, *pieces, *swapped[:2])
+    second, parts, rhs = call(
         rhs_kernel,
-        (
-            shape((total, 2 * rows), jnp.bfloat16),
-            copies,
-            state,
-            shape((1, 2 * rows), f32),
-            shape((4, 128), f32),
-        ),
-        [SMEM] * 5 + [VMEM] * (1 + 2 * SIDE),
-    )(place, counts, eig_low, eig_high, damping, parts, *pieces, *swapped)
+        (shape((total // 2, rows), jnp.bfloat16), copies, state),
+        [SMEM] + [VMEM] * 7,
+    )(place, coef, scale, parts, own, first, *swapped[2:])
+    feats = (own, first, second)
     parts = sum_parts(parts)
-    parts, direction, residual = call(step_kernel, (copies, state, state), [VMEM] * 5)(
-        coef, scale, parts, feats, rhs
+    parts, direction, residual = call(step_kernel, (copies, state, state), [VMEM] * 7)(
+        coef, scale, parts, *feats, rhs
     )
     parts = sum_parts(parts)
     out = call(
         last_kernel,
         shape((members, 2 * cols, width), f32),
-        [SMEM] + [VMEM] * 7,
+        [SMEM] + [VMEM] * 9,
         [pltpu.VMEM((2 * cols, total), f32)],
-    )(place, coef, scale, parts, feats, rhs, direction, residual)
+    )(place, coef, scale, parts, *feats, rhs, direction, residual)
     out = lax.all_to_all(out, MEMBERS, 0, 0, tiled=True)
-    merged = out[:, :cols].reshape(members * cols, width).T
-    residual = out[:, cols:].reshape(members * cols, width).T
-    return merged, residual
+    turned = shape((width, members * cols), f32)
+    return tuple(call(turn_kernel, (turned, turned), [VMEM])(out))
 
 
 def solution(mesh):

time: 118 us -> 113 us (0.958)
  blocking collectives: 67.8 us -> 64.6 us
  waiting for transfers between devices: 12 us -> 9.28 us
  Pallas kernels: 13.5 us -> 15.6 us
  starting transfers between devices: 17.6 us -> 19.5 us
  local copies, waits for them, and re-layouts: 1.53 us -> 0.08 us
    all_to_all x1, waiting for transfers between devices: 10.4 us -> 7.82 us  [body(): parts = lax.all_to_all(parts, ('z', 'core'), 0, 0, tiled=True)]
    all_to_all x2, blocking collectives: 26.1 us -> 23.9 us  [exchange(): lax.all_to_all(blocks, MEMBERS, 0, 0, axis_index_groups=lines(first), til...]
    pallas_call x2 -> x5, Pallas kernels: 8.78 us -> 10.9 us  [the longest x1 4.35 us: body(): call(rhs_kernel, (shape((total // 2, rows), jnp.bfloat16), copies, state)...]
    ppermute x3, starting transfers between devices: 2.3 us -> 3.91 us  [along(): return lax.ppermute(value, MEMBERS, ring_pairs(shift))]
    reshape x3 -> x0, local copies, waits for them, and re-layouts: 1.45 us -> none  [the longest x2 0.74 us: body(): residual = out[:, cols:].reshape(members * cols, width).T]
  transfers between devices with their start and end apart: 9 -> 9, of which waited for: 3 -> 3; matrix products, arithmetic and copies ran while one was open for 0% -> 0% of each run, Pallas kernels for 1% -> 3%
where the time goes in v5:
time: 113 us
  blocking collectives  64.6 us (57%)
  starting transfers between devices  19.5 us (17%)
  Pallas kernels  15.6 us (14%)
  waiting for transfers between devices  9.28 us (8%)
  between operations  2.7 us (2%)
  other arithmetic  1.17 us (1%)
    all_to_all x2, blocking collectives, sum_parts(): return lax.all_to_all(copies, 'z', 0, 0, tiled=True)  26.2 us
    all_to_all x2, blocking collectives, exchange(): lax.all_to_all(blocks, MEMBERS, 0, 0, axis_index_groups=lines(first), til...  23.9 us
    all_to_all x1, blocking collectives, body(): out = lax.all_to_all(out, MEMBERS, 0, 0, tiled=True)  14.5 us
    all_to_all x1, starting transfers between devices, body(): parts = lax.all_to_all(parts, ('z', 'core'), 0, 0, tiled=True)  11.6 us
    all_to_all x1, waiting for transfers between devices, body(): parts = lax.all_to_all(parts, ('z', 'core'), 0, 0, tiled=True)  7.82 us
    pallas_call x1, Pallas kernels, body(): call(rhs_kernel, (shape((total // 2, rows), jnp.bfloat16), copies, state)...  4.35 us
    ppermute x5, starting transfers between devices, swap(): return lax.ppermute(value, 'core', [(0, 1), (1, 0)])  4.03 us
    ppermute x3, starting transfers between devices, along(): return lax.ppermute(value, MEMBERS, ring_pairs(shift))  3.91 us
  transfers between devices with their start and end apart: 9, of which 3 were waited for; matrix products, arithmetic and copies ran while one was open for 0% of the time, Pallas kernels for 3%

profile of v5, /device:TPU:1, one launch (start us, length us, event | category | flops | bytes accessed | tf_op | source)
XLA Modules:
  0.0 113.0 jit_solution(4799424425536474034)
XLA Ops:
  0.6 1.0 broadcast_select_fusion.1
  1.7 3.3 %collective-permute-start = (bf16[72,1024]{1,0:T(8,128)(2,1)S(1)}, bf16[72,1024]{1,0:T(8,128)(2,1)S(1)}, u32[]{:S(2)}, u32[]{:S(2)}) collective-permute-start(bf16[72,1024]{1,0:T(8,128)(2,1)S(1)} %get-tuple-element.45), channel_id=1, source_target_pairs={{0,1},{1,0},{2,3},{3,2},{4,5},{5,4},{6,7},{7,6},{8,9},{9,8},{10,11... | collective-permute-start | bytes 442376 | tf_op jit(solution)/shard_map/ppermute | solution.py:58
  5.0 0.1 pad_add_fusion.place_ref
  5.1 0.9 collective-permute-done.got_ref
  6.1 0.8 shard_map.95
  6.9 12.0 %all_to_all.30.packed_ref = bf16[4,160,768]{2,1,0:T(8,128)(2,1)S(1)} all-to-all(bf16[4,160,768]{2,1,0:T(8,128)(2,1)S(1)} %shard_map.95), channel_id=1, replica_groups={{0,4,8,12},{128,132,136,140},{2,6,10,14},{130,134,138,142},{1,129,3,131..., dimensions={0} | all-to-all | bytes 1966080 | tf_op jit(solution)/shard_map/all_to_all | solution.py:50
  18.9 0.1 slice.14.near_ref.refs_0_
  18.9 0.0 copy-start
  18.9 0.9 collective-permute-start.1
  19.8 1.9 %collective-permute-start.2 = (bf16[4,144,768]{2,1,0:T(8,128)(2,1)S(1)}, bf16[4,144,768]{2,1,0:T(8,128)(2,1)S(1)}, u32[]{:S(2)}, u32[]{:S(2)}) collective-permute-start(bf16[4,144,768]{2,1,0:T(8,128)(2,1)S(1)} %slice.14.near_ref.refs_0_), channel_id=1, source_target_pairs={{0,130},{1,13},{4,134},{5,1},{8,138},{9,5},{12,142},{13,9},{128,0}... | collective-permute-start | bytes 2654216 | tf_op jit(solution)/shard_map/ppermute | solution.py:54
  21.7 0.3 shard_map.96
  22.0 11.9 %all_to_all.31.shares_ref = f32[4,16,768]{2,1,0:T(8,128)S(1)} all-to-all(f32[4,16,768]{2,1,0:T(8,128)S(1)} %shard_map.96), channel_id=1, replica_groups={{0,128,2,130},{4,132,6,134},{8,136,10,138},{12,140,14,142},{1,5,9,13},{..., dimensions={0} | all-to-all | bytes 393216 | tf_op jit(solution)/shard_map/all_to_all | solution.py:50
  33.9 1.2 %collective-permute-start.3 = (bf16[4,144,768]{2,1,0:T(8,128)(2,1)S(1)}, bf16[4,144,768]{2,1,0:T(8,128)(2,1)}, u32[]{:S(2)}, u32[]{:S(2)}) collective-permute-start(bf16[4,144,768]{2,1,0:T(8,128)(2,1)S(1)} %collective-permute-done.1.refs_1_), channel_id=1, source_target_pairs={{0,128},{1,5},{4,132},{5,9},{8,136},{9,13},{12,140},{13,1},{128,2}... | collective-permute-start | bytes 2654216 | tf_op jit(solution)/shard_map/ppermute | solution.py:54
  35.1 0.8 shard_map.97
  35.9 11.6 %all-to-all-start.2 = ((s16[16,8,896]{2,1,0:T(8,128)(2,1)}), s16[16,8,896]{2,1,0:T(8,128)(2,1)S(1)}, u32[]{:S(2)}, u32[]{:S(2)}) async-start(s16[16,8,896]{2,1,0:T(8,128)(2,1)} %shard_map.97), calls=%async_computation.2 | async-start | bytes 458752 | tf_op jit(solution)/shard_map/all_to_all | solution.py:335
  49.4 0.6 shard_map.98
  50.0 0.2 collective-permute-start.4
  50.2 0.4 collective-permute-start.5
  50.6 0.1 collective-permute-start.6
  50.7 7.8 %all-to-all-done.2.parts_ref = s16[16,8,896]{2,1,0:T(8,128)(2,1)S(1)} async-done(((s16[16,8,896]{2,1,0:T(8,128)(2,1)}), s16[16,8,896]{2,1,0:T(8,128)(2,1)S(1)}, u32[]{:S(2)}, u32[]{:S(2)}) %all-to-all-start.2) | async-done | bytes 229408 | tf_op jit(solution)/shard_map/all_to_all | solution.py:335
  58.5 0.0 collective-permute-done.3.refs_3_
  58.5 0.0 collective-permute-start.7
  58.5 0.0 collective-permute-done.4.refs_4_
  58.5 2.1 %shard_map.99 = (bf16[2304,768]{1,0:T(8,128)(2,1)S(1)}, bf16[1152,768]{1,0:T(8,128)(2,1)S(1)}) custom-call(s32[3]{0:T(128)S(1)} %pad_add_fusion.place_ref, bf16[4,144,768]{2,1,0:T(8,128)(2,1)S(1)} %slice.14.near_ref.refs_0_, bf16[4,144,768]{2,1,0:T(8,128)(2,1)S(1)} %collective-permute-done.1.refs_1_, ...), custom_call_target="tpu_custom_call" | custom-call | tf_op jit(solution)/shard_map/pallas_call | solution.py:343
  60.6 0.5 collective-permute-done.7.refs_1_
  61.2 4.3 %shard_map.100 = (bf16[1152,768]{1,0:T(8,128)(2,1)S(1)}, s16[8,8,1664]{2,1,0:T(8,128)(2,1)S(1)}, f32[8,1536]{1,0:T(8,128)S(1)}) custom-call(s32[3]{0:T(128)S(1)} %pad_add_fusion.place_ref, f32[4,128]{1,0:T(4,128)S(1)} %get-tuple-element.31.coef_ref, f32[1,1536]{1,0:T(1,128)S(1)} %get-tuple-element.32.scale_ref, ...), custom_call_target="tpu_custom_call" | custom-call | tf_op jit(solution)/shard_map/pallas_call | solution.py:348
  65.5 13.7 %all_to_all.32.parts_ref = s16[8,8,1664]{2,1,0:T(8,128)(2,1)S(1)} all-to-all(s16[8,8,1664]{2,1,0:T(8,128)(2,1)S(1)} %get-tuple-element.38), channel_id=1, replica_groups=mesh['xl'=2,'z'=8,'y'=4,'xh'=2,'core'=2] {'z'}, dimensions={0} | all-to-all | bytes 425984 | tf_op jit(solution)/shard_map/all_to_all | solution.py:287
  79.2 3.2 %shard_map.101 = (s16[8,8,1664]{2,1,0:T(8,128)(2,1)S(1)}, f32[8,1536]{1,0:T(8,128)S(1)}, f32[8,1536]{1,0:T(8,128)S(1)}) custom-call(f32[4,128]{1,0:T(4,128)S(1)} %get-tuple-element.31.coef_ref, f32[1,1536]{1,0:T(1,128)S(1)} %get-tuple-element.32.scale_ref, s16[8,8,1664]{2,1,0:T(8,128)(2,1)S(1)} %all_to_all.32.parts_ref, ...), custom_call_target="tpu_custom_call" | custom-call | tf_op jit(solution)/shard_map/pallas_call | solution.py:355
  82.4 12.6 %all_to_all.33.parts_ref = s16[8,8,1664]{2,1,0:T(8,128)(2,1)S(1)} all-to-all(s16[8,8,1664]{2,1,0:T(8,128)(2,1)S(1)} %get-tuple-element.41), channel_id=1, replica_groups=mesh['xl'=2,'z'=8,'y'=4,'xh'=2,'core'=2] {'z'}, dimensions={0} | all-to-all | bytes 425984 | tf_op jit(solution)/shard_map/all_to_all | solution.py:287
  94.9 2.8 %shard_map.102 = f32[32,16,72]{2,1,0:T(8,128)S(1)} custom-call(s32[3]{0:T(128)S(1)} %pad_add_fusion.place_ref, f32[4,128]{1,0:T(4,128)S(1)} %get-tuple-element.31.coef_ref, f32[1,1536]{1,0:T(1,128)S(1)} %get-tuple-element.32.scale_ref, s16[8,8,1664]{2,1,0:T(8,128)(2,1)S(1)} %all_to_all.33.parts_ref, bf16[2304,768]{1,0:T(8,128)(2,1)S(1)} %get-tuple-element.36.own_ref.refs_0_, ...), custom_call_target="tpu_custom_call" | custom-call | tf_op jit(solution)/shard_map/pallas_call | solution.py:359
  97.7 14.5 %all_to_all.34.blocks_ref = f32[32,16,72]{2,1,0:T(8,128)S(1)} all-to-all(f32[32,16,72]{2,1,0:T(8,128)S(1)} %shard_map.102), channel_id=1, replica_groups=mesh['xl'=2,'z'=8,'y'=4,'xh'=2,'core'=2] {'xl','y','xh','core'}, dimensions={0} | all-to-all | bytes 294912 | tf_op jit(solution)/shard_map/all_to_all | solution.py:365
  112.2 0.8 shard_map.103
  (8 shorter events, 0.1 us)
Async XLA Ops:
  1.7 4.3 %collective-permute-start = (bf16[72,1024]{1,0:T(8,128)(2,1)S(1)}, bf16[72,1024]{1,0:T(8,128)(2,1)S(1)}, u32[]{:S(2)}, u32[]{:S(2)}) collective-permute-start(bf16[72,1024]{1,0:T(8,128)(2,1)S(1)} %get-tuple-element.45), channel_id=1, source_target_pairs={{0,1},{1,0},{2,3},{3,2},{4,5},{5,4},{6,7},{7,6},{8,9},{9,8},{10,11... | collective-permute-start | bytes 442376 | tf_op jit(solution)/shard_map/ppermute | solution.py:58
  18.9 30.5 %copy-start = (s32[2]{0:T(128)S(1)}, s32[2]{0:T(128)}, u32[]{:S(2)}) copy-start(s32[2]{0:T(128)} %counts_ref.1) | copy-start | bytes 28
  18.9 15.0 %collective-permute-start.1 = (bf16[4,144,768]{2,1,0:T(8,128)(2,1)S(1)}, bf16[4,144,768]{2,1,0:T(8,128)(2,1)S(1)}, u32[]{:S(2)}, u32[]{:S(2)}) collective-permute-start(bf16[4,144,768]{2,1,0:T(8,128)(2,1)S(1)} %slice.14.near_ref.refs_0_), channel_id=1, source_target_pairs={{0,128},{1,5},{4,132},{5,9},{8,136},{9,13},{12,140},{13,1},{128,2}... | collective-permute-start | bytes 2654216 | tf_op jit(solution)/shard_map/ppermute | solution.py:54
  19.8 14.1 %collective-permute-start.2 = (bf16[4,144,768]{2,1,0:T(8,128)(2,1)S(1)}, bf16[4,144,768]{2,1,0:T(8,128)(2,1)S(1)}, u32[]{:S(2)}, u32[]{:S(2)}) collective-permute-start(bf16[4,144,768]{2,1,0:T(8,128)(2,1)S(1)} %slice.14.near_ref.refs_0_), channel_id=1, source_target_pairs={{0,130},{1,13},{4,134},{5,1},{8,138},{9,5},{12,142},{13,9},{128,0}... | collective-permute-start | bytes 2654216 | tf_op jit(solution)/shard_map/ppermute | solution.py:54
  33.9 24.6 %collective-permute-start.3 = (bf16[4,144,768]{2,1,0:T(8,128)(2,1)S(1)}, bf16[4,144,768]{2,1,0:T(8,128)(2,1)}, u32[]{:S(2)}, u32[]{:S(2)}) collective-permute-start(bf16[4,144,768]{2,1,0:T(8,128)(2,1)S(1)} %collective-permute-done.1.refs_1_), channel_id=1, source_target_pairs={{0,128},{1,5},{4,132},{5,9},{8,136},{9,13},{12,140},{13,1},{128,2}... | collective-permute-start | bytes 2654216 | tf_op jit(solution)/shard_map/ppermute | solution.py:54
  35.9 22.7 %all-to-all-start.2 = ((s16[16,8,896]{2,1,0:T(8,128)(2,1)}), s16[16,8,896]{2,1,0:T(8,128)(2,1)S(1)}, u32[]{:S(2)}, u32[]{:S(2)}) async-start(s16[16,8,896]{2,1,0:T(8,128)(2,1)} %shard_map.97), calls=%async_computation.2 | async-start | bytes 458752 | tf_op jit(solution)/shard_map/all_to_all | solution.py:335
  50.0 8.5 %collective-permute-start.4 = (bf16[4,144,768]{2,1,0:T(8,128)(2,1)S(1)}, bf16[4,144,768]{2,1,0:T(8,128)(2,1)}, u32[]{:S(2)}, u32[]{:S(2)}) collective-permute-start(bf16[4,144,768]{2,1,0:T(8,128)(2,1)S(1)} %slice.14.near_ref.refs_0_), channel_id=1, source_target_pairs={{0,1},{1,0},{2,3},{3,2},{4,5},{5,4},{6,7},{7,6},{8,9},{9,8},{10,11... | collective-permute-start | bytes 2654216 | tf_op jit(solution)/shard_map/ppermute | solution.py:58
  50.2 8.4 %collective-permute-start.5 = (bf16[4,144,768]{2,1,0:T(8,128)(2,1)S(1)}, bf16[4,144,768]{2,1,0:T(8,128)(2,1)}, u32[]{:S(2)}, u32[]{:S(2)}) collective-permute-start(bf16[4,144,768]{2,1,0:T(8,128)(2,1)S(1)} %collective-permute-done.1.refs_1_), channel_id=1, source_target_pairs={{0,1},{1,0},{2,3},{3,2},{4,5},{5,4},{6,7},{7,6},{8,9},{9,8},{10,11... | collective-permute-start | bytes 2654216 | tf_op jit(solution)/shard_map/ppermute | solution.py:58
  50.6 10.0 %collective-permute-start.6 = (bf16[4,144,768]{2,1,0:T(8,128)(2,1)S(1)}, bf16[4,144,768]{2,1,0:T(8,128)(2,1)}, u32[]{:S(2)}, u32[]{:S(2)}) collective-permute-start(bf16[4,144,768]{2,1,0:T(8,128)(2,1)S(1)} %collective-permute-done.2.refs_2_), channel_id=1, source_target_pairs={{0,1},{1,0},{2,3},{3,2},{4,5},{5,4},{6,7},{7,6},{8,9},{9,8},{10,11... | collective-permute-start | bytes 2654216 | tf_op jit(solution)/shard_map/ppermute | solution.py:58
  58.5 2.6 %collective-permute-start.7 = (bf16[4,144,768]{2,1,0:T(8,128)(2,1)}, bf16[4,144,768]{2,1,0:T(8,128)(2,1)S(1)}, u32[]{:S(2)}, u32[]{:S(2)}) collective-permute-start(bf16[4,144,768]{2,1,0:T(8,128)(2,1)} %collective-permute-done.3.refs_3_), channel_id=1, source_target_pairs={{0,1},{1,0},{2,3},{3,2},{4,5},{5,4},{6,7},{7,6},{8,9},{9,8},{10,11... | collective-permute-start | bytes 2654216 | tf_op jit(solution)/shard_map/ppermute | solution.py:58

commit v6 on v5

--- a/solution.py
+++ b/solution.py
@@ -155,7 +155,7 @@
         out_ref[across] = out[across * each : (across + 1) * each]
 
 
-def plane_kernel(shares_ref, out_ref):
+def plane_kernel(shares_ref, _, out_ref, __):
     total = jnp.sum(shares_ref[...], axis=0)
     cols = out_ref.shape[1]
     coded = [code(total[k * cols : (k + 1) * cols]) for k in range(2)]
@@ -323,8 +323,18 @@
         [pltpu.VMEM((SIDE * 2 * cols, SIDE * block.shape[0]), f32)],
     )(packed, near)
     shares = exchange(shares, False)
-    shares, back, front = lax.optimization_barrier((shares, back, front))
-    parts = call(plane_kernel, shape((2 * depth, cols, rows + TILE), jnp.int16), [VMEM])(shares)
+    anywhere = pl.BlockSpec(memory_space=pl.ANY)
+    parts, back = pl.pallas_call(
+        plane_kernel,
+        out_shape=(
+            shape((2 * depth, cols, rows + TILE), jnp.int16),
+            shape(back.shape, back.dtype),
+        ),
+        in_specs=[VMEM, anywhere],
+        out_specs=(VMEM, anywhere),
+        input_output_aliases={1: 1},
+        compiler_params=pltpu.CompilerParams(vmem_limit_bytes=32 * 1024 * 1024),
+    )(shares, back)
     far = along(back, 1)
     parts, eig_low, eig_high, damping = lax.optimization_barrier(
         (parts, eig_low, eig_high, damping)

time: 113 us -> 113 us (level)
  blocking collectives: 64.6 us -> 53.7 us
  waiting for transfers between devices: 9.28 us -> 15.8 us
  starting transfers between devices: 19.5 us -> 22.8 us
    all_to_all x2 -> x1, blocking collectives: 23.9 us -> 12 us  [exchange(): lax.all_to_all(blocks, MEMBERS, 0, 0, axis_index_groups=lines(first), til...]
    all_to_all x0 -> x1, waiting for transfers between devices: none -> 6.53 us  [exchange(): lax.all_to_all(blocks, MEMBERS, 0, 0, axis_index_groups=lines(first), til...]
    all_to_all x0 -> x1, starting transfers between devices: none -> 3.89 us  [exchange(): lax.all_to_all(blocks, MEMBERS, 0, 0, axis_index_groups=lines(first), til...]
    all_to_all x1, blocking collectives: 14.5 us -> 18.1 us  [body(): out = lax.all_to_all(out, MEMBERS, 0, 0, tiled=True)]
    all_to_all x2, blocking collectives: 26.2 us -> 23.6 us  [sum_parts(): return lax.all_to_all(copies, 'z', 0, 0, tiled=True)]
  transfers between devices with their start and end apart: 9 -> 10, of which waited for: 3 -> 4; matrix products, arithmetic and copies ran while one was open for 0% -> 0% of each run, Pallas kernels for 3% -> 4%
where the time goes in v6:
time: 113 us
  blocking collectives  53.7 us (48%)
  starting transfers between devices  22.8 us (20%)
  Pallas kernels  16.3 us (14%)
  waiting for transfers between devices  15.8 us (14%)
  between operations  2.69 us (2%)
  other arithmetic  1.17 us (1%)
    all_to_all x2, blocking collectives, sum_parts(): return lax.all_to_all(copies, 'z', 0, 0, tiled=True)  23.6 us
    all_to_all x1, blocking collectives, body(): out = lax.all_to_all(out, MEMBERS, 0, 0, tiled=True)  18.1 us
    all_to_all x1, blocking collectives, exchange(): lax.all_to_all(blocks, MEMBERS, 0, 0, axis_index_groups=lines(first), til...  12 us
    all_to_all x1, starting transfers between devices, body(): parts = lax.all_to_all(parts, ('z', 'core'), 0, 0, tiled=True)  11.3 us
    all_to_all x1, waiting for transfers between devices, body(): parts = lax.all_to_all(parts, ('z', 'core'), 0, 0, tiled=True)  7.82 us
    all_to_all x1, waiting for transfers between devices, exchange(): lax.all_to_all(blocks, MEMBERS, 0, 0, axis_index_groups=lines(first), til...  6.53 us
    pallas_call x1, Pallas kernels, body(): call(rhs_kernel, (shape((total // 2, rows), jnp.bfloat16), copies, state)...  4.35 us
    ppermute x5, starting transfers between devices, swap(): return lax.ppermute(value, 'core', [(0, 1), (1, 0)])  4.03 us
  transfers between devices with their start and end apart: 10, of which 4 were waited for; matrix products, arithmetic and copies ran while one was open for 0% of the time, Pallas kernels for 4%

profile of v6, /device:TPU:1, one launch (start us, length us, event | category | flops | bytes accessed | tf_op | source)
XLA Modules:
  0.0 112.5 jit_solution(2545720077746992602)
XLA Ops:
  0.6 1.0 broadcast_select_fusion.1
  1.7 3.3 %collective-permute-start = (bf16[72,1024]{1,0:T(8,128)(2,1)S(1)}, bf16[72,1024]{1,0:T(8,128)(2,1)S(1)}, u32[]{:S(2)}, u32[]{:S(2)}) collective-permute-start(bf16[72,1024]{1,0:T(8,128)(2,1)S(1)} %get-tuple-element.43), channel_id=1, source_target_pairs={{0,1},{1,0},{2,3},{3,2},{4,5},{5,4},{6,7},{7,6},{8,9},{9,8},{10,11... | collective-permute-start | bytes 442376 | tf_op jit(solution)/shard_map/ppermute | solution.py:58
  5.0 0.1 pad_add_fusion.place_ref
  5.1 0.9 collective-permute-done.got_ref
  6.1 0.8 shard_map.95
  6.9 12.0 %all_to_all.30.packed_ref = bf16[4,160,768]{2,1,0:T(8,128)(2,1)S(1)} all-to-all(bf16[4,160,768]{2,1,0:T(8,128)(2,1)S(1)} %shard_map.95), channel_id=1, replica_groups={{0,4,8,12},{128,132,136,140},{2,6,10,14},{130,134,138,142},{1,129,3,131..., dimensions={0} | all-to-all | bytes 1966080 | tf_op jit(solution)/shard_map/all_to_all | solution.py:50
  18.9 0.1 slice.14.near_ref.refs_0_
  18.9 0.0 copy-start
  18.9 0.9 collective-permute-start.1
  19.8 1.0 shard_map.96
  20.8 3.9 %all-to-all-start.1 = ((f32[4,16,768]{2,1,0:T(8,128)}), f32[4,16,768]{2,1,0:T(8,128)S(1)}, u32[]{:S(2)}, u32[]{:S(2)}) async-start(f32[4,16,768]{2,1,0:T(8,128)} %shard_map.96), calls=%async_computation.1 | async-start | bytes 393216 | tf_op jit(solution)/shard_map/all_to_all | solution.py:50
  24.7 2.7 %collective-permute-start.3 = (bf16[4,144,768]{2,1,0:T(8,128)(2,1)S(1)}, bf16[4,144,768]{2,1,0:T(8,128)(2,1)S(1)}, u32[]{:S(2)}, u32[]{:S(2)}) collective-permute-start(bf16[4,144,768]{2,1,0:T(8,128)(2,1)S(1)} %slice.14.near_ref.refs_0_), channel_id=1, source_target_pairs={{0,130},{1,13},{4,134},{5,1},{8,138},{9,5},{12,142},{13,9},{128,0}... | collective-permute-start | bytes 2654216 | tf_op jit(solution)/shard_map/ppermute | solution.py:54
  27.4 6.5 %all-to-all-done.1.shares_ref = f32[4,16,768]{2,1,0:T(8,128)S(1)} async-done(((f32[4,16,768]{2,1,0:T(8,128)}), f32[4,16,768]{2,1,0:T(8,128)S(1)}, u32[]{:S(2)}, u32[]{:S(2)}) %all-to-all-start.1) | async-done | bytes 196640 | tf_op jit(solution)/shard_map/all_to_all | solution.py:50
  33.9 0.0 collective-permute-done.1._
  33.9 0.8 shard_map.97
  34.7 11.3 %all-to-all-start.2 = ((s16[16,8,896]{2,1,0:T(8,128)(2,1)}), s16[16,8,896]{2,1,0:T(8,128)(2,1)S(1)}, u32[]{:S(2)}, u32[]{:S(2)}) async-start(s16[16,8,896]{2,1,0:T(8,128)(2,1)} %get-tuple-element.23), calls=%async_computation.2 | async-start | bytes 458752 | tf_op jit(solution)/shard_map/all_to_all | solution.py:345
  48.0 0.6 shard_map.98
  48.6 0.2 collective-permute-start.4
  48.8 0.4 collective-permute-start.5
  49.2 0.0 collective-permute-done.3.refs_2_
  49.2 0.1 collective-permute-start.6
  49.3 7.8 %all-to-all-done.2.parts_ref = s16[16,8,896]{2,1,0:T(8,128)(2,1)S(1)} async-done(((s16[16,8,896]{2,1,0:T(8,128)(2,1)}), s16[16,8,896]{2,1,0:T(8,128)(2,1)S(1)}, u32[]{:S(2)}, u32[]{:S(2)}) %all-to-all-start.2) | async-done | bytes 229408 | tf_op jit(solution)/shard_map/all_to_all | solution.py:345
  57.1 0.0 collective-permute-done.5.refs_5_
  57.1 2.1 %shard_map.99 = (bf16[2304,768]{1,0:T(8,128)(2,1)S(1)}, bf16[1152,768]{1,0:T(8,128)(2,1)S(1)}) custom-call(s32[3]{0:T(128)S(1)} %pad_add_fusion.place_ref, bf16[4,144,768]{2,1,0:T(8,128)(2,1)S(1)} %slice.14.near_ref.refs_0_, bf16[4,144,768]{2,1,0:T(8,128)(2,1)S(1)} %get-tuple-element.24.refs_1_, bf16[4,144,768]{2,1,0:T(8,128)(2,1)S(1)} %collective-permute-done.3.refs_2_, ...), custom_call_target="tpu_custom_call" | custom-call | tf_op jit(solution)/shard_map/pallas_call | solution.py:353
  59.2 0.5 collective-permute-done.7.refs_1_
  59.7 4.3 %shard_map.100 = (bf16[1152,768]{1,0:T(8,128)(2,1)S(1)}, s16[8,8,1664]{2,1,0:T(8,128)(2,1)S(1)}, f32[8,1536]{1,0:T(8,128)S(1)}) custom-call(s32[3]{0:T(128)S(1)} %pad_add_fusion.place_ref, f32[4,128]{1,0:T(4,128)S(1)} %get-tuple-element.30.coef_ref, f32[1,1536]{1,0:T(1,128)S(1)} %get-tuple-element.31.scale_ref, ...), custom_call_target="tpu_custom_call" | custom-call | tf_op jit(solution)/shard_map/pallas_call | solution.py:358
  64.1 12.2 %all_to_all.31.parts_ref = s16[8,8,1664]{2,1,0:T(8,128)(2,1)S(1)} all-to-all(s16[8,8,1664]{2,1,0:T(8,128)(2,1)S(1)} %get-tuple-element.36), channel_id=1, replica_groups=mesh['xl'=2,'z'=8,'y'=4,'xh'=2,'core'=2] {'z'}, dimensions={0} | all-to-all | bytes 425984 | tf_op jit(solution)/shard_map/all_to_all | solution.py:287
  76.3 3.2 %shard_map.101 = (s16[8,8,1664]{2,1,0:T(8,128)(2,1)S(1)}, f32[8,1536]{1,0:T(8,128)S(1)}, f32[8,1536]{1,0:T(8,128)S(1)}) custom-call(f32[4,128]{1,0:T(4,128)S(1)} %get-tuple-element.30.coef_ref, f32[1,1536]{1,0:T(1,128)S(1)} %get-tuple-element.31.scale_ref, s16[8,8,1664]{2,1,0:T(8,128)(2,1)S(1)} %all_to_all.31.parts_ref, ...), custom_call_target="tpu_custom_call" | custom-call | tf_op jit(solution)/shard_map/pallas_call | solution.py:365
  79.5 11.4 %all_to_all.32.parts_ref = s16[8,8,1664]{2,1,0:T(8,128)(2,1)S(1)} all-to-all(s16[8,8,1664]{2,1,0:T(8,128)(2,1)S(1)} %get-tuple-element.39), channel_id=1, replica_groups=mesh['xl'=2,'z'=8,'y'=4,'xh'=2,'core'=2] {'z'}, dimensions={0} | all-to-all | bytes 425984 | tf_op jit(solution)/shard_map/all_to_all | solution.py:287
  90.9 2.8 %shard_map.102 = f32[32,16,72]{2,1,0:T(8,128)S(1)} custom-call(s32[3]{0:T(128)S(1)} %pad_add_fusion.place_ref, f32[4,128]{1,0:T(4,128)S(1)} %get-tuple-element.30.coef_ref, f32[1,1536]{1,0:T(1,128)S(1)} %get-tuple-element.31.scale_ref, s16[8,8,1664]{2,1,0:T(8,128)(2,1)S(1)} %all_to_all.32.parts_ref, bf16[2304,768]{1,0:T(8,128)(2,1)S(1)} %get-tuple-element.34.own_ref.refs_0_, ...), custom_call_target="tpu_custom_call" | custom-call | tf_op jit(solution)/shard_map/pallas_call | solution.py:369
  93.7 18.1 %all_to_all.33.blocks_ref = f32[32,16,72]{2,1,0:T(8,128)S(1)} all-to-all(f32[32,16,72]{2,1,0:T(8,128)S(1)} %shard_map.102), channel_id=1, replica_groups=mesh['xl'=2,'z'=8,'y'=4,'xh'=2,'core'=2] {'xl','y','xh','core'}, dimensions={0} | all-to-all | bytes 294912 | tf_op jit(solution)/shard_map/all_to_all | solution.py:375
  111.8 0.8 shard_map.103
  (9 shorter events, 0.1 us)
Async XLA Ops:
  1.7 4.3 %collective-permute-start = (bf16[72,1024]{1,0:T(8,128)(2,1)S(1)}, bf16[72,1024]{1,0:T(8,128)(2,1)S(1)}, u32[]{:S(2)}, u32[]{:S(2)}) collective-permute-start(bf16[72,1024]{1,0:T(8,128)(2,1)S(1)} %get-tuple-element.43), channel_id=1, source_target_pairs={{0,1},{1,0},{2,3},{3,2},{4,5},{5,4},{6,7},{7,6},{8,9},{9,8},{10,11... | collective-permute-start | bytes 442376 | tf_op jit(solution)/shard_map/ppermute | solution.py:58
  18.9 29.1 %copy-start = (s32[2]{0:T(128)S(1)}, s32[2]{0:T(128)}, u32[]{:S(2)}) copy-start(s32[2]{0:T(128)} %counts_ref.1) | copy-start | bytes 28
  18.9 15.0 %collective-permute-start.1 = (bf16[4,144,768]{2,1,0:T(8,128)(2,1)S(1)}, bf16[4,144,768]{2,1,0:T(8,128)(2,1)S(1)}, u32[]{:S(2)}, u32[]{:S(2)}) collective-permute-start(bf16[4,144,768]{2,1,0:T(8,128)(2,1)S(1)} %slice.14.near_ref.refs_0_), channel_id=1, source_target_pairs={{0,128},{1,5},{4,132},{5,9},{8,136},{9,13},{12,140},{13,1},{128,2}... | collective-permute-start | bytes 2654216 | tf_op jit(solution)/shard_map/ppermute | solution.py:54
  20.8 13.1 %all-to-all-start.1 = ((f32[4,16,768]{2,1,0:T(8,128)}), f32[4,16,768]{2,1,0:T(8,128)S(1)}, u32[]{:S(2)}, u32[]{:S(2)}) async-start(f32[4,16,768]{2,1,0:T(8,128)} %shard_map.96), calls=%async_computation.1 | async-start | bytes 393216 | tf_op jit(solution)/shard_map/all_to_all | solution.py:50
  24.7 24.5 %collective-permute-start.3 = (bf16[4,144,768]{2,1,0:T(8,128)(2,1)S(1)}, bf16[4,144,768]{2,1,0:T(8,128)(2,1)S(1)}, u32[]{:S(2)}, u32[]{:S(2)}) collective-permute-start(bf16[4,144,768]{2,1,0:T(8,128)(2,1)S(1)} %slice.14.near_ref.refs_0_), channel_id=1, source_target_pairs={{0,130},{1,13},{4,134},{5,1},{8,138},{9,5},{12,142},{13,9},{128,0}... | collective-permute-start | bytes 2654216 | tf_op jit(solution)/shard_map/ppermute | solution.py:54
  34.7 22.4 %collective-permute-start.2 = (bf16[4,144,768]{2,1,0:T(8,128)(2,1)S(1)}, bf16[4,144,768]{2,1,0:T(8,128)(2,1)}, u32[]{:S(2)}, u32[]{:S(2)}) collective-permute-start(bf16[4,144,768]{2,1,0:T(8,128)(2,1)S(1)} %get-tuple-element.24.refs_1_), channel_id=1, source_target_pairs={{0,128},{1,5},{4,132},{5,9},{8,136},{9,13},{12,140},{13,1},{128,2}... | collective-permute-start | bytes 2654216 | tf_op jit(solution)/shard_map/ppermute | solution.py:54
  34.7 22.4 %all-to-all-start.2 = ((s16[16,8,896]{2,1,0:T(8,128)(2,1)}), s16[16,8,896]{2,1,0:T(8,128)(2,1)S(1)}, u32[]{:S(2)}, u32[]{:S(2)}) async-start(s16[16,8,896]{2,1,0:T(8,128)(2,1)} %get-tuple-element.23), calls=%async_computation.2 | async-start | bytes 458752 | tf_op jit(solution)/shard_map/all_to_all | solution.py:345
  48.6 8.5 %collective-permute-start.4 = (bf16[4,144,768]{2,1,0:T(8,128)(2,1)S(1)}, bf16[4,144,768]{2,1,0:T(8,128)(2,1)}, u32[]{:S(2)}, u32[]{:S(2)}) collective-permute-start(bf16[4,144,768]{2,1,0:T(8,128)(2,1)S(1)} %slice.14.near_ref.refs_0_), channel_id=1, source_target_pairs={{0,1},{1,0},{2,3},{3,2},{4,5},{5,4},{6,7},{7,6},{8,9},{9,8},{10,11... | collective-permute-start | bytes 2654216 | tf_op jit(solution)/shard_map/ppermute | solution.py:58
  48.8 8.4 %collective-permute-start.5 = (bf16[4,144,768]{2,1,0:T(8,128)(2,1)S(1)}, bf16[4,144,768]{2,1,0:T(8,128)(2,1)}, u32[]{:S(2)}, u32[]{:S(2)}) collective-permute-start(bf16[4,144,768]{2,1,0:T(8,128)(2,1)S(1)} %get-tuple-element.24.refs_1_), channel_id=1, source_target_pairs={{0,1},{1,0},{2,3},{3,2},{4,5},{5,4},{6,7},{7,6},{8,9},{9,8},{10,11... | collective-permute-start | bytes 2654216 | tf_op jit(solution)/shard_map/ppermute | solution.py:58
  49.2 10.0 %collective-permute-start.6 = (bf16[4,144,768]{2,1,0:T(8,128)(2,1)S(1)}, bf16[4,144,768]{2,1,0:T(8,128)(2,1)}, u32[]{:S(2)}, u32[]{:S(2)}) collective-permute-start(bf16[4,144,768]{2,1,0:T(8,128)(2,1)S(1)} %collective-permute-done.3.refs_2_), channel_id=1, source_target_pairs={{0,1},{1,0},{2,3},{3,2},{4,5},{5,4},{6,7},{7,6},{8,9},{9,8},{10,11... | collective-permute-start | bytes 2654216 | tf_op jit(solution)/shard_map/ppermute | solution.py:58
  57.1 2.6 %collective-permute-start.7 = (bf16[4,144,768]{2,1,0:T(8,128)(2,1)}, bf16[4,144,768]{2,1,0:T(8,128)(2,1)S(1)}, u32[]{:S(2)}, u32[]{:S(2)}) collective-permute-start(bf16[4,144,768]{2,1,0:T(8,128)(2,1)} %collective-permute-done.2.refs_3_), channel_id=1, source_target_pairs={{0,1},{1,0},{2,3},{3,2},{4,5},{5,4},{6,7},{7,6},{8,9},{9,8},{10,11... | collective-permute-start | bytes 2654216 | tf_op jit(solution)/shard_map/ppermute | solution.py:58

commit v7 on v6

--- a/solution.py
+++ b/solution.py
@@ -163,17 +163,25 @@
         out_ref[k] = coded[k % 2]
 
 
-def lay_kernel(place_ref, *refs):
-    mine, theirs = refs[:SIDE], refs[SIDE : SIDE + 2]
-    own_ref, other_ref = refs[SIDE + 2 :]
-    deep = mine[0].shape[1]
-    line, _ = line_place(place_ref)
-    for inner in range(SIDE):
-        here = lax.rem(line + SIDE - ORDER[inner], SIDE)
+def lay_kernel(place_ref, near_ref, back_ref, other_ref, sems):
+    deep = near_ref.shape[1]
+    _, across = line_place(place_ref)
+    copies = []
+    for inner, source_ref in enumerate((near_ref, back_ref)):
         for outer in range(SIDE):
-            at = (inner * SIDE + outer) * deep
-            own_ref[at : at + deep] = mine[outer][here]
-    lay_others(place_ref, theirs, other_ref)
+            there = lax.rem(across + SIDE - ORDER[outer], SIDE)
+            spot = inner * SIDE + outer
+            copies.append(
+                pltpu.make_async_copy(
+                    source_ref.at[there],
+                    other_ref.at[pl.ds(spot * deep, deep)],
+                    sems.at[spot],
+                )
+            )
+    for copy in copies:
+        copy.start()
+    for copy in copies:
+        copy.wait()
 
 
 def coef_kernel(place_ref, counts_ref, low_ref, high_ref, ridge_ref, scale_ref, coef_ref):
@@ -207,34 +215,53 @@
             other_ref[at : at + deep] = theirs[inner][there]
 
 
-def rhs_kernel(place_ref, coef_ref, scale_ref, parts_ref, own_ref, first_ref, *refs):
-    theirs, (second_ref, out_ref, rhs_ref) = refs[:2], refs[2:]
+def rhs_kernel(place_ref, coef_ref, scale_ref, parts_ref, *refs):
+    mine, (own_ref, rhs_ref, inner_ref) = refs[:SIDE], refs[SIDE:]
     core = place_ref[2]
-    rows = own_ref.shape[1]
-    lay_others(place_ref, theirs, second_ref)
+    deep, rows = mine[0].shape[1:]
+    line, _ = line_place(place_ref)
+    for inner in range(SIDE):
+        here = lax.rem(line + SIDE - ORDER[inner], SIDE)
+        for outer in range(SIDE):
+            at = (inner * SIDE + outer) * deep
+            own_ref[at : at + deep] = mine[outer][here]
     half = parts_ref.shape[0] // 2
     for at, side in ((core, 0), (1 - core, 1)):
         total = sum_coded(parts_ref, [2 * k + at for k in range(half)])
         rhs_ref[:, side * rows : (side + 1) * rows] = total
-    ahead(rhs_ref[...] / coef_ref[0:1, 0:1], scale_ref, (own_ref, first_ref, second_ref), out_ref)
+    first = rhs_ref[:, :rows] / coef_ref[0:1, 0:1] * scale_ref[:, :rows]
+    inner_ref[...] = times(first, own_ref[...], NT)
+
+
+def first_kernel(place_ref, coef_ref, scale_ref, rhs_ref, inner_ref, own_ref, first_ref, *refs):
+    theirs, (second_ref, out_ref) = refs[:2], refs[2:]
+    lay_others(place_ref, theirs, second_ref)
+    rows = own_ref.shape[1]
+    feats = (own_ref, first_ref, second_ref)
+    value = rhs_ref[:, rows:] / coef_ref[0:1, 0:1] * scale_ref[:, rows:]
+    from_features(inner_ref[...] + others_to_features(value, feats), feats, out_ref)
+
+
+def others_to_features(value, feats):
+    return jnp.concatenate([times(value, f[...], NT) for f in feats[1:]], axis=1)
 
 
 def to_features(value, feats):
-    own, first, second = (f[...] for f in feats)
-    rows = own.shape[1]
-    other = jnp.concatenate(
-        [times(value[:, rows:], first, NT), times(value[:, rows:], second, NT)], axis=1
-    )
-    return times(value[:, :rows], own, NT) + other
-
-
-def ahead(direction, scale_ref, feats, out_ref):
+    rows = feats[0].shape[1]
+    own = times(value[:, :rows], feats[0][...], NT)
+    return own + others_to_features(value[:, rows:], feats)
+
+
+def from_features(inner, feats, out_ref):
     own, first, second = (f[...] for f in feats)
     half = first.shape[0]
-    inner = to_features(direction * scale_ref[...], feats)
     left = times(inner, own, NN)
     right = times(inner[:, :half], first, NN) + times(inner[:, half:], second, NN)
     send_all(jnp.concatenate([left, right], axis=1), out_ref)
+
+
+def ahead(direction, scale_ref, feats, out_ref):
+    from_features(to_features(direction * scale_ref[...], feats), feats, out_ref)
 
 
 def step_kernel(coef_ref, scale_ref, parts_ref, *refs):
@@ -343,23 +370,29 @@
         coef_kernel, (shape((1, 2 * rows), f32), shape((4, 128), f32)), [SMEM] * 5
     )(place, counts, eig_low, eig_high, damping)
     parts = lax.all_to_all(parts, ("z", "core"), 0, 0, tiled=True)
-    parts, far, scale, coef = lax.optimization_barrier((parts, far, scale, coef))
-    pieces = [near, back, front, far]
-    swapped = [swap(p) for p in pieces]
-
     total = members * width
+    near_swapped, back_swapped = swap(near), swap(back)
+    first = pl.pallas_call(
+        lay_kernel,
+        out_shape=shape((total // 2, rows), jnp.bfloat16),
+        in_specs=[SMEM, anywhere, anywhere],
+        out_specs=VMEM,
+        scratch_shapes=[pltpu.SemaphoreType.DMA((2 * SIDE,))],
+    )(place, near_swapped, back_swapped)
+    parts, far, scale, coef, first = lax.optimization_barrier((parts, far, scale, coef, first))
+    others = swap(front), swap(far)
     copies = shape((depth, cols, 2 * rows + TILE), jnp.int16)
     state = shape((cols, 2 * rows), f32)
-    own, first = call(
-        lay_kernel,
-        (shape((total, rows), jnp.bfloat16), shape((total // 2, rows), jnp.bfloat16)),
-        [SMEM] + [VMEM] * (SIDE + 2),
-    )(place, *pieces, *swapped[:2])
-    second, parts, rhs = call(
+    own, rhs, inner = call(
         rhs_kernel,
-        (shape((total // 2, rows), jnp.bfloat16), copies, state),
+        (shape((total, rows), jnp.bfloat16), state, shape((cols, total), f32)),
         [SMEM] + [VMEM] * 7,
-    )(place, coef, scale, parts, own, first, *swapped[2:])
+    )(place, coef, scale, parts, near, back, front, far)
+    second, parts = call(
+        first_kernel,
+        (shape((total // 2, rows), jnp.bfloat16), copies),
+        [SMEM] + [VMEM] * 8,
+    )(place, coef, scale, rhs, inner, own, first, *others)
     feats = (own, first, second)
     parts = sum_parts(parts)
     parts, direction, residual = call(step_kernel, (copies, state, state), [VMEM] * 7)(

time: 113 us -> 111 us (0.982)
  waiting for transfers between devices: 15.8 us -> 11.8 us
  Pallas kernels: 16.3 us -> 18.5 us
    ppermute x5, starting transfers between devices: 4.03 us -> 8.64 us  [swap(): return lax.ppermute(value, 'core', [(0, 1), (1, 0)])]
    all_to_all x1, waiting for transfers between devices: 7.82 us -> 4.78 us  [body(): parts = lax.all_to_all(parts, ('z', 'core'), 0, 0, tiled=True)]
    all_to_all x1, blocking collectives: 18.1 us -> 15.3 us  [body(): out = lax.all_to_all(out, MEMBERS, 0, 0, tiled=True)]
    all_to_all x1, starting transfers between devices: 11.3 us -> 8.59 us  [body(): parts = lax.all_to_all(parts, ('z', 'core'), 0, 0, tiled=True)]
    pallas_call x2 -> x3, Pallas kernels: 6.41 us -> 8.8 us  [the longest x1 3.52 us: body(): pl.pallas_call(lay_kernel, out_shape=shape((total // 2, rows), jnp.bfloat...]
    all_to_all x2, blocking collectives: 23.6 us -> 25.8 us  [sum_parts(): return lax.all_to_all(copies, 'z', 0, 0, tiled=True)]
    ppermute x3, starting transfers between devices: 3.53 us -> 2.03 us  [along(): return lax.ppermute(value, MEMBERS, ring_pairs(shift))]
  transfers between devices with their start and end apart: 10 -> 10, of which waited for: 4 -> 3; matrix products, arithmetic and copies ran while one was open for 0% -> 0% of each run, Pallas kernels for 4% -> 8%
where the time goes in v7:
time: 111 us; the launch traced here: 110 us
  blocking collectives  53.1 us (48%)
  starting transfers between devices  23.1 us (21%)
  Pallas kernels  18.5 us (17%)
  waiting for transfers between devices  11.8 us (11%)
  between operations  2.74 us (2%)
  other arithmetic  1.17 us (1%)
    all_to_all x2, blocking collectives, sum_parts(): return lax.all_to_all(copies, 'z', 0, 0, tiled=True)  25.8 us
    all_to_all x1, blocking collectives, body(): out = lax.all_to_all(out, MEMBERS, 0, 0, tiled=True)  15.3 us
    all_to_all x1, blocking collectives, exchange(): lax.all_to_all(blocks, MEMBERS, 0, 0, axis_index_groups=lines(first), til...  12 us
    ppermute x5, starting transfers between devices, swap(): return lax.ppermute(value, 'core', [(0, 1), (1, 0)])  8.64 us
    all_to_all x1, starting transfers between devices, body(): parts = lax.all_to_all(parts, ('z', 'core'), 0, 0, tiled=True)  8.59 us
    all_to_all x1, waiting for transfers between devices, exchange(): lax.all_to_all(blocks, MEMBERS, 0, 0, axis_index_groups=lines(first), til...  6.07 us
    all_to_all x1, waiting for transfers between devices, body(): parts = lax.all_to_all(parts, ('z', 'core'), 0, 0, tiled=True)  4.78 us
    all_to_all x1, starting transfers between devices, exchange(): lax.all_to_all(blocks, MEMBERS, 0, 0, axis_index_groups=lines(first), til...  3.89 us
  transfers between devices with their start and end apart: 10, of which 3 were waited for; matrix products, arithmetic and copies ran while one was open for 0% of the time, Pallas kernels for 8%

profile of v7, /device:TPU:1, one launch (start us, length us, event | category | flops | bytes accessed | tf_op | source)
XLA Modules:
  0.0 110.5 jit_solution(6499885796260689911)
XLA Ops:
  0.6 1.0 broadcast_select_fusion.1
  1.7 3.3 %collective-permute-start = (bf16[72,1024]{1,0:T(8,128)(2,1)S(1)}, bf16[72,1024]{1,0:T(8,128)(2,1)S(1)}, u32[]{:S(2)}, u32[]{:S(2)}) collective-permute-start(bf16[72,1024]{1,0:T(8,128)(2,1)S(1)} %get-tuple-element.45), channel_id=1, source_target_pairs={{0,1},{1,0},{2,3},{3,2},{4,5},{5,4},{6,7},{7,6},{8,9},{9,8},{10,11... | collective-permute-start | bytes 442376 | tf_op jit(solution)/shard_map/ppermute | solution.py:58
  5.0 0.1 pad_add_fusion.place_ref
  5.1 0.9 collective-permute-done.got_ref
  6.1 0.8 shard_map.95
  6.9 12.0 %all_to_all.30.packed_ref = bf16[4,160,768]{2,1,0:T(8,128)(2,1)S(1)} all-to-all(bf16[4,160,768]{2,1,0:T(8,128)(2,1)S(1)} %shard_map.95), channel_id=1, replica_groups={{0,4,8,12},{128,132,136,140},{2,6,10,14},{130,134,138,142},{1,129,3,131..., dimensions={0} | all-to-all | bytes 1966080 | tf_op jit(solution)/shard_map/all_to_all | solution.py:50
  18.9 0.1 slice.14.near_ref.refs_0_
  18.9 0.0 copy-start.3
  18.9 0.9 collective-permute-start.1
  19.8 1.0 shard_map.96
  20.8 3.9 %all-to-all-start.1 = ((f32[4,16,768]{2,1,0:T(8,128)}), f32[4,16,768]{2,1,0:T(8,128)S(1)}, u32[]{:S(2)}, u32[]{:S(2)}) async-start(f32[4,16,768]{2,1,0:T(8,128)} %shard_map.96), calls=%async_computation.1 | async-start | bytes 393216 | tf_op jit(solution)/shard_map/all_to_all | solution.py:50
  24.7 2.3 %collective-permute-start.3 = (bf16[4,144,768]{2,1,0:T(8,128)(2,1)S(1)}, bf16[4,144,768]{2,1,0:T(8,128)(2,1)}, u32[]{:S(2)}, u32[]{:S(2)}) collective-permute-start(bf16[4,144,768]{2,1,0:T(8,128)(2,1)S(1)} %slice.14.near_ref.refs_0_), channel_id=1, source_target_pairs={{0,1},{1,0},{2,3},{3,2},{4,5},{5,4},{6,7},{7,6},{8,9},{9,8},{10,11... | collective-permute-start | bytes 2654216 | tf_op jit(solution)/shard_map/ppermute | solution.py:58
  26.9 0.9 collective-permute-start.5
  27.8 6.1 %all-to-all-done.1.shares_ref = f32[4,16,768]{2,1,0:T(8,128)S(1)} async-done(((f32[4,16,768]{2,1,0:T(8,128)}), f32[4,16,768]{2,1,0:T(8,128)S(1)}, u32[]{:S(2)}, u32[]{:S(2)}) %all-to-all-start.1) | async-done | bytes 196640 | tf_op jit(solution)/shard_map/all_to_all | solution.py:50
  33.9 0.8 shard_map.97
  34.7 2.9 %collective-permute-start.4 = (bf16[4,144,768]{2,1,0:T(8,128)(2,1)S(1)}, bf16[4,144,768]{2,1,0:T(8,128)(2,1)}, u32[]{:S(2)}, u32[]{:S(2)}) collective-permute-start(bf16[4,144,768]{2,1,0:T(8,128)(2,1)S(1)} %get-tuple-element.25.refs_1_), channel_id=1, source_target_pairs={{0,1},{1,0},{2,3},{3,2},{4,5},{5,4},{6,7},{7,6},{8,9},{9,8},{10,11... | collective-permute-start | bytes 2654216 | tf_op jit(solution)/shard_map/ppermute | solution.py:58
  37.6 0.3 collective-permute-start.2
  37.9 8.6 %all-to-all-start.2 = ((s16[16,8,896]{2,1,0:T(8,128)(2,1)}), s16[16,8,896]{2,1,0:T(8,128)(2,1)S(1)}, u32[]{:S(2)}, u32[]{:S(2)}) async-start(s16[16,8,896]{2,1,0:T(8,128)(2,1)} %get-tuple-element.24), calls=%async_computation.2 | async-start | bytes 458752 | tf_op jit(solution)/shard_map/all_to_all | solution.py:372
  48.4 0.6 shard_map.98
  49.0 0.0 copy-start.2
  49.0 0.2 collective-permute-start.6
  49.2 3.5 %shard_map.99.first_ref.refs_1_ = bf16[1152,768]{1,0:T(8,128)(2,1)} custom-call(s32[3]{0:T(128)} %copy-done.1, bf16[4,144,768]{2,1,0:T(8,128)(2,1)} %collective-permute-done.3.near_ref, bf16[4,144,768]{2,1,0:T(8,128)(2,1)} %collective-permute-done.4.back_ref), custom_call_target="tpu_custom_call" | custom-call | tf_op jit(solution)/shard_map/pallas_call | solution.py:375
  52.7 4.8 %all-to-all-done.2.parts_ref = s16[16,8,896]{2,1,0:T(8,128)(2,1)S(1)} async-done(((s16[16,8,896]{2,1,0:T(8,128)(2,1)}), s16[16,8,896]{2,1,0:T(8,128)(2,1)S(1)}, u32[]{:S(2)}, u32[]{:S(2)}) %all-to-all-start.2) | async-done | bytes 229408 | tf_op jit(solution)/shard_map/all_to_all | solution.py:372
  57.5 2.7 %shard_map.100 = (bf16[2304,768]{1,0:T(8,128)(2,1)S(1)}, f32[8,1536]{1,0:T(8,128)S(1)}, f32[8,2304]{1,0:T(8,128)S(1)}) custom-call(s32[3]{0:T(128)S(1)} %copy-done.2, f32[4,128]{1,0:T(4,128)S(1)} %get-tuple-element.31.coef_ref, f32[1,1536]{1,0:T(1,128)S(1)} %get-tuple-element.32.scale_ref, s16[16,8,896]{2,1,0:T(8,128)(2,1)S(1)} %all-to-all-done.2.parts_ref, ...), custom_call_target="tpu_custom_call" | custom-call | tf_op jit(solution)/shard_map/pallas_call | solution.py:386
  60.2 0.0 collective-permute-done.7.refs_1_
  60.2 2.6 %shard_map.101 = (bf16[1152,768]{1,0:T(8,128)(2,1)S(1)}, s16[8,8,1664]{2,1,0:T(8,128)(2,1)S(1)}) custom-call(s32[3]{0:T(128)S(1)} %copy-done.2, f32[4,128]{1,0:T(4,128)S(1)} %get-tuple-element.31.coef_ref, f32[1,1536]{1,0:T(1,128)S(1)} %get-tuple-element.32.scale_ref, f32[8,1536]{1,0:T(8,128)S(1)} %get-tuple-element.35.rhs_ref.refs_3_, ...), custom_call_target="tpu_custom_call" | custom-call | tf_op jit(solution)/shard_map/pallas_call | solution.py:391
  62.9 13.6 %all_to_all.31.parts_ref = s16[8,8,1664]{2,1,0:T(8,128)(2,1)S(1)} all-to-all(s16[8,8,1664]{2,1,0:T(8,128)(2,1)S(1)} %get-tuple-element.39), channel_id=1, replica_groups=mesh['xl'=2,'z'=8,'y'=4,'xh'=2,'core'=2] {'z'}, dimensions={0} | all-to-all | bytes 425984 | tf_op jit(solution)/shard_map/all_to_all | solution.py:314
  76.4 3.0 %shard_map.102 = (s16[8,8,1664]{2,1,0:T(8,128)(2,1)S(1)}, f32[8,1536]{1,0:T(8,128)S(1)}, f32[8,1536]{1,0:T(8,128)S(1)}) custom-call(f32[4,128]{1,0:T(4,128)S(1)} %get-tuple-element.31.coef_ref, f32[1,1536]{1,0:T(1,128)S(1)} %get-tuple-element.32.scale_ref, s16[8,8,1664]{2,1,0:T(8,128)(2,1)S(1)} %all_to_all.31.parts_ref, ...), custom_call_target="tpu_custom_call" | custom-call | tf_op jit(solution)/shard_map/pallas_call | solution.py:398
  79.5 12.2 %all_to_all.32.parts_ref = s16[8,8,1664]{2,1,0:T(8,128)(2,1)S(1)} all-to-all(s16[8,8,1664]{2,1,0:T(8,128)(2,1)S(1)} %get-tuple-element.41), channel_id=1, replica_groups=mesh['xl'=2,'z'=8,'y'=4,'xh'=2,'core'=2] {'z'}, dimensions={0} | all-to-all | bytes 425984 | tf_op jit(solution)/shard_map/all_to_all | solution.py:314
  91.7 2.7 %shard_map.103 = f32[32,16,72]{2,1,0:T(8,128)S(1)} custom-call(s32[3]{0:T(128)S(1)} %copy-done.2, f32[4,128]{1,0:T(4,128)S(1)} %get-tuple-element.31.coef_ref, f32[1,1536]{1,0:T(1,128)S(1)} %get-tuple-element.32.scale_ref, s16[8,8,1664]{2,1,0:T(8,128)(2,1)S(1)} %all_to_all.32.parts_ref, bf16[2304,768]{1,0:T(8,128)(2,1)S(1)} %get-tuple-element.37.own_ref.refs_0_, ...), custom_call_target="tpu_custom_call" | custom-call | tf_op jit(solution)/shard_map/pallas_call | solution.py:402
  94.4 15.3 %all_to_all.33.blocks_ref = f32[32,16,72]{2,1,0:T(8,128)S(1)} all-to-all(f32[32,16,72]{2,1,0:T(8,128)S(1)} %shard_map.103), channel_id=1, replica_groups=mesh['xl'=2,'z'=8,'y'=4,'xh'=2,'core'=2] {'xl','y','xh','core'}, dimensions={0} | all-to-all | bytes 294912 | tf_op jit(solution)/shard_map/all_to_all | solution.py:408
  109.7 0.8 shard_map.104
  (16 shorter events, 0.1 us)
Async XLA Ops:
  1.7 4.3 %collective-permute-start = (bf16[72,1024]{1,0:T(8,128)(2,1)S(1)}, bf16[72,1024]{1,0:T(8,128)(2,1)S(1)}, u32[]{:S(2)}, u32[]{:S(2)}) collective-permute-start(bf16[72,1024]{1,0:T(8,128)(2,1)S(1)} %get-tuple-element.45), channel_id=1, source_target_pairs={{0,1},{1,0},{2,3},{3,2},{4,5},{5,4},{6,7},{7,6},{8,9},{9,8},{10,11... | collective-permute-start | bytes 442376 | tf_op jit(solution)/shard_map/ppermute | solution.py:58
  5.1 43.3 %copy-start.1 = (s32[3]{0:T(128)}, s32[3]{0:T(128)S(1)}, u32[]{:S(2)}) copy-start(s32[3]{0:T(128)S(1)} %pad_add_fusion.place_ref) | copy-start | bytes 40
  18.9 29.5 %copy-start.3 = (s32[2]{0:T(128)S(1)}, s32[2]{0:T(128)}, u32[]{:S(2)}) copy-start(s32[2]{0:T(128)} %counts_ref.1) | copy-start | bytes 28
  18.9 15.0 %collective-permute-start.1 = (bf16[4,144,768]{2,1,0:T(8,128)(2,1)S(1)}, bf16[4,144,768]{2,1,0:T(8,128)(2,1)S(1)}, u32[]{:S(2)}, u32[]{:S(2)}) collective-permute-start(bf16[4,144,768]{2,1,0:T(8,128)(2,1)S(1)} %slice.14.near_ref.refs_0_), channel_id=1, source_target_pairs={{0,128},{1,5},{4,132},{5,9},{8,136},{9,13},{12,140},{13,1},{128,2}... | collective-permute-start | bytes 2654216 | tf_op jit(solution)/shard_map/ppermute | solution.py:54
  20.8 13.1 %all-to-all-start.1 = ((f32[4,16,768]{2,1,0:T(8,128)}), f32[4,16,768]{2,1,0:T(8,128)S(1)}, u32[]{:S(2)}, u32[]{:S(2)}) async-start(f32[4,16,768]{2,1,0:T(8,128)} %shard_map.96), calls=%async_computation.1 | async-start | bytes 393216 | tf_op jit(solution)/shard_map/all_to_all | solution.py:50
  24.7 24.5 %collective-permute-start.3 = (bf16[4,144,768]{2,1,0:T(8,128)(2,1)S(1)}, bf16[4,144,768]{2,1,0:T(8,128)(2,1)}, u32[]{:S(2)}, u32[]{:S(2)}) collective-permute-start(bf16[4,144,768]{2,1,0:T(8,128)(2,1)S(1)} %slice.14.near_ref.refs_0_), channel_id=1, source_target_pairs={{0,1},{1,0},{2,3},{3,2},{4,5},{5,4},{6,7},{7,6},{8,9},{9,8},{10,11... | collective-permute-start | bytes 2654216 | tf_op jit(solution)/shard_map/ppermute | solution.py:58
  26.9 22.1 %collective-permute-start.5 = (bf16[4,144,768]{2,1,0:T(8,128)(2,1)S(1)}, bf16[4,144,768]{2,1,0:T(8,128)(2,1)}, u32[]{:S(2)}, u32[]{:S(2)}) collective-permute-start(bf16[4,144,768]{2,1,0:T(8,128)(2,1)S(1)} %slice.14.near_ref.refs_0_), channel_id=1, source_target_pairs={{0,130},{1,13},{4,134},{5,1},{8,138},{9,5},{12,142},{13,9},{128,0}... | collective-permute-start | bytes 2654216 | tf_op jit(solution)/shard_map/ppermute | solution.py:54
  34.7 14.5 %collective-permute-start.4 = (bf16[4,144,768]{2,1,0:T(8,128)(2,1)S(1)}, bf16[4,144,768]{2,1,0:T(8,128)(2,1)}, u32[]{:S(2)}, u32[]{:S(2)}) collective-permute-start(bf16[4,144,768]{2,1,0:T(8,128)(2,1)S(1)} %get-tuple-element.25.refs_1_), channel_id=1, source_target_pairs={{0,1},{1,0},{2,3},{3,2},{4,5},{5,4},{6,7},{7,6},{8,9},{9,8},{10,11... | collective-permute-start | bytes 2654216 | tf_op jit(solution)/shard_map/ppermute | solution.py:58
  37.6 19.9 %collective-permute-start.2 = (bf16[4,144,768]{2,1,0:T(8,128)(2,1)S(1)}, bf16[4,144,768]{2,1,0:T(8,128)(2,1)}, u32[]{:S(2)}, u32[]{:S(2)}) collective-permute-start(bf16[4,144,768]{2,1,0:T(8,128)(2,1)S(1)} %get-tuple-element.25.refs_1_), channel_id=1, source_target_pairs={{0,128},{1,5},{4,132},{5,9},{8,136},{9,13},{12,140},{13,1},{128,2}... | collective-permute-start | bytes 2654216 | tf_op jit(solution)/shard_map/ppermute | solution.py:54
  37.9 19.6 %all-to-all-start.2 = ((s16[16,8,896]{2,1,0:T(8,128)(2,1)}), s16[16,8,896]{2,1,0:T(8,128)(2,1)S(1)}, u32[]{:S(2)}, u32[]{:S(2)}) async-start(s16[16,8,896]{2,1,0:T(8,128)(2,1)} %get-tuple-element.24), calls=%async_computation.2 | async-start | bytes 458752 | tf_op jit(solution)/shard_map/all_to_all | solution.py:372
  49.0 8.5 %copy-start.2 = (s32[3]{0:T(128)S(1)}, s32[3]{0:T(128)}, u32[]{:S(2)}) copy-start(s32[3]{0:T(128)} %copy-done.1) | copy-start | bytes 40
  49.0 11.2 %collective-permute-start.6 = (bf16[4,144,768]{2,1,0:T(8,128)(2,1)}, bf16[4,144,768]{2,1,0:T(8,128)(2,1)S(1)}, u32[]{:S(2)}, u32[]{:S(2)}) collective-permute-start(bf16[4,144,768]{2,1,0:T(8,128)(2,1)} %collective-permute-done.5.refs_2_), channel_id=1, source_target_pairs={{0,1},{1,0},{2,3},{3,2},{4,5},{5,4},{6,7},{7,6},{8,9},{9,8},{10,11... | collective-permute-start | bytes 2654216 | tf_op jit(solution)/shard_map/ppermute | solution.py:58
  57.5 2.7 %copy-start = (bf16[1152,768]{1,0:T(8,128)(2,1)S(1)}, bf16[1152,768]{1,0:T(8,128)(2,1)}, u32[]{:S(2)}) copy-start(bf16[1152,768]{1,0:T(8,128)(2,1)} %shard_map.99.first_ref.refs_1_) | copy-start | bytes 5308420
  57.5 2.7 %collective-permute-start.7 = (bf16[4,144,768]{2,1,0:T(8,128)(2,1)}, bf16[4,144,768]{2,1,0:T(8,128)(2,1)S(1)}, u32[]{:S(2)}, u32[]{:S(2)}) collective-permute-start(bf16[4,144,768]{2,1,0:T(8,128)(2,1)} %collective-permute-done.2.refs_3_), channel_id=1, source_target_pairs={{0,1},{1,0},{2,3},{3,2},{4,5},{5,4},{6,7},{7,6},{8,9},{9,8},{10,11... | collective-permute-start | bytes 2654216 | tf_op jit(solution)/shard_map/ppermute | solution.py:58

commit v8 on v7

--- a/solution.py
+++ b/solution.py
@@ -155,7 +155,7 @@
         out_ref[across] = out[across * each : (across + 1) * each]
 
 
-def plane_kernel(shares_ref, _, out_ref, __):
+def plane_kernel(shares_ref, _, __, out_ref, *unused):
     total = jnp.sum(shares_ref[...], axis=0)
     cols = out_ref.shape[1]
     coded = [code(total[k * cols : (k + 1) * cols]) for k in range(2)]
@@ -328,7 +328,13 @@
     lead = core == 0
     first = jnp.concatenate([x_first.T, w_first], axis=1)
     second = jnp.concatenate([x_second.T, w_second], axis=1)
-    kept, give = jnp.where(lead, first, second), jnp.where(lead, second, first)
+    give = jnp.where(lead, second, first)
+    give, *own_args = lax.optimization_barrier((give, x_first, x_second, w_first, w_second))
+    kept = jnp.where(
+        lead,
+        jnp.concatenate([own_args[0].T, own_args[2]], axis=1),
+        jnp.concatenate([own_args[1].T, own_args[3]], axis=1),
+    )
     got_all = swap(give)
     mine, got = kept[:, :rows], got_all[:, :rows]
     block = jnp.where(
@@ -349,6 +355,12 @@
         [VMEM] * 2,
         [pltpu.VMEM((SIDE * 2 * cols, SIDE * block.shape[0]), f32)],
     )(packed, near)
+    shares, eig_low, eig_high, damping = lax.optimization_barrier(
+        (shares, eig_low, eig_high, damping)
+    )
+    scale, coef = call(
+        coef_kernel, (shape((1, 2 * rows), f32), shape((4, 128), f32)), [SMEM] * 5
+    )(place, counts, eig_low, eig_high, damping)
     shares = exchange(shares, False)
     anywhere = pl.BlockSpec(memory_space=pl.ANY)
     parts, back = pl.pallas_call(
@@ -357,18 +369,12 @@
             shape((2 * depth, cols, rows + TILE), jnp.int16),
             shape(back.shape, back.dtype),
         ),
-        in_specs=[VMEM, anywhere],
+        in_specs=[VMEM, anywhere, anywhere],
         out_specs=(VMEM, anywhere),
         input_output_aliases={1: 1},
         compiler_params=pltpu.CompilerParams(vmem_limit_bytes=32 * 1024 * 1024),
-    )(shares, back)
+    )(shares, back, coef)
     far = along(back, 1)
-    parts, eig_low, eig_high, damping = lax.optimization_barrier(
-        (parts, eig_low, eig_high, damping)
-    )
-    scale, coef = call(
-        coef_kernel, (shape((1, 2 * rows), f32), shape((4, 128), f32)), [SMEM] * 5
-    )(place, counts, eig_low, eig_high, damping)
     parts = lax.all_to_all(parts, ("z", "core"), 0, 0, tiled=True)
     total = members * width
     near_swapped, back_swapped = swap(near), swap(back)

time: 111 us -> 111 us (level)
    all_to_all x1, waiting for transfers between devices: 4.78 us -> 7.3 us  [body(): parts = lax.all_to_all(parts, ('z', 'core'), 0, 0, tiled=True)]
    all_to_all x1, waiting for transfers between devices: 6.07 us -> 3.58 us  [exchange(): lax.all_to_all(blocks, MEMBERS, 0, 0, axis_index_groups=lines(first), til...]
  transfers between devices with their start and end apart: 10 -> 10, of which waited for: 3 -> 2; matrix products, arithmetic and copies ran while one was open for 0% -> 1% of each run, Pallas kernels for 8% -> 8%
where the time goes in v8:
time: 111 us; the launch traced here: 110 us
  blocking collectives  53 us (48%)
  starting transfers between devices  23.1 us (21%)
  Pallas kernels  18.5 us (17%)
  waiting for transfers between devices  10.9 us (10%)
  between operations  2.74 us (2%)
  other arithmetic  2.19 us (2%)
    all_to_all x2, blocking collectives, sum_parts(): return lax.all_to_all(copies, 'z', 0, 0, tiled=True)  25.8 us
    all_to_all x1, blocking collectives, body(): out = lax.all_to_all(out, MEMBERS, 0, 0, tiled=True)  15.3 us
    all_to_all x1, blocking collectives, exchange(): lax.all_to_all(blocks, MEMBERS, 0, 0, axis_index_groups=lines(first), til...  11.8 us
    all_to_all x1, starting transfers between devices, body(): parts = lax.all_to_all(parts, ('z', 'core'), 0, 0, tiled=True)  8.59 us
    ppermute x5, starting transfers between devices, swap(): return lax.ppermute(value, 'core', [(0, 1), (1, 0)])  8.46 us
    all_to_all x1, waiting for transfers between devices, body(): parts = lax.all_to_all(parts, ('z', 'core'), 0, 0, tiled=True)  7.3 us
    all_to_all x1, starting transfers between devices, exchange(): lax.all_to_all(blocks, MEMBERS, 0, 0, axis_index_groups=lines(first), til...  3.89 us
    all_to_all x1, waiting for transfers between devices, exchange(): lax.all_to_all(blocks, MEMBERS, 0, 0, axis_index_groups=lines(first), til...  3.58 us
  transfers between devices with their start and end apart: 10, of which 2 were waited for; matrix products, arithmetic and copies ran while one was open for 1% of the time, Pallas kernels for 8%

profile of v8, /device:TPU:1, one launch (start us, length us, event | category | flops | bytes accessed | tf_op | source)
XLA Modules:
  0.0 110.5 jit_solution(15606291104125558430)
XLA Ops:
  0.6 1.0 maximum_select_fusion.1
  1.7 3.3 %collective-permute-start = (bf16[72,1024]{1,0:T(8,128)(2,1)S(1)}, bf16[72,1024]{1,0:T(8,128)(2,1)S(1)}, u32[]{:S(2)}, u32[]{:S(2)}) collective-permute-start(bf16[72,1024]{1,0:T(8,128)(2,1)S(1)} %maximum_select_fusion.1), channel_id=1, source_target_pairs={{0,1},{1,0},{2,3},{3,2},{4,5},{5,4},{6,7},{7,6},{8,9},{9,8},{10,11... | collective-permute-start | bytes 442376 | tf_op jit(solution)/shard_map/ppermute | solution.py:58
  5.0 1.0 maximum_select_fusion.2.keep_ref
  6.1 0.1 pad_add_fusion.place_ref
  6.1 0.0 collective-permute-done.got_ref
  6.2 0.8 shard_map.95
  7.0 11.8 %all_to_all.30.packed_ref = bf16[4,160,768]{2,1,0:T(8,128)(2,1)S(1)} all-to-all(bf16[4,160,768]{2,1,0:T(8,128)(2,1)S(1)} %shard_map.95), channel_id=1, replica_groups={{0,4,8,12},{128,132,136,140},{2,6,10,14},{130,134,138,142},{1,129,3,131..., dimensions={0} | all-to-all | bytes 1966080 | tf_op jit(solution)/shard_map/all_to_all | solution.py:50
  18.9 0.1 slice.14.near_ref.refs_0_
  18.9 1.0 collective-permute-start.1
  19.9 1.0 shard_map.96
  20.9 3.9 %all-to-all-start.1 = ((f32[4,16,768]{2,1,0:T(8,128)}), f32[4,16,768]{2,1,0:T(8,128)S(1)}, u32[]{:S(2)}, u32[]{:S(2)}) async-start(f32[4,16,768]{2,1,0:T(8,128)} %shard_map.96), calls=%async_computation.1 | async-start | bytes 393216 | tf_op jit(solution)/shard_map/all_to_all | solution.py:50
  26.8 0.6 shard_map.97
  27.3 2.2 %collective-permute-start.3 = (bf16[4,144,768]{2,1,0:T(8,128)(2,1)S(1)}, bf16[4,144,768]{2,1,0:T(8,128)(2,1)}, u32[]{:S(2)}, u32[]{:S(2)}) collective-permute-start(bf16[4,144,768]{2,1,0:T(8,128)(2,1)S(1)} %slice.14.near_ref.refs_0_), channel_id=1, source_target_pairs={{0,1},{1,0},{2,3},{3,2},{4,5},{5,4},{6,7},{7,6},{8,9},{9,8},{10,11... | collective-permute-start | bytes 2654216 | tf_op jit(solution)/shard_map/ppermute | solution.py:58
  29.6 0.9 collective-permute-start.5
  30.4 3.6 %all-to-all-done.1.shares_ref = f32[4,16,768]{2,1,0:T(8,128)S(1)} async-done(((f32[4,16,768]{2,1,0:T(8,128)}), f32[4,16,768]{2,1,0:T(8,128)S(1)}, u32[]{:S(2)}, u32[]{:S(2)}) %all-to-all-start.1) | async-done | bytes 196640 | tf_op jit(solution)/shard_map/all_to_all | solution.py:50
  34.0 0.0 collective-permute-done.1._
  34.0 0.8 shard_map.98
  34.8 2.7 %collective-permute-start.4 = (bf16[4,144,768]{2,1,0:T(8,128)(2,1)S(1)}, bf16[4,144,768]{2,1,0:T(8,128)(2,1)}, u32[]{:S(2)}, u32[]{:S(2)}) collective-permute-start(bf16[4,144,768]{2,1,0:T(8,128)(2,1)S(1)} %get-tuple-element.39.refs_1_), channel_id=1, source_target_pairs={{0,1},{1,0},{2,3},{3,2},{4,5},{5,4},{6,7},{7,6},{8,9},{9,8},{10,11... | collective-permute-start | bytes 2654216 | tf_op jit(solution)/shard_map/ppermute | solution.py:58
  37.6 0.3 collective-permute-start.2
  37.8 8.6 %all-to-all-start.2 = ((s16[16,8,896]{2,1,0:T(8,128)(2,1)}), s16[16,8,896]{2,1,0:T(8,128)(2,1)S(1)}, u32[]{:S(2)}, u32[]{:S(2)}) async-start(s16[16,8,896]{2,1,0:T(8,128)(2,1)} %get-tuple-element.38), calls=%async_computation.2 | async-start | bytes 458752 | tf_op jit(solution)/shard_map/all_to_all | solution.py:378
  46.5 0.2 collective-permute-start.6
  46.7 3.5 %shard_map.99.first_ref.refs_1_ = bf16[1152,768]{1,0:T(8,128)(2,1)} custom-call(s32[3]{0:T(128)} %copy-done.1, bf16[4,144,768]{2,1,0:T(8,128)(2,1)} %collective-permute-done.3.near_ref, bf16[4,144,768]{2,1,0:T(8,128)(2,1)} %collective-permute-done.4.back_ref), custom_call_target="tpu_custom_call" | custom-call | tf_op jit(solution)/shard_map/pallas_call | solution.py:381
  50.2 7.3 %all-to-all-done.2.parts_ref = s16[16,8,896]{2,1,0:T(8,128)(2,1)S(1)} async-done(((s16[16,8,896]{2,1,0:T(8,128)(2,1)}), s16[16,8,896]{2,1,0:T(8,128)(2,1)S(1)}, u32[]{:S(2)}, u32[]{:S(2)}) %all-to-all-start.2) | async-done | bytes 229408 | tf_op jit(solution)/shard_map/all_to_all | solution.py:378
  57.5 2.7 %shard_map.100 = (bf16[2304,768]{1,0:T(8,128)(2,1)S(1)}, f32[8,1536]{1,0:T(8,128)S(1)}, f32[8,2304]{1,0:T(8,128)S(1)}) custom-call(s32[3]{0:T(128)S(1)} %copy-done.2, f32[4,128]{1,0:T(4,128)S(1)} %get-tuple-element.41.__.coef_ref, f32[1,1536]{1,0:T(1,128)S(1)} %get-tuple-element.42.scale_ref, s16[16,8,896]{2,1,0:T(8,128)(2,1)S(1)} %all-to-all-done.2.parts_ref, ...), custom_call_target="tpu_custom_call" | custom-call | tf_op jit(solution)/shard_map/pallas_call | solution.py:392
  60.2 0.0 collective-permute-done.7.refs_1_
  60.2 2.6 %shard_map.101 = (bf16[1152,768]{1,0:T(8,128)(2,1)S(1)}, s16[8,8,1664]{2,1,0:T(8,128)(2,1)S(1)}) custom-call(s32[3]{0:T(128)S(1)} %copy-done.2, f32[4,128]{1,0:T(4,128)S(1)} %get-tuple-element.41.__.coef_ref, f32[1,1536]{1,0:T(1,128)S(1)} %get-tuple-element.42.scale_ref, f32[8,1536]{1,0:T(8,128)S(1)} %get-tuple-element.45.rhs_ref.refs_3_, ...), custom_call_target="tpu_custom_call" | custom-call | tf_op jit(solution)/shard_map/pallas_call | solution.py:397
  62.8 13.6 %all_to_all.31.parts_ref = s16[8,8,1664]{2,1,0:T(8,128)(2,1)S(1)} all-to-all(s16[8,8,1664]{2,1,0:T(8,128)(2,1)S(1)} %get-tuple-element.49), channel_id=1, replica_groups=mesh['xl'=2,'z'=8,'y'=4,'xh'=2,'core'=2] {'z'}, dimensions={0} | all-to-all | bytes 425984 | tf_op jit(solution)/shard_map/all_to_all | solution.py:314
  76.4 3.0 %shard_map.102 = (s16[8,8,1664]{2,1,0:T(8,128)(2,1)S(1)}, f32[8,1536]{1,0:T(8,128)S(1)}, f32[8,1536]{1,0:T(8,128)S(1)}) custom-call(f32[4,128]{1,0:T(4,128)S(1)} %get-tuple-element.41.__.coef_ref, f32[1,1536]{1,0:T(1,128)S(1)} %get-tuple-element.42.scale_ref, s16[8,8,1664]{2,1,0:T(8,128)(2,1)S(1)} %all_to_all.31.parts_ref, ...), custom_call_target="tpu_custom_call" | custom-call | tf_op jit(solution)/shard_map/pallas_call | solution.py:404
  79.4 12.2 %all_to_all.32.parts_ref = s16[8,8,1664]{2,1,0:T(8,128)(2,1)S(1)} all-to-all(s16[8,8,1664]{2,1,0:T(8,128)(2,1)S(1)} %get-tuple-element.51), channel_id=1, replica_groups=mesh['xl'=2,'z'=8,'y'=4,'xh'=2,'core'=2] {'z'}, dimensions={0} | all-to-all | bytes 425984 | tf_op jit(solution)/shard_map/all_to_all | solution.py:314
  91.7 2.7 %shard_map.103 = f32[32,16,72]{2,1,0:T(8,128)S(1)} custom-call(s32[3]{0:T(128)S(1)} %copy-done.2, f32[4,128]{1,0:T(4,128)S(1)} %get-tuple-element.41.__.coef_ref, f32[1,1536]{1,0:T(1,128)S(1)} %get-tuple-element.42.scale_ref, s16[8,8,1664]{2,1,0:T(8,128)(2,1)S(1)} %all_to_all.32.parts_ref, bf16[2304,768]{1,0:T(8,128)(2,1)S(1)} %get-tuple-element.47.own_ref.refs_0_, ...), custom_call_target="tpu_custom_call" | custom-call | tf_op jit(solution)/shard_map/pallas_call | solution.py:408
  94.4 15.3 %all_to_all.33.blocks_ref = f32[32,16,72]{2,1,0:T(8,128)S(1)} all-to-all(f32[32,16,72]{2,1,0:T(8,128)S(1)} %shard_map.103), channel_id=1, replica_groups=mesh['xl'=2,'z'=8,'y'=4,'xh'=2,'core'=2] {'xl','y','xh','core'}, dimensions={0} | all-to-all | bytes 294912 | tf_op jit(solution)/shard_map/all_to_all | solution.py:414
  109.7 0.8 shard_map.104
  (17 shorter events, 0.1 us)
Async XLA Ops:
  1.7 4.5 %collective-permute-start = (bf16[72,1024]{1,0:T(8,128)(2,1)S(1)}, bf16[72,1024]{1,0:T(8,128)(2,1)S(1)}, u32[]{:S(2)}, u32[]{:S(2)}) collective-permute-start(bf16[72,1024]{1,0:T(8,128)(2,1)S(1)} %maximum_select_fusion.1), channel_id=1, source_target_pairs={{0,1},{1,0},{2,3},{3,2},{4,5},{5,4},{6,7},{7,6},{8,9},{9,8},{10,11... | collective-permute-start | bytes 442376 | tf_op jit(solution)/shard_map/ppermute | solution.py:58
  6.1 20.6 %copy-start.1 = (s32[3]{0:T(128)}, s32[3]{0:T(128)S(1)}, u32[]{:S(2)}) copy-start(s32[3]{0:T(128)S(1)} %pad_add_fusion.place_ref) | copy-start | bytes 40
  18.9 7.9 %copy-start.3 = (s32[2]{0:T(128)S(1)}, s32[2]{0:T(128)}, u32[]{:S(2)}) copy-start(s32[2]{0:T(128)} %counts_ref.1) | copy-start | bytes 28
  18.9 15.1 %collective-permute-start.1 = (bf16[4,144,768]{2,1,0:T(8,128)(2,1)S(1)}, bf16[4,144,768]{2,1,0:T(8,128)(2,1)S(1)}, u32[]{:S(2)}, u32[]{:S(2)}) collective-permute-start(bf16[4,144,768]{2,1,0:T(8,128)(2,1)S(1)} %slice.14.near_ref.refs_0_), channel_id=1, source_target_pairs={{0,128},{1,5},{4,132},{5,9},{8,136},{9,13},{12,140},{13,1},{128,2}... | collective-permute-start | bytes 2654216 | tf_op jit(solution)/shard_map/ppermute | solution.py:54
  20.9 13.1 %all-to-all-start.1 = ((f32[4,16,768]{2,1,0:T(8,128)}), f32[4,16,768]{2,1,0:T(8,128)S(1)}, u32[]{:S(2)}, u32[]{:S(2)}) async-start(f32[4,16,768]{2,1,0:T(8,128)} %shard_map.96), calls=%async_computation.1 | async-start | bytes 393216 | tf_op jit(solution)/shard_map/all_to_all | solution.py:50
  27.3 19.3 %collective-permute-start.3 = (bf16[4,144,768]{2,1,0:T(8,128)(2,1)S(1)}, bf16[4,144,768]{2,1,0:T(8,128)(2,1)}, u32[]{:S(2)}, u32[]{:S(2)}) collective-permute-start(bf16[4,144,768]{2,1,0:T(8,128)(2,1)S(1)} %slice.14.near_ref.refs_0_), channel_id=1, source_target_pairs={{0,1},{1,0},{2,3},{3,2},{4,5},{5,4},{6,7},{7,6},{8,9},{9,8},{10,11... | collective-permute-start | bytes 2654216 | tf_op jit(solution)/shard_map/ppermute | solution.py:58
  29.6 16.9 %collective-permute-start.5 = (bf16[4,144,768]{2,1,0:T(8,128)(2,1)S(1)}, bf16[4,144,768]{2,1,0:T(8,128)(2,1)}, u32[]{:S(2)}, u32[]{:S(2)}) collective-permute-start(bf16[4,144,768]{2,1,0:T(8,128)(2,1)S(1)} %slice.14.near_ref.refs_0_), channel_id=1, source_target_pairs={{0,130},{1,13},{4,134},{5,1},{8,138},{9,5},{12,142},{13,9},{128,0}... | collective-permute-start | bytes 2654216 | tf_op jit(solution)/shard_map/ppermute | solution.py:54
  34.8 11.8 %collective-permute-start.4 = (bf16[4,144,768]{2,1,0:T(8,128)(2,1)S(1)}, bf16[4,144,768]{2,1,0:T(8,128)(2,1)}, u32[]{:S(2)}, u32[]{:S(2)}) collective-permute-start(bf16[4,144,768]{2,1,0:T(8,128)(2,1)S(1)} %get-tuple-element.39.refs_1_), channel_id=1, source_target_pairs={{0,1},{1,0},{2,3},{3,2},{4,5},{5,4},{6,7},{7,6},{8,9},{9,8},{10,11... | collective-permute-start | bytes 2654216 | tf_op jit(solution)/shard_map/ppermute | solution.py:58
  37.6 19.9 %collective-permute-start.2 = (bf16[4,144,768]{2,1,0:T(8,128)(2,1)S(1)}, bf16[4,144,768]{2,1,0:T(8,128)(2,1)}, u32[]{:S(2)}, u32[]{:S(2)}) collective-permute-start(bf16[4,144,768]{2,1,0:T(8,128)(2,1)S(1)} %get-tuple-element.39.refs_1_), channel_id=1, source_target_pairs={{0,128},{1,5},{4,132},{5,9},{8,136},{9,13},{12,140},{13,1},{128,2}... | collective-permute-start | bytes 2654216 | tf_op jit(solution)/shard_map/ppermute | solution.py:54
  37.8 19.6 %all-to-all-start.2 = ((s16[16,8,896]{2,1,0:T(8,128)(2,1)}), s16[16,8,896]{2,1,0:T(8,128)(2,1)S(1)}, u32[]{:S(2)}, u32[]{:S(2)}) async-start(s16[16,8,896]{2,1,0:T(8,128)(2,1)} %get-tuple-element.38), calls=%async_computation.2 | async-start | bytes 458752 | tf_op jit(solution)/shard_map/all_to_all | solution.py:378
  46.4 11.1 %copy-start.2 = (s32[3]{0:T(128)S(1)}, s32[3]{0:T(128)}, u32[]{:S(2)}) copy-start(s32[3]{0:T(128)} %copy-done.1) | copy-start | bytes 40
  46.5 13.7 %collective-permute-start.6 = (bf16[4,144,768]{2,1,0:T(8,128)(2,1)}, bf16[4,144,768]{2,1,0:T(8,128)(2,1)S(1)}, u32[]{:S(2)}, u32[]{:S(2)}) collective-permute-start(bf16[4,144,768]{2,1,0:T(8,128)(2,1)} %collective-permute-done.5.refs_2_), channel_id=1, source_target_pairs={{0,1},{1,0},{2,3},{3,2},{4,5},{5,4},{6,7},{7,6},{8,9},{9,8},{10,11... | collective-permute-start | bytes 2654216 | tf_op jit(solution)/shard_map/ppermute | solution.py:58
  57.5 2.7 %copy-start = (bf16[1152,768]{1,0:T(8,128)(2,1)S(1)}, bf16[1152,768]{1,0:T(8,128)(2,1)}, u32[]{:S(2)}) copy-start(bf16[1152,768]{1,0:T(8,128)(2,1)} %shard_map.99.first_ref.refs_1_) | copy-start | bytes 5308420
  57.5 2.7 %collective-permute-start.7 = (bf16[4,144,768]{2,1,0:T(8,128)(2,1)}, bf16[4,144,768]{2,1,0:T(8,128)(2,1)S(1)}, u32[]{:S(2)}, u32[]{:S(2)}) collective-permute-start(bf16[4,144,768]{2,1,0:T(8,128)(2,1)} %collective-permute-done.2.refs_3_), channel_id=1, source_target_pairs={{0,1},{1,0},{2,3},{3,2},{4,5},{5,4},{6,7},{7,6},{8,9},{9,8},{10,11... | collective-permute-start | bytes 2654216 | tf_op jit(solution)/shard_map/ppermute | solution.py:58

commit v9 on v8

--- a/solution.py
+++ b/solution.py
@@ -152,11 +152,11 @@
         preferred_element_type=jnp.float32,
     )
     for across in range(SIDE):
-        out_ref[across] = out[across * each : (across + 1) * each]
+        out_ref[across] = code(out[across * each : (across + 1) * each])
 
 
 def plane_kernel(shares_ref, _, __, out_ref, *unused):
-    total = jnp.sum(shares_ref[...], axis=0)
+    total = sum_coded(shares_ref, range(shares_ref.shape[0]))
     cols = out_ref.shape[1]
     coded = [code(total[k * cols : (k + 1) * cols]) for k in range(2)]
     for k in range(out_ref.shape[0]):
@@ -351,7 +351,7 @@
     back, front = along(near, 1), along(near, 3)
     shares = call(
         line_kernel,
-        shape((SIDE, 2 * cols, rows), f32),
+        shape((SIDE, 2 * cols, rows + TILE), jnp.int16),
         [VMEM] * 2,
         [pltpu.VMEM((SIDE * 2 * cols, SIDE * block.shape[0]), f32)],
     )(packed, near)

time: 111 us -> 111 us (level)
  no operation moved by 1% of the time
where the time goes in v9:
time: 111 us; the launch traced here: 110 us
  blocking collectives  53 us (48%)
  starting transfers between devices  23.1 us (21%)
  Pallas kernels  18.7 us (17%)
  waiting for transfers between devices  10.4 us (9%)
  between operations  2.74 us (2%)
  other arithmetic  2.19 us (2%)
    all_to_all x2, blocking collectives, sum_parts(): return lax.all_to_all(copies, 'z', 0, 0, tiled=True)  25.8 us
    all_to_all x1, blocking collectives, body(): out = lax.all_to_all(out, MEMBERS, 0, 0, tiled=True)  15.3 us
    all_to_all x1, blocking collectives, exchange(): lax.all_to_all(blocks, MEMBERS, 0, 0, axis_index_groups=lines(first), til...  11.8 us
    all_to_all x1, starting transfers between devices, body(): parts = lax.all_to_all(parts, ('z', 'core'), 0, 0, tiled=True)  8.59 us
    ppermute x5, starting transfers between devices, swap(): return lax.ppermute(value, 'core', [(0, 1), (1, 0)])  8.46 us
    all_to_all x1, waiting for transfers between devices, body(): parts = lax.all_to_all(parts, ('z', 'core'), 0, 0, tiled=True)  7.3 us
    all_to_all x1, starting transfers between devices, exchange(): lax.all_to_all(blocks, MEMBERS, 0, 0, axis_index_groups=lines(first), til...  3.89 us
    pallas_call x1, Pallas kernels, body(): pl.pallas_call(lay_kernel, out_shape=shape((total // 2, rows), jnp.bfloat...  3.52 us
  transfers between devices with their start and end apart: 10, of which 2 were waited for; matrix products, arithmetic and copies ran while one was open for 1% of the time, Pallas kernels for 8%

profile of v9, /device:TPU:1, one launch (start us, length us, event | category | flops | bytes accessed | tf_op | source)
XLA Modules:
  0.0 110.2 jit_solution(15355249809017982423)
XLA Ops:
  0.6 1.0 maximum_select_fusion.1
  1.7 3.3 %collective-permute-start = (bf16[72,1024]{1,0:T(8,128)(2,1)S(1)}, bf16[72,1024]{1,0:T(8,128)(2,1)S(1)}, u32[]{:S(2)}, u32[]{:S(2)}) collective-permute-start(bf16[72,1024]{1,0:T(8,128)(2,1)S(1)} %maximum_select_fusion.1), channel_id=1, source_target_pairs={{0,1},{1,0},{2,3},{3,2},{4,5},{5,4},{6,7},{7,6},{8,9},{9,8},{10,11... | collective-permute-start | bytes 442376 | tf_op jit(solution)/shard_map/ppermute | solution.py:58
  5.0 1.0 maximum_select_fusion.2.keep_ref
  6.1 0.1 pad_add_fusion.place_ref
  6.1 0.0 collective-permute-done.got_ref
  6.2 0.8 shard_map.95
  7.0 11.8 %all_to_all.30.packed_ref = bf16[4,160,768]{2,1,0:T(8,128)(2,1)S(1)} all-to-all(bf16[4,160,768]{2,1,0:T(8,128)(2,1)S(1)} %shard_map.95), channel_id=1, replica_groups={{0,4,8,12},{128,132,136,140},{2,6,10,14},{130,134,138,142},{1,129,3,131..., dimensions={0} | all-to-all | bytes 1966080 | tf_op jit(solution)/shard_map/all_to_all | solution.py:50
  18.9 0.1 slice.14.near_ref.refs_0_
  18.9 1.0 collective-permute-start.1
  19.9 1.1 shard_map.96
  21.0 3.9 %all-to-all-start.1 = ((s16[4,16,896]{2,1,0:T(8,128)(2,1)}), s16[4,16,896]{2,1,0:T(8,128)(2,1)S(1)}, u32[]{:S(2)}, u32[]{:S(2)}) async-start(s16[4,16,896]{2,1,0:T(8,128)(2,1)} %shard_map.96), calls=%async_computation.1 | async-start | bytes 229376 | tf_op jit(solution)/shard_map/all_to_all | solution.py:50
  26.9 0.6 shard_map.97
  27.4 2.2 %collective-permute-start.3 = (bf16[4,144,768]{2,1,0:T(8,128)(2,1)S(1)}, bf16[4,144,768]{2,1,0:T(8,128)(2,1)}, u32[]{:S(2)}, u32[]{:S(2)}) collective-permute-start(bf16[4,144,768]{2,1,0:T(8,128)(2,1)S(1)} %slice.14.near_ref.refs_0_), channel_id=1, source_target_pairs={{0,1},{1,0},{2,3},{3,2},{4,5},{5,4},{6,7},{7,6},{8,9},{9,8},{10,11... | collective-permute-start | bytes 2654216 | tf_op jit(solution)/shard_map/ppermute | solution.py:58
  29.6 0.9 collective-permute-start.5
  30.5 3.0 %all-to-all-done.1.shares_ref = s16[4,16,896]{2,1,0:T(8,128)(2,1)S(1)} async-done(((s16[4,16,896]{2,1,0:T(8,128)(2,1)}), s16[4,16,896]{2,1,0:T(8,128)(2,1)S(1)}, u32[]{:S(2)}, u32[]{:S(2)}) %all-to-all-start.1) | async-done | bytes 114720 | tf_op jit(solution)/shard_map/all_to_all | solution.py:50
  33.6 0.0 collective-permute-done.1._
  33.6 1.0 shard_map.98
  34.5 2.7 %collective-permute-start.4 = (bf16[4,144,768]{2,1,0:T(8,128)(2,1)S(1)}, bf16[4,144,768]{2,1,0:T(8,128)(2,1)}, u32[]{:S(2)}, u32[]{:S(2)}) collective-permute-start(bf16[4,144,768]{2,1,0:T(8,128)(2,1)S(1)} %get-tuple-element.39.refs_1_), channel_id=1, source_target_pairs={{0,1},{1,0},{2,3},{3,2},{4,5},{5,4},{6,7},{7,6},{8,9},{9,8},{10,11... | collective-permute-start | bytes 2654216 | tf_op jit(solution)/shard_map/ppermute | solution.py:58
  37.3 0.3 collective-permute-start.2
  37.5 8.6 %all-to-all-start.2 = ((s16[16,8,896]{2,1,0:T(8,128)(2,1)}), s16[16,8,896]{2,1,0:T(8,128)(2,1)S(1)}, u32[]{:S(2)}, u32[]{:S(2)}) async-start(s16[16,8,896]{2,1,0:T(8,128)(2,1)} %get-tuple-element.38), calls=%async_computation.2 | async-start | bytes 458752 | tf_op jit(solution)/shard_map/all_to_all | solution.py:378
  46.2 0.2 collective-permute-start.6
  46.4 3.5 %shard_map.99.first_ref.refs_1_ = bf16[1152,768]{1,0:T(8,128)(2,1)} custom-call(s32[3]{0:T(128)} %copy-done.1, bf16[4,144,768]{2,1,0:T(8,128)(2,1)} %collective-permute-done.3.near_ref, bf16[4,144,768]{2,1,0:T(8,128)(2,1)} %collective-permute-done.4.back_ref), custom_call_target="tpu_custom_call" | custom-call | tf_op jit(solution)/shard_map/pallas_call | solution.py:381
  49.9 7.3 %all-to-all-done.2.parts_ref = s16[16,8,896]{2,1,0:T(8,128)(2,1)S(1)} async-done(((s16[16,8,896]{2,1,0:T(8,128)(2,1)}), s16[16,8,896]{2,1,0:T(8,128)(2,1)S(1)}, u32[]{:S(2)}, u32[]{:S(2)}) %all-to-all-start.2) | async-done | bytes 229408 | tf_op jit(solution)/shard_map/all_to_all | solution.py:378
  57.2 2.7 %shard_map.100 = (bf16[2304,768]{1,0:T(8,128)(2,1)S(1)}, f32[8,1536]{1,0:T(8,128)S(1)}, f32[8,2304]{1,0:T(8,128)S(1)}) custom-call(s32[3]{0:T(128)S(1)} %copy-done.2, f32[4,128]{1,0:T(4,128)S(1)} %get-tuple-element.41.__.coef_ref, f32[1,1536]{1,0:T(1,128)S(1)} %get-tuple-element.42.scale_ref, s16[16,8,896]{2,1,0:T(8,128)(2,1)S(1)} %all-to-all-done.2.parts_ref, ...), custom_call_target="tpu_custom_call" | custom-call | tf_op jit(solution)/shard_map/pallas_call | solution.py:392
  59.9 0.0 collective-permute-done.7.refs_1_
  59.9 2.6 %shard_map.101 = (bf16[1152,768]{1,0:T(8,128)(2,1)S(1)}, s16[8,8,1664]{2,1,0:T(8,128)(2,1)S(1)}) custom-call(s32[3]{0:T(128)S(1)} %copy-done.2, f32[4,128]{1,0:T(4,128)S(1)} %get-tuple-element.41.__.coef_ref, f32[1,1536]{1,0:T(1,128)S(1)} %get-tuple-element.42.scale_ref, f32[8,1536]{1,0:T(8,128)S(1)} %get-tuple-element.45.rhs_ref.refs_3_, ...), custom_call_target="tpu_custom_call" | custom-call | tf_op jit(solution)/shard_map/pallas_call | solution.py:397
  62.5 13.6 %all_to_all.31.parts_ref = s16[8,8,1664]{2,1,0:T(8,128)(2,1)S(1)} all-to-all(s16[8,8,1664]{2,1,0:T(8,128)(2,1)S(1)} %get-tuple-element.49), channel_id=1, replica_groups=mesh['xl'=2,'z'=8,'y'=4,'xh'=2,'core'=2] {'z'}, dimensions={0} | all-to-all | bytes 425984 | tf_op jit(solution)/shard_map/all_to_all | solution.py:314
  76.1 3.0 %shard_map.102 = (s16[8,8,1664]{2,1,0:T(8,128)(2,1)S(1)}, f32[8,1536]{1,0:T(8,128)S(1)}, f32[8,1536]{1,0:T(8,128)S(1)}) custom-call(f32[4,128]{1,0:T(4,128)S(1)} %get-tuple-element.41.__.coef_ref, f32[1,1536]{1,0:T(1,128)S(1)} %get-tuple-element.42.scale_ref, s16[8,8,1664]{2,1,0:T(8,128)(2,1)S(1)} %all_to_all.31.parts_ref, ...), custom_call_target="tpu_custom_call" | custom-call | tf_op jit(solution)/shard_map/pallas_call | solution.py:404
  79.1 12.2 %all_to_all.32.parts_ref = s16[8,8,1664]{2,1,0:T(8,128)(2,1)S(1)} all-to-all(s16[8,8,1664]{2,1,0:T(8,128)(2,1)S(1)} %get-tuple-element.51), channel_id=1, replica_groups=mesh['xl'=2,'z'=8,'y'=4,'xh'=2,'core'=2] {'z'}, dimensions={0} | all-to-all | bytes 425984 | tf_op jit(solution)/shard_map/all_to_all | solution.py:314
  91.4 2.7 %shard_map.103 = f32[32,16,72]{2,1,0:T(8,128)S(1)} custom-call(s32[3]{0:T(128)S(1)} %copy-done.2, f32[4,128]{1,0:T(4,128)S(1)} %get-tuple-element.41.__.coef_ref, f32[1,1536]{1,0:T(1,128)S(1)} %get-tuple-element.42.scale_ref, s16[8,8,1664]{2,1,0:T(8,128)(2,1)S(1)} %all_to_all.32.parts_ref, bf16[2304,768]{1,0:T(8,128)(2,1)S(1)} %get-tuple-element.47.own_ref.refs_0_, ...), custom_call_target="tpu_custom_call" | custom-call | tf_op jit(solution)/shard_map/pallas_call | solution.py:408
  94.1 15.3 %all_to_all.33.blocks_ref = f32[32,16,72]{2,1,0:T(8,128)S(1)} all-to-all(f32[32,16,72]{2,1,0:T(8,128)S(1)} %shard_map.103), channel_id=1, replica_groups=mesh['xl'=2,'z'=8,'y'=4,'xh'=2,'core'=2] {'xl','y','xh','core'}, dimensions={0} | all-to-all | bytes 294912 | tf_op jit(solution)/shard_map/all_to_all | solution.py:414
  109.4 0.8 shard_map.104
  (17 shorter events, 0.1 us)
Async XLA Ops:
  1.7 4.5 %collective-permute-start = (bf16[72,1024]{1,0:T(8,128)(2,1)S(1)}, bf16[72,1024]{1,0:T(8,128)(2,1)S(1)}, u32[]{:S(2)}, u32[]{:S(2)}) collective-permute-start(bf16[72,1024]{1,0:T(8,128)(2,1)S(1)} %maximum_select_fusion.1), channel_id=1, source_target_pairs={{0,1},{1,0},{2,3},{3,2},{4,5},{5,4},{6,7},{7,6},{8,9},{9,8},{10,11... | collective-permute-start | bytes 442376 | tf_op jit(solution)/shard_map/ppermute | solution.py:58
  6.1 20.7 %copy-start.1 = (s32[3]{0:T(128)}, s32[3]{0:T(128)S(1)}, u32[]{:S(2)}) copy-start(s32[3]{0:T(128)S(1)} %pad_add_fusion.place_ref) | copy-start | bytes 40
  18.9 8.0 %copy-start.3 = (s32[2]{0:T(128)S(1)}, s32[2]{0:T(128)}, u32[]{:S(2)}) copy-start(s32[2]{0:T(128)} %counts_ref.1) | copy-start | bytes 28
  18.9 14.7 %collective-permute-start.1 = (bf16[4,144,768]{2,1,0:T(8,128)(2,1)S(1)}, bf16[4,144,768]{2,1,0:T(8,128)(2,1)S(1)}, u32[]{:S(2)}, u32[]{:S(2)}) collective-permute-start(bf16[4,144,768]{2,1,0:T(8,128)(2,1)S(1)} %slice.14.near_ref.refs_0_), channel_id=1, source_target_pairs={{0,128},{1,5},{4,132},{5,9},{8,136},{9,13},{12,140},{13,1},{128,2}... | collective-permute-start | bytes 2654216 | tf_op jit(solution)/shard_map/ppermute | solution.py:54
  21.0 12.6 %all-to-all-start.1 = ((s16[4,16,896]{2,1,0:T(8,128)(2,1)}), s16[4,16,896]{2,1,0:T(8,128)(2,1)S(1)}, u32[]{:S(2)}, u32[]{:S(2)}) async-start(s16[4,16,896]{2,1,0:T(8,128)(2,1)} %shard_map.96), calls=%async_computation.1 | async-start | bytes 229376 | tf_op jit(solution)/shard_map/all_to_all | solution.py:50
  27.4 18.9 %collective-permute-start.3 = (bf16[4,144,768]{2,1,0:T(8,128)(2,1)S(1)}, bf16[4,144,768]{2,1,0:T(8,128)(2,1)}, u32[]{:S(2)}, u32[]{:S(2)}) collective-permute-start(bf16[4,144,768]{2,1,0:T(8,128)(2,1)S(1)} %slice.14.near_ref.refs_0_), channel_id=1, source_target_pairs={{0,1},{1,0},{2,3},{3,2},{4,5},{5,4},{6,7},{7,6},{8,9},{9,8},{10,11... | collective-permute-start | bytes 2654216 | tf_op jit(solution)/shard_map/ppermute | solution.py:58
  29.6 16.5 %collective-permute-start.5 = (bf16[4,144,768]{2,1,0:T(8,128)(2,1)S(1)}, bf16[4,144,768]{2,1,0:T(8,128)(2,1)}, u32[]{:S(2)}, u32[]{:S(2)}) collective-permute-start(bf16[4,144,768]{2,1,0:T(8,128)(2,1)S(1)} %slice.14.near_ref.refs_0_), channel_id=1, source_target_pairs={{0,130},{1,13},{4,134},{5,1},{8,138},{9,5},{12,142},{13,9},{128,0}... | collective-permute-start | bytes 2654216 | tf_op jit(solution)/shard_map/ppermute | solution.py:54
  34.5 11.8 %collective-permute-start.4 = (bf16[4,144,768]{2,1,0:T(8,128)(2,1)S(1)}, bf16[4,144,768]{2,1,0:T(8,128)(2,1)}, u32[]{:S(2)}, u32[]{:S(2)}) collective-permute-start(bf16[4,144,768]{2,1,0:T(8,128)(2,1)S(1)} %get-tuple-element.39.refs_1_), channel_id=1, source_target_pairs={{0,1},{1,0},{2,3},{3,2},{4,5},{5,4},{6,7},{7,6},{8,9},{9,8},{10,11... | collective-permute-start | bytes 2654216 | tf_op jit(solution)/shard_map/ppermute | solution.py:58
  37.3 19.9 %collective-permute-start.2 = (bf16[4,144,768]{2,1,0:T(8,128)(2,1)S(1)}, bf16[4,144,768]{2,1,0:T(8,128)(2,1)}, u32[]{:S(2)}, u32[]{:S(2)}) collective-permute-start(bf16[4,144,768]{2,1,0:T(8,128)(2,1)S(1)} %get-tuple-element.39.refs_1_), channel_id=1, source_target_pairs={{0,128},{1,5},{4,132},{5,9},{8,136},{9,13},{12,140},{13,1},{128,2}... | collective-permute-start | bytes 2654216 | tf_op jit(solution)/shard_map/ppermute | solution.py:54
  37.5 19.6 %all-to-all-start.2 = ((s16[16,8,896]{2,1,0:T(8,128)(2,1)}), s16[16,8,896]{2,1,0:T(8,128)(2,1)S(1)}, u32[]{:S(2)}, u32[]{:S(2)}) async-start(s16[16,8,896]{2,1,0:T(8,128)(2,1)} %get-tuple-element.38), calls=%async_computation.2 | async-start | bytes 458752 | tf_op jit(solution)/shard_map/all_to_all | solution.py:378
  46.1 11.1 %copy-start.2 = (s32[3]{0:T(128)S(1)}, s32[3]{0:T(128)}, u32[]{:S(2)}) copy-start(s32[3]{0:T(128)} %copy-done.1) | copy-start | bytes 40
  46.2 13.7 %collective-permute-start.6 = (bf16[4,144,768]{2,1,0:T(8,128)(2,1)}, bf16[4,144,768]{2,1,0:T(8,128)(2,1)S(1)}, u32[]{:S(2)}, u32[]{:S(2)}) collective-permute-start(bf16[4,144,768]{2,1,0:T(8,128)(2,1)} %collective-permute-done.5.refs_2_), channel_id=1, source_target_pairs={{0,1},{1,0},{2,3},{3,2},{4,5},{5,4},{6,7},{7,6},{8,9},{9,8},{10,11... | collective-permute-start | bytes 2654216 | tf_op jit(solution)/shard_map/ppermute | solution.py:58
  57.2 2.7 %copy-start = (bf16[1152,768]{1,0:T(8,128)(2,1)S(1)}, bf16[1152,768]{1,0:T(8,128)(2,1)}, u32[]{:S(2)}) copy-start(bf16[1152,768]{1,0:T(8,128)(2,1)} %shard_map.99.first_ref.refs_1_) | copy-start | bytes 5308420
  57.2 2.7 %collective-permute-start.7 = (bf16[4,144,768]{2,1,0:T(8,128)(2,1)}, bf16[4,144,768]{2,1,0:T(8,128)(2,1)S(1)}, u32[]{:S(2)}, u32[]{:S(2)}) collective-permute-start(bf16[4,144,768]{2,1,0:T(8,128)(2,1)} %collective-permute-done.2.refs_3_), channel_id=1, source_target_pairs={{0,1},{1,0},{2,3},{3,2},{4,5},{5,4},{6,7},{7,6},{8,9},{9,8},{10,11... | collective-permute-start | bytes 2654216 | tf_op jit(solution)/shard_map/ppermute | solution.py:58

commit v10 on v8

--- a/solution.py
+++ b/solution.py
@@ -328,13 +328,7 @@
     lead = core == 0
     first = jnp.concatenate([x_first.T, w_first], axis=1)
     second = jnp.concatenate([x_second.T, w_second], axis=1)
-    give = jnp.where(lead, second, first)
-    give, *own_args = lax.optimization_barrier((give, x_first, x_second, w_first, w_second))
-    kept = jnp.where(
-        lead,
-        jnp.concatenate([own_args[0].T, own_args[2]], axis=1),
-        jnp.concatenate([own_args[1].T, own_args[3]], axis=1),
-    )
+    kept, give = jnp.where(lead, first, second), jnp.where(lead, second, first)
     got_all = swap(give)
     mine, got = kept[:, :rows], got_all[:, :rows]
     block = jnp.where(

time: 111 us -> 111 us (level)
  transfers between devices with their start and end apart: 10 -> 10, of which waited for: 2 -> 3; matrix products, arithmetic and copies ran while one was open for 1% -> 0% of each run, Pallas kernels for 8% -> 8%
where the time goes in v10:
time: 111 us; the launch traced here: 110 us
  blocking collectives  53.1 us (48%)
  starting transfers between devices  23.2 us (21%)
  Pallas kernels  18.5 us (17%)
  waiting for transfers between devices  11.7 us (11%)
  between operations  2.73 us (2%)
  other arithmetic  1.17 us (1%)
    all_to_all x2, blocking collectives, sum_parts(): return lax.all_to_all(copies, 'z', 0, 0, tiled=True)  25.8 us
    all_to_all x1, blocking collectives, body(): out = lax.all_to_all(out, MEMBERS, 0, 0, tiled=True)  15.3 us
    all_to_all x1, blocking collectives, exchange(): lax.all_to_all(blocks, MEMBERS, 0, 0, axis_index_groups=lines(first), til...  12 us
    ppermute x5, starting transfers between devices, swap(): return lax.ppermute(value, 'core', [(0, 1), (1, 0)])  8.74 us
    all_to_all x1, starting transfers between devices, body(): parts = lax.all_to_all(parts, ('z', 'core'), 0, 0, tiled=True)  8.59 us
    all_to_all x1, waiting for transfers between devices, body(): parts = lax.all_to_all(parts, ('z', 'core'), 0, 0, tiled=True)  7.31 us
    all_to_all x1, starting transfers between devices, exchange(): lax.all_to_all(blocks, MEMBERS, 0, 0, axis_index_groups=lines(first), til...  3.89 us
    pallas_call x1, Pallas kernels, body(): pl.pallas_call(lay_kernel, out_shape=shape((total // 2, rows), jnp.bfloat...  3.52 us
  transfers between devices with their start and end apart: 10, of which 3 were waited for; matrix products, arithmetic and copies ran while one was open for 0% of the time, Pallas kernels for 8%

profile of v10, /device:TPU:1, one launch (start us, length us, event | category | flops | bytes accessed | tf_op | source)
XLA Modules:
  0.0 110.5 jit_solution(1394292707090886768)
XLA Ops:
  0.6 1.0 broadcast_select_fusion.1
  1.7 3.3 %collective-permute-start = (bf16[72,1024]{1,0:T(8,128)(2,1)S(1)}, bf16[72,1024]{1,0:T(8,128)(2,1)S(1)}, u32[]{:S(2)}, u32[]{:S(2)}) collective-permute-start(bf16[72,1024]{1,0:T(8,128)(2,1)S(1)} %get-tuple-element.45), channel_id=1, source_target_pairs={{0,1},{1,0},{2,3},{3,2},{4,5},{5,4},{6,7},{7,6},{8,9},{9,8},{10,11... | collective-permute-start | bytes 442376 | tf_op jit(solution)/shard_map/ppermute | solution.py:58
  5.0 0.1 pad_add_fusion.place_ref
  5.1 0.9 collective-permute-done.got_ref
  6.1 0.8 shard_map.95
  6.9 12.0 %all_to_all.30.packed_ref = bf16[4,160,768]{2,1,0:T(8,128)(2,1)S(1)} all-to-all(bf16[4,160,768]{2,1,0:T(8,128)(2,1)S(1)} %shard_map.95), channel_id=1, replica_groups={{0,4,8,12},{128,132,136,140},{2,6,10,14},{130,134,138,142},{1,129,3,131..., dimensions={0} | all-to-all | bytes 1966080 | tf_op jit(solution)/shard_map/all_to_all | solution.py:50
  18.9 0.1 slice.14.near_ref.refs_0_
  18.9 0.9 collective-permute-start.1
  19.8 1.0 shard_map.96
  20.8 3.9 %all-to-all-start.1 = ((f32[4,16,768]{2,1,0:T(8,128)}), f32[4,16,768]{2,1,0:T(8,128)S(1)}, u32[]{:S(2)}, u32[]{:S(2)}) async-start(f32[4,16,768]{2,1,0:T(8,128)} %shard_map.96), calls=%async_computation.1 | async-start | bytes 393216 | tf_op jit(solution)/shard_map/all_to_all | solution.py:50
  26.6 0.6 shard_map.97
  27.2 2.4 %collective-permute-start.3 = (bf16[4,144,768]{2,1,0:T(8,128)(2,1)S(1)}, bf16[4,144,768]{2,1,0:T(8,128)(2,1)}, u32[]{:S(2)}, u32[]{:S(2)}) collective-permute-start(bf16[4,144,768]{2,1,0:T(8,128)(2,1)S(1)} %slice.14.near_ref.refs_0_), channel_id=1, source_target_pairs={{0,1},{1,0},{2,3},{3,2},{4,5},{5,4},{6,7},{7,6},{8,9},{9,8},{10,11... | collective-permute-start | bytes 2654216 | tf_op jit(solution)/shard_map/ppermute | solution.py:58
  29.6 0.9 collective-permute-start.5
  30.4 3.5 %all-to-all-done.1.shares_ref = f32[4,16,768]{2,1,0:T(8,128)S(1)} async-done(((f32[4,16,768]{2,1,0:T(8,128)}), f32[4,16,768]{2,1,0:T(8,128)S(1)}, u32[]{:S(2)}, u32[]{:S(2)}) %all-to-all-start.1) | async-done | bytes 196640 | tf_op jit(solution)/shard_map/all_to_all | solution.py:50
  33.9 0.8 shard_map.98
  34.7 2.9 %collective-permute-start.4 = (bf16[4,144,768]{2,1,0:T(8,128)(2,1)S(1)}, bf16[4,144,768]{2,1,0:T(8,128)(2,1)}, u32[]{:S(2)}, u32[]{:S(2)}) collective-permute-start(bf16[4,144,768]{2,1,0:T(8,128)(2,1)S(1)} %get-tuple-element.29.refs_1_), channel_id=1, source_target_pairs={{0,1},{1,0},{2,3},{3,2},{4,5},{5,4},{6,7},{7,6},{8,9},{9,8},{10,11... | collective-permute-start | bytes 2654216 | tf_op jit(solution)/shard_map/ppermute | solution.py:58
  37.6 0.3 collective-permute-start.2
  37.9 8.6 %all-to-all-start.2 = ((s16[16,8,896]{2,1,0:T(8,128)(2,1)}), s16[16,8,896]{2,1,0:T(8,128)(2,1)S(1)}, u32[]{:S(2)}, u32[]{:S(2)}) async-start(s16[16,8,896]{2,1,0:T(8,128)(2,1)} %get-tuple-element.28), calls=%async_computation.2 | async-start | bytes 458752 | tf_op jit(solution)/shard_map/all_to_all | solution.py:372
  46.5 0.0 collective-permute-done.5.refs_2_
  46.5 0.2 collective-permute-start.6
  46.7 0.0 collective-permute-done.4.back_ref
  46.7 3.5 %shard_map.99.first_ref.refs_1_ = bf16[1152,768]{1,0:T(8,128)(2,1)} custom-call(s32[3]{0:T(128)} %copy-done.1, bf16[4,144,768]{2,1,0:T(8,128)(2,1)} %collective-permute-done.3.near_ref, bf16[4,144,768]{2,1,0:T(8,128)(2,1)} %collective-permute-done.4.back_ref), custom_call_target="tpu_custom_call" | custom-call | tf_op jit(solution)/shard_map/pallas_call | solution.py:375
  50.2 7.3 %all-to-all-done.2.parts_ref = s16[16,8,896]{2,1,0:T(8,128)(2,1)S(1)} async-done(((s16[16,8,896]{2,1,0:T(8,128)(2,1)}), s16[16,8,896]{2,1,0:T(8,128)(2,1)S(1)}, u32[]{:S(2)}, u32[]{:S(2)}) %all-to-all-start.2) | async-done | bytes 229408 | tf_op jit(solution)/shard_map/all_to_all | solution.py:372
  57.5 2.7 %shard_map.100 = (bf16[2304,768]{1,0:T(8,128)(2,1)S(1)}, f32[8,1536]{1,0:T(8,128)S(1)}, f32[8,2304]{1,0:T(8,128)S(1)}) custom-call(s32[3]{0:T(128)S(1)} %copy-done.2, f32[4,128]{1,0:T(4,128)S(1)} %get-tuple-element.31.__.coef_ref, f32[1,1536]{1,0:T(1,128)S(1)} %get-tuple-element.32.scale_ref, s16[16,8,896]{2,1,0:T(8,128)(2,1)S(1)} %all-to-all-done.2.parts_ref, ...), custom_call_target="tpu_custom_call" | custom-call | tf_op jit(solution)/shard_map/pallas_call | solution.py:386
  60.2 0.0 collective-permute-done.7.refs_1_
  60.2 2.6 %shard_map.101 = (bf16[1152,768]{1,0:T(8,128)(2,1)S(1)}, s16[8,8,1664]{2,1,0:T(8,128)(2,1)S(1)}) custom-call(s32[3]{0:T(128)S(1)} %copy-done.2, f32[4,128]{1,0:T(4,128)S(1)} %get-tuple-element.31.__.coef_ref, f32[1,1536]{1,0:T(1,128)S(1)} %get-tuple-element.32.scale_ref, f32[8,1536]{1,0:T(8,128)S(1)} %get-tuple-element.35.rhs_ref.refs_3_, ...), custom_call_target="tpu_custom_call" | custom-call | tf_op jit(solution)/shard_map/pallas_call | solution.py:391
  62.8 13.6 %all_to_all.31.parts_ref = s16[8,8,1664]{2,1,0:T(8,128)(2,1)S(1)} all-to-all(s16[8,8,1664]{2,1,0:T(8,128)(2,1)S(1)} %get-tuple-element.39), channel_id=1, replica_groups=mesh['xl'=2,'z'=8,'y'=4,'xh'=2,'core'=2] {'z'}, dimensions={0} | all-to-all | bytes 425984 | tf_op jit(solution)/shard_map/all_to_all | solution.py:314
  76.4 3.0 %shard_map.102 = (s16[8,8,1664]{2,1,0:T(8,128)(2,1)S(1)}, f32[8,1536]{1,0:T(8,128)S(1)}, f32[8,1536]{1,0:T(8,128)S(1)}) custom-call(f32[4,128]{1,0:T(4,128)S(1)} %get-tuple-element.31.__.coef_ref, f32[1,1536]{1,0:T(1,128)S(1)} %get-tuple-element.32.scale_ref, s16[8,8,1664]{2,1,0:T(8,128)(2,1)S(1)} %all_to_all.31.parts_ref, ...), custom_call_target="tpu_custom_call" | custom-call | tf_op jit(solution)/shard_map/pallas_call | solution.py:398
  79.4 12.2 %all_to_all.32.parts_ref = s16[8,8,1664]{2,1,0:T(8,128)(2,1)S(1)} all-to-all(s16[8,8,1664]{2,1,0:T(8,128)(2,1)S(1)} %get-tuple-element.41), channel_id=1, replica_groups=mesh['xl'=2,'z'=8,'y'=4,'xh'=2,'core'=2] {'z'}, dimensions={0} | all-to-all | bytes 425984 | tf_op jit(solution)/shard_map/all_to_all | solution.py:314
  91.7 2.7 %shard_map.103 = f32[32,16,72]{2,1,0:T(8,128)S(1)} custom-call(s32[3]{0:T(128)S(1)} %copy-done.2, f32[4,128]{1,0:T(4,128)S(1)} %get-tuple-element.31.__.coef_ref, f32[1,1536]{1,0:T(1,128)S(1)} %get-tuple-element.32.scale_ref, s16[8,8,1664]{2,1,0:T(8,128)(2,1)S(1)} %all_to_all.32.parts_ref, bf16[2304,768]{1,0:T(8,128)(2,1)S(1)} %get-tuple-element.37.own_ref.refs_0_, ...), custom_call_target="tpu_custom_call" | custom-call | tf_op jit(solution)/shard_map/pallas_call | solution.py:402
  94.4 15.3 %all_to_all.33.blocks_ref = f32[32,16,72]{2,1,0:T(8,128)S(1)} all-to-all(f32[32,16,72]{2,1,0:T(8,128)S(1)} %shard_map.103), channel_id=1, replica_groups=mesh['xl'=2,'z'=8,'y'=4,'xh'=2,'core'=2] {'xl','y','xh','core'}, dimensions={0} | all-to-all | bytes 294912 | tf_op jit(solution)/shard_map/all_to_all | solution.py:408
  109.7 0.8 shard_map.104
  (16 shorter events, 0.1 us)
Async XLA Ops:
  1.7 4.3 %collective-permute-start = (bf16[72,1024]{1,0:T(8,128)(2,1)S(1)}, bf16[72,1024]{1,0:T(8,128)(2,1)S(1)}, u32[]{:S(2)}, u32[]{:S(2)}) collective-permute-start(bf16[72,1024]{1,0:T(8,128)(2,1)S(1)} %get-tuple-element.45), channel_id=1, source_target_pairs={{0,1},{1,0},{2,3},{3,2},{4,5},{5,4},{6,7},{7,6},{8,9},{9,8},{10,11... | collective-permute-start | bytes 442376 | tf_op jit(solution)/shard_map/ppermute | solution.py:58
  5.1 21.5 %copy-start.1 = (s32[3]{0:T(128)}, s32[3]{0:T(128)S(1)}, u32[]{:S(2)}) copy-start(s32[3]{0:T(128)S(1)} %pad_add_fusion.place_ref) | copy-start | bytes 40
  18.9 7.7 %copy-start.3 = (s32[2]{0:T(128)S(1)}, s32[2]{0:T(128)}, u32[]{:S(2)}) copy-start(s32[2]{0:T(128)} %counts_ref.1) | copy-start | bytes 28
  18.9 15.0 %collective-permute-start.1 = (bf16[4,144,768]{2,1,0:T(8,128)(2,1)S(1)}, bf16[4,144,768]{2,1,0:T(8,128)(2,1)S(1)}, u32[]{:S(2)}, u32[]{:S(2)}) collective-permute-start(bf16[4,144,768]{2,1,0:T(8,128)(2,1)S(1)} %slice.14.near_ref.refs_0_), channel_id=1, source_target_pairs={{0,128},{1,5},{4,132},{5,9},{8,136},{9,13},{12,140},{13,1},{128,2}... | collective-permute-start | bytes 2654216 | tf_op jit(solution)/shard_map/ppermute | solution.py:54
  20.8 13.1 %all-to-all-start.1 = ((f32[4,16,768]{2,1,0:T(8,128)}), f32[4,16,768]{2,1,0:T(8,128)S(1)}, u32[]{:S(2)}, u32[]{:S(2)}) async-start(f32[4,16,768]{2,1,0:T(8,128)} %shard_map.96), calls=%async_computation.1 | async-start | bytes 393216 | tf_op jit(solution)/shard_map/all_to_all | solution.py:50
  27.2 19.5 %collective-permute-start.3 = (bf16[4,144,768]{2,1,0:T(8,128)(2,1)S(1)}, bf16[4,144,768]{2,1,0:T(8,128)(2,1)}, u32[]{:S(2)}, u32[]{:S(2)}) collective-permute-start(bf16[4,144,768]{2,1,0:T(8,128)(2,1)S(1)} %slice.14.near_ref.refs_0_), channel_id=1, source_target_pairs={{0,1},{1,0},{2,3},{3,2},{4,5},{5,4},{6,7},{7,6},{8,9},{9,8},{10,11... | collective-permute-start | bytes 2654216 | tf_op jit(solution)/shard_map/ppermute | solution.py:58
  29.6 16.9 %collective-permute-start.5 = (bf16[4,144,768]{2,1,0:T(8,128)(2,1)S(1)}, bf16[4,144,768]{2,1,0:T(8,128)(2,1)}, u32[]{:S(2)}, u32[]{:S(2)}) collective-permute-start(bf16[4,144,768]{2,1,0:T(8,128)(2,1)S(1)} %slice.14.near_ref.refs_0_), channel_id=1, source_target_pairs={{0,130},{1,13},{4,134},{5,1},{8,138},{9,5},{12,142},{13,9},{128,0}... | collective-permute-start | bytes 2654216 | tf_op jit(solution)/shard_map/ppermute | solution.py:54
  34.7 12.0 %collective-permute-start.4 = (bf16[4,144,768]{2,1,0:T(8,128)(2,1)S(1)}, bf16[4,144,768]{2,1,0:T(8,128)(2,1)}, u32[]{:S(2)}, u32[]{:S(2)}) collective-permute-start(bf16[4,144,768]{2,1,0:T(8,128)(2,1)S(1)} %get-tuple-element.29.refs_1_), channel_id=1, source_target_pairs={{0,1},{1,0},{2,3},{3,2},{4,5},{5,4},{6,7},{7,6},{8,9},{9,8},{10,11... | collective-permute-start | bytes 2654216 | tf_op jit(solution)/shard_map/ppermute | solution.py:58
  37.6 19.9 %collective-permute-start.2 = (bf16[4,144,768]{2,1,0:T(8,128)(2,1)S(1)}, bf16[4,144,768]{2,1,0:T(8,128)(2,1)}, u32[]{:S(2)}, u32[]{:S(2)}) collective-permute-start(bf16[4,144,768]{2,1,0:T(8,128)(2,1)S(1)} %get-tuple-element.29.refs_1_), channel_id=1, source_target_pairs={{0,128},{1,5},{4,132},{5,9},{8,136},{9,13},{12,140},{13,1},{128,2}... | collective-permute-start | bytes 2654216 | tf_op jit(solution)/shard_map/ppermute | solution.py:54
  37.9 19.6 %all-to-all-start.2 = ((s16[16,8,896]{2,1,0:T(8,128)(2,1)}), s16[16,8,896]{2,1,0:T(8,128)(2,1)S(1)}, u32[]{:S(2)}, u32[]{:S(2)}) async-start(s16[16,8,896]{2,1,0:T(8,128)(2,1)} %get-tuple-element.28), calls=%async_computation.2 | async-start | bytes 458752 | tf_op jit(solution)/shard_map/all_to_all | solution.py:372
  46.4 11.1 %copy-start.2 = (s32[3]{0:T(128)S(1)}, s32[3]{0:T(128)}, u32[]{:S(2)}) copy-start(s32[3]{0:T(128)} %copy-done.1) | copy-start | bytes 40
  46.5 13.7 %collective-permute-start.6 = (bf16[4,144,768]{2,1,0:T(8,128)(2,1)}, bf16[4,144,768]{2,1,0:T(8,128)(2,1)S(1)}, u32[]{:S(2)}, u32[]{:S(2)}) collective-permute-start(bf16[4,144,768]{2,1,0:T(8,128)(2,1)} %collective-permute-done.5.refs_2_), channel_id=1, source_target_pairs={{0,1},{1,0},{2,3},{3,2},{4,5},{5,4},{6,7},{7,6},{8,9},{9,8},{10,11... | collective-permute-start | bytes 2654216 | tf_op jit(solution)/shard_map/ppermute | solution.py:58
  57.5 2.7 %copy-start = (bf16[1152,768]{1,0:T(8,128)(2,1)S(1)}, bf16[1152,768]{1,0:T(8,128)(2,1)}, u32[]{:S(2)}) copy-start(bf16[1152,768]{1,0:T(8,128)(2,1)} %shard_map.99.first_ref.refs_1_) | copy-start | bytes 5308420
  57.5 2.7 %collective-permute-start.7 = (bf16[4,144,768]{2,1,0:T(8,128)(2,1)}, bf16[4,144,768]{2,1,0:T(8,128)(2,1)S(1)}, u32[]{:S(2)}, u32[]{:S(2)}) collective-permute-start(bf16[4,144,768]{2,1,0:T(8,128)(2,1)} %collective-permute-done.2.refs_3_), channel_id=1, source_target_pairs={{0,1},{1,0},{2,3},{3,2},{4,5},{5,4},{6,7},{7,6},{8,9},{9,8},{10,11... | collective-permute-start | bytes 2654216 | tf_op jit(solution)/shard_map/ppermute | solution.py:58
